TPU v7x, 256 devices: a whole 4x4x8 slice. The times are simulated.
256 devices in a mesh: ep: 32 (over y_lo, z, core), tp: 8 (over x, y_hi).
Axes of the slice: x: 4, y: 4 (y_hi: 2, y_lo: 2; y = y_hi * 2 + y_lo), z: 8, core: 2. Of those that a mesh axis runs over, the one named last changes fastest.
Arguments:
- tokens_in: bfloat16 [32768, 1536], P('ep'), may hold values from -12 to 12
- lengths: int32 [32], P('ep'), may hold values from 1 to 1024, 16384 in all
- attn_gain: float32 [1536], replicated, may hold values from 0.1 to 1.9
- q_proj: float32 [1536, 1536], P('ep', 'tp'), may hold values from -2 to 2
- k_proj: float32 [1536, 512], P('ep', 'tp'), may hold values from -2 to 2
- value_projection: float32 [1536, 512], P('ep', 'tp'), may hold values from -0.15625 to 0.15625
- o_proj: float32 [1536, 1536], P('tp', 'ep'), may hold values from -2.5 to 2.5
- key_value_pages: bfloat16 [256, 16, 1024], P('ep', None, 'tp'), may hold values from -6 to 6
- page_table: int32 [32, 32, 2], P(None, 'ep'), may hold values from 0 to 7
- moe_gain: float32 [1536], replicated, may hold values from 0.1 to 1.9
- router: bfloat16 [1536, 32], replicated, may hold values from -5 to 5
- expert_ids: int32 [32768, 8], P(('ep', 'tp')), may hold values from 0 to 31, all different within a row; in each aligned block of 128 rows (0 to 127, 128 to 255, ...) at most 48 rows name the same one
- gate_up_proj: float32 [32, 1536, 1024], P('ep', 'tp'), may hold values from -0.15625 to 0.15625
- down_proj: float32 [32, 512, 1536], P('ep', 'tp'), may hold values from -0.25 to 0.25
Outputs:
- layer_out: bfloat16 [32768, 1536], P(('ep', 'tp'))
Inputs may be any that keep to these rules, and one draw needn't show every extreme that they name: `expert_ids`: among the 128 token slots of each aligned block (one device's slots), no expert is named more than 48 times, a bound that some block reaches. `lengths`: some prompt is 1024 tokens long.
All inputs are finite; a program needn't handle non-finite values. No bound on the sum of `lengths` on one device may be relied on, other than what follows from the above.
Results may differ from a plain program's by a relative error of at most 0.018.
Values may be sent and summed in bfloat16 or wider, within the bound.
No kernel may reach another device: no remote copies, remote signals or barrier semaphores. Data moves between devices by JAX's collectives and lax.ppermute only.
A program may use at most 128 MiB of HBM per device.

v0:
```python
import math

import jax
import jax.numpy as jnp
from jax import lax
from jax.sharding import PartitionSpec as P

HEAD_WIDTH = 64
FF = 512


epsilon = 1e-05


def rms_scale(values, norm_gain):
    mean_square = jnp.mean(values * values, axis=-1, keepdims=True)
    return values * lax.rsqrt(mean_square + epsilon) * norm_gain


def apply_rotary(vectors, token_positions):
    half_width = vectors.shape[-1] // 2
    frequency = jnp.exp(
        jnp.arange(half_width, dtype=jnp.float32) * (-2.0 * math.log(10000.0) / vectors.shape[-1])
    )
    angles = token_positions.astype(jnp.float32)[:, None] * frequency[None, :]
    cosine = jnp.cos(angles)[:, None, :]
    sine_table = jnp.sin(angles)[:, None, :]
    first_half = vectors[..., :half_width]
    second_half = vectors[..., half_width:]
    return jnp.concatenate(
        [
            first_half * cosine - second_half * sine_table,
            second_half * cosine + first_half * sine_table,
        ],
        axis=-1,
    )


def on_device(
    tokens_in,
    lengths,
    attn_gain,
    q_proj,
    k_proj,
    value_projection,
    o_proj,
    key_value_pages,
    page_table,
    moe_gain,
    router,
    expert_ids,
    gate_up_proj,
    down_proj,
):
    seq_len, model_width = tokens_in.shape
    ep_count = lax.axis_size("ep")
    tp_index = lax.axis_index("tp")
    kv_local = key_value_pages.shape[2] // (2 * HEAD_WIDTH)
    query_local = q_proj.shape[1] // HEAD_WIDTH
    query_weight, key_matrix, value_matrix, output_weight = (
        lax.all_gather(q_proj.astype(jnp.bfloat16), "ep", axis=0, tiled=True),
        lax.all_gather(k_proj.astype(jnp.bfloat16), "ep", axis=0, tiled=True),
        lax.all_gather(value_projection.astype(jnp.bfloat16), "ep", axis=0, tiled=True),
        lax.all_gather(o_proj.astype(jnp.bfloat16), "ep", axis=1, tiled=True),
    )
    chosen_pages = key_value_pages[page_table[:, 0, :]]
    arrived = lax.all_to_all(chosen_pages, "ep", split_axis=0, concat_axis=0, tiled=True)
    prefix_length = arrived.shape[0] * arrived.shape[1] * arrived.shape[2]
    prefix = arrived.reshape(prefix_length, kv_local, 2, HEAD_WIDTH)
    normalized_input = rms_scale(tokens_in.astype(jnp.float32), attn_gain).astype(jnp.bfloat16)
    token_positions = prefix_length + jnp.arange(seq_len)
    query_rows = apply_rotary(
        jnp.dot(normalized_input, query_weight, preferred_element_type=jnp.float32).reshape(
            seq_len, query_local, HEAD_WIDTH
        ),
        token_positions,
    ).astype(jnp.bfloat16)
    fresh_keys = apply_rotary(
        jnp.dot(normalized_input, key_matrix, preferred_element_type=jnp.float32).reshape(
            seq_len, kv_local, HEAD_WIDTH
        ),
        token_positions,
    ).astype(jnp.bfloat16)
    fresh_values = (
        jnp.dot(normalized_input, value_matrix, preferred_element_type=jnp.float32)
        .reshape(seq_len, kv_local, HEAD_WIDTH)
        .astype(jnp.bfloat16)
    )
    length_here = lengths[0]
    own = jnp.arange(prefix_length + seq_len)[None, :] - prefix_length
    block_rows = min(512, seq_len)
    all_keys = jnp.concatenate([prefix[:, 0, 0], fresh_keys[:, 0]], 0)
    all_values = jnp.concatenate([prefix[:, 0, 1], fresh_values[:, 0]], 0)
    grouped_queries = query_rows.transpose(1, 0, 2)
    blocks = []
    for block_start in range(0, seq_len, block_rows):
        query_block = grouped_queries[:, block_start : block_start + block_rows]
        scores = jnp.einsum(
            "gqd,kd->gqk", query_block, all_keys, preferred_element_type=jnp.float32
        ) * HEAD_WIDTH ** (-0.5)
        query_pos = block_start + jnp.arange(block_rows)
        allowed = (own < 0) | (own <= query_pos[:, None]) & (own < length_here)
        scores = jnp.where(allowed[None], scores, -1e30)
        top_score = jnp.max(scores, axis=-1, keepdims=True)
        weights = jnp.exp(scores - top_score)
        probs = (weights / jnp.sum(weights, axis=-1, keepdims=True)).astype(jnp.bfloat16)
        blocks.append(
            jnp.einsum("gqk,kd->gqd", probs, all_values, preferred_element_type=jnp.float32).astype(
                jnp.bfloat16
            )
        )
    head_outputs = jnp.concatenate(blocks, axis=1)
    attended = head_outputs.transpose(1, 0, 2).reshape(seq_len, query_local * HEAD_WIDTH)
    partial_out = jnp.dot(attended, output_weight, preferred_element_type=jnp.float32)
    attn_sum = lax.psum_scatter(
        partial_out.astype(jnp.bfloat16), "tp", scatter_dimension=0, tiled=True
    ).astype(jnp.float32)
    row_count = attn_sum.shape[0]
    own_rows = lax.dynamic_slice_in_dim(tokens_in, tp_index * row_count, row_count, 0)
    hidden = own_rows.astype(jnp.float32) + attn_sum
    moe_in = rms_scale(hidden, moe_gain).astype(jnp.bfloat16)
    expert_count = router.shape[1]
    choose_count = expert_ids.shape[1]
    capacity = max(2, 3 * row_count * choose_count // (2 * expert_count))
    logits = jnp.dot(moe_in, router, preferred_element_type=jnp.float32)
    expert_range = jnp.arange(expert_count)
    matches = expert_ids[:, :, None] == expert_range[None, None, :]
    picked = jnp.sum(jnp.where(matches, logits[:, None, :], 0.0), axis=-1)
    top_logit = jnp.max(picked, axis=-1, keepdims=True)
    raised = jnp.exp(picked - top_logit)
    gates = raised / jnp.sum(raised, axis=-1, keepdims=True)
    flat_ids = expert_ids.reshape(-1)
    one_hot = (flat_ids[:, None] == expert_range[None, :]).astype(jnp.int32)
    earlier = jnp.cumsum(one_hot, axis=0) - one_hot
    slot_rank = jnp.sum(earlier * one_hot, axis=1)
    destination = flat_ids * capacity + slot_rank
    send_rows = (
        jnp.zeros((expert_count * capacity, model_width), jnp.bfloat16)
        .at[destination]
        .set(jnp.repeat(moe_in, choose_count, axis=0))
    )
    received = lax.all_to_all(
        send_rows.reshape(ep_count, -1, model_width), "ep", split_axis=0, concat_axis=0, tiled=True
    )
    exp_local = gate_up_proj.shape[0]
    batch_rows = ep_count * capacity
    batch = (
        received.reshape(ep_count, exp_local, capacity, model_width)
        .transpose(1, 0, 2, 3)
        .reshape(exp_local, batch_rows, model_width)
    )
    gate_up_local = gate_up_proj.astype(jnp.bfloat16)
    down_local = down_proj.astype(jnp.bfloat16)
    gate_up_full, down_full = (
        lax.all_gather(gate_up_local, "tp", axis=1, tiled=True),
        lax.all_gather(down_local, "tp", axis=1, tiled=True),
    )
    gate_up = jnp.einsum("erd,edf->erf", batch, gate_up_full, preferred_element_type=jnp.float32)
    activated = (jax.nn.silu(gate_up[..., :FF]) * gate_up[..., FF:]).astype(jnp.bfloat16)
    expert_out = jnp.einsum(
        "erf,efd->erd", activated, down_full, preferred_element_type=jnp.float32
    ).astype(jnp.bfloat16)
    outgoing = (
        expert_out.reshape(exp_local, ep_count, capacity, model_width)
        .transpose(1, 0, 2, 3)
        .reshape(ep_count, exp_local * capacity, model_width)
    )
    returned = lax.all_to_all(outgoing, "ep", split_axis=0, concat_axis=0, tiled=True).reshape(
        expert_count * capacity, model_width
    )
    picked_rows = (
        returned[destination].reshape(row_count, choose_count, model_width).astype(jnp.float32)
    )
    mixed = jnp.sum(picked_rows * gates[:, :, None], axis=1)
    valid = tp_index * row_count + jnp.arange(row_count) < length_here
    return jnp.where(valid[:, None], hidden + mixed, 0.0).astype(jnp.bfloat16)


def solution(mesh):
    in_specs = (
        P("ep", None),
        P("ep"),
        P(),
        P("ep", "tp"),
        P("ep", "tp"),
        P("ep", "tp"),
        P("tp", "ep"),
        P("ep", None, "tp"),
        P(None, "ep", None),
        P(),
        P(),
        P(("ep", "tp"), None),
        P("ep", "tp", None),
        P("ep", "tp", None),
    )
    out_specs = P(("ep", "tp"), None)
    return jax.shard_map(
        on_device, mesh=mesh, in_specs=in_specs, out_specs=out_specs, check_vma=False
    )
```

profile of v0, /device:TPU:1, one launch (start us, length us, event | category | flops | bytes accessed | tf_op | source)
XLA Modules:
  0.0 618.2 jit_solution(13134275733922751719)
XLA Ops:
  6.5 0.8 compare_select_fusion.1
  7.4 0.1 copy.29
  7.5 0.1 reshape.435
  7.6 2.1 gather_fusion
  9.7 11.1 %all-to-all-start = ((bf16[32,2,16,128]{3,2,1,0:T(8,128)(2,1)}), bf16[32,2,16,128]{3,2,1,0:T(8,128)(2,1)S(1)}, u32[]{:S(2)}, u32[]{:S(2)}) async-start(bf16[32,2,16,128]{3,2,1,0:T(8,128)(2,1)} %bitcast.102), calls=%async_computation | async-start | bytes 524288 | tf_op jit(solution)/shard_map/all_to_all | solution.py:67
  20.8 0.0 reduce-scatter.2.cloned.1.call-start
  20.9 2.6 fusion.4
  23.5 0.8 convert_element_type.105
  24.3 36.5 %all_gather.18 = bf16[1536,192]{1,0:T(8,128)(2,1)S(1)} all-gather(bf16[48,192]{1,0:T(8,128)(2,1)S(1)} %convert_element_type.105), channel_id=1, replica_groups=mesh['ep'=32,'tp'=8] {'ep'}, dimensions={0}, use_global_device_ids=true | all-gather | bytes 608256 | tf_op jit(solution)/shard_map/all_gather | solution.py:61
  60.8 31.7 %all_gather.19 = bf16[1536,64]{1,0:T(8,128)(2,1)S(1)} all-gather(bf16[48,64]{1,0:T(8,128)(2,1)S(1)} %convert_element_type.107), channel_id=1, replica_groups=mesh['ep'=32,'tp'=8] {'ep'}, dimensions={0}, use_global_device_ids=true | all-gather | bytes 202752 | tf_op jit(solution)/shard_map/all_gather | solution.py:62
  92.6 0.8 fusion.6
  93.4 1.2 fusion.83
  94.6 1.1 convolution_bitcast_fusion.1
  95.6 0.5 multiply_cosine_fusion.1
  96.2 1.2 fusion.60
  98.1 33.1 %all_gather.20 = bf16[1536,64]{1,0:T(8,128)(2,1)S(1)} all-gather(bf16[48,64]{1,0:T(8,128)(2,1)S(1)} %convert_element_type.109), channel_id=1, replica_groups=mesh['ep'=32,'tp'=8] {'ep'}, dimensions={0}, use_global_device_ids=true | all-gather | bytes 202752 | tf_op jit(solution)/shard_map/all_gather | solution.py:63
  131.2 1.7 convolution_convert_fusion.2
  132.9 35.5 %all_gather.21 = bf16[192,1536]{0,1:T(8,128)(2,1)} all-gather(bf16[192,48]{0,1:T(8,128)(2,1)S(1)} %convert_element_type.114), channel_id=1, replica_groups=mesh['ep'=32,'tp'=8] {'ep'}, dimensions={1}, use_global_device_ids=true | all-gather | bytes 608256 | tf_op jit(solution)/shard_map/all_gather | solution.py:64
  168.4 0.1 subtract_convert_fusion
  168.5 0.8 maximum_bitcast_fusion
  169.3 2.9 fusion.17
  172.2 1.1 reshape.421
  173.3 3.1 fusion.72
  176.3 1.2 copy.38
  177.6 1.7 copy.39
  179.3 10.5 %fusion.78 = (f32[3,512]{1,0:T(4,128)S(1)}, f32[3,512,2048]{2,1,0:T(8,128)}) fusion(pred[512,2048]{1,0:T(8,128)(4,1)} %get-tuple-element.11, bf16[3,1024,64]{1,2,0:T(8,128)(2,1)} %maximum_bitcast_fusion, bf16[1024,32]{0,1:T(8,128)(2,1)} %get-tuple-element.10, bf16[1024,32]{0,1:T(8,128)(2,1)} %get-tuple-element.9, bf16[1024,64]{0,1:T(8,128)(2,1)S(1)} %bitcast.106), kind=kOutput, calls=%fused_computation.116 | convolution fusion | flops 416024576 | bytes 14096384 | tf_op jit(solution)/shard_map/sub | solution.py:105
  189.8 10.5 %fusion.73 = (f32[3,512]{1,0:T(4,128)S(1)}, f32[3,512,2048]{2,1,0:T(8,128)}) fusion(pred[512,2048]{1,0:T(8,128)(4,1)} %get-tuple-element.12, bf16[3,1024,64]{1,2,0:T(8,128)(2,1)} %maximum_bitcast_fusion, bf16[1024,32]{0,1:T(8,128)(2,1)} %get-tuple-element.10, bf16[1024,32]{0,1:T(8,128)(2,1)} %get-tuple-element.9, bf16[1024,64]{0,1:T(8,128)(2,1)} %bitcast.107), kind=kOutput, calls=%fused_computation.115 | convolution fusion | flops 416024576 | bytes 14096384 | tf_op jit(solution)/shard_map/sub | solution.py:105
  200.2 6.8 %fusion.32 = bf16[3,512,64]{1,2,0:T(8,128)(2,1)S(1)} fusion(f32[3,512,2048]{2,1,0:T(8,128)} %get-tuple-element.18, f32[3,512]{1,0:T(4,128)S(1)} %get-tuple-element.17, bf16[1024,64]{0,1:T(8,128)(2,1)S(1)} %copy-done.3, bf16[1024,64]{0,1:T(8,128)(2,1)S(1)} %bitcast.104), kind=kOutput, calls=%fused_computation.47 | convolution fusion | flops 409567232 | bytes 13047808 | tf_op jit(solution)/shard_map/gqk,kd->gqd/dot_general | solution.py:108
  207.0 1.3 copy-done.11
  208.4 2.3 fusion.31
  210.7 2.7 convolution_convert_fusion.1
  213.5 0.0 reduce-scatter.2.cloned.1.call-update
  213.5 0.1 copy.33
  213.6 0.1 eq.42
  213.7 0.1 eq.38
  213.8 9.0 %reduce-window.6 = s32[32,8,128]{2,1,0:T(8,128)S(1)} reduce-window(s32[32,8,128]{2,1,0:T(8,128)S(1)} %fusion.58, s32[]{:T(128)} %constant.20.clone.1), window={size=1x1x128 pad=0_0x0_0x127_0}, to_apply=%region_6.7 | reduce-window | flops 4161536 | bytes 262148 | tf_op jit(solution)/shard_map/reduce-window
  222.8 0.1 slice.60
  222.9 0.1 copy.35
  223.1 0.1 copy.36
  223.2 0.1 copy.32
  223.3 0.1 mul.250
  223.4 0.1 broadcast_add_fusion
  223.6 70.8 %reduce-scatter.2.cloned.1.call-done = bf16[128,1536]{1,0:T(8,128)(2,1)} async-done(((bf16[1024,1536]{1,0:T(8,128)(2,1)}), bf16[128,1536]{1,0:T(8,128)(2,1)}) %reduce-scatter.2.cloned.1.call-update) | async-done | bytes 393232 | tf_op jit(solution)/shard_map/reduce_scatter | solution.py:115
  294.3 1.2 multiply_reduce_fusion
  295.5 1.9 multiply_convert_fusion
  297.4 8.6 %scatter_custom_fusion = bf16[1536,1536]{1,0:T(8,128)(2,1)} fusion(s32[1024]{0:T(1024)S(1)} %bitcast.110, bf16[]{:T(256)} %constant.14.clone.1, bf16[128,1536]{1,0:T(8,128)(2,1)} %multiply_convert_fusion), kind=kCustom, calls=%fused_computation.38 | custom fusion | bytes 5111810 | tf_op jit(solution)/shard_map/scatter | solution.py:140
  306.1 9.3 %all-to-all-start.1 = ((bf16[32,48,1536]{2,1,0:T(8,128)(2,1)}), bf16[32,48,1536]{2,1,0:T(8,128)(2,1)}, u32[]{:S(2)}, u32[]{:S(2)}) async-start(bf16[32,48,1536]{2,1,0:T(8,128)(2,1)} %bitcast.98), calls=%async_computation.2 | async-start | bytes 9437184 | tf_op jit(solution)/shard_map/all_to_all | solution.py:142
  315.4 0.0 all-gather.3.cloned.1.call-start
  315.4 2.0 convert_element_type.120
  317.4 0.0 all-gather.5.cloned.1.call-start
  317.5 1.7 convert_element_type.122
  319.2 89.2 %all-gather.3.cloned.1.call-done = bf16[1,1536,1024]{2,1,0:T(8,128)(2,1)} async-done(((bf16[1,192,1024]{2,1,0:T(8,128)(2,1)}), bf16[1,1536,1024]{2,1,0:T(8,128)(2,1)}) %all-gather.3.cloned.1.call-update) | async-done | bytes 3145744 | tf_op jit(solution)/shard_map/all_gather | solution.py:155
  408.4 12.9 %all-to-all-done.1 = bf16[32,48,1536]{2,1,0:T(8,128)(2,1)} async-done(((bf16[32,48,1536]{2,1,0:T(8,128)(2,1)}), bf16[32,48,1536]{2,1,0:T(8,128)(2,1)}, u32[]{:S(2)}, u32[]{:S(2)}) %all-to-all-start.1) | async-done | bytes 4718624 | tf_op jit(solution)/shard_map/all_to_all | solution.py:142
  421.3 9.8 %convolution_bitcast_fusion = f32[1,1536,1024]{2,1,0:T(8,128)} fusion(bf16[1536,1536]{1,0:T(8,128)(2,1)} %bitcast.20, bf16[1,1536,1024]{2,1,0:T(8,128)(2,1)} %all-gather.3.cloned.1.call-done), kind=kOutput, calls=%fused_computation.29 | convolution fusion | flops 4831838208 | bytes 14155776 | tf_op jit(solution)/shard_map/erd,edf->erf/dot_general | solution.py:158
  431.1 39.7 %all-gather.5.cloned.1.call-done = bf16[1,512,1536]{2,1,0:T(8,128)(2,1)} async-done(((bf16[1,64,1536]{2,1,0:T(8,128)(2,1)}), bf16[1,512,1536]{2,1,0:T(8,128)(2,1)}) %all-gather.5.cloned.1.call-update) | async-done | bytes 1572880 | tf_op jit(solution)/shard_map/all_gather | solution.py:156
  470.8 8.2 %convolution_convert_fusion = bf16[1536,1536]{1,0:T(8,128)(2,1)} fusion(bf16[1,512,1536]{2,1,0:T(8,128)(2,1)} %all-gather.5.cloned.1.call-done, f32[1,1536,1024]{2,1,0:T(8,128)} %convolution_bitcast_fusion), kind=kOutput, calls=%fused_computation.15 | convolution fusion | flops 2422996992 | bytes 12582912 | tf_op jit(solution)/shard_map/erf,efd->erd/dot_general | solution.py:160
  478.9 9.9 %all-to-all-start.2 = ((bf16[32,48,1536]{2,1,0:T(8,128)(2,1)}), bf16[32,48,1536]{2,1,0:T(8,128)(2,1)}, u32[]{:S(2)}, u32[]{:S(2)}) async-start(bf16[32,48,1536]{2,1,0:T(8,128)(2,1)} %bitcast.99), calls=%async_computation.3 | async-start | bytes 9437184 | tf_op jit(solution)/shard_map/all_to_all | solution.py:168
  488.9 1.2 fusion.84
  490.1 0.1 select_reduce_fusion
  490.2 0.1 copy.37
  490.3 104.3 %all-to-all-done.2 = bf16[32,48,1536]{2,1,0:T(8,128)(2,1)} async-done(((bf16[32,48,1536]{2,1,0:T(8,128)(2,1)}), bf16[32,48,1536]{2,1,0:T(8,128)(2,1)}, u32[]{:S(2)}, u32[]{:S(2)}) %all-to-all-start.2) | async-done | bytes 4718624 | tf_op jit(solution)/shard_map/all_to_all | solution.py:168
  594.6 10.2 %gather_fusion.1 = bf16[1024,1536]{1,0:T(8,128)(2,1)} fusion(bf16[1536,1536]{1,0:T(8,128)(2,1)} %bitcast.26, s32[1024]{0:T(1024)S(1)} %broadcast_clamp_fusion), kind=kCustom, calls=%fused_computation.1 | custom fusion | bytes 6295552 | tf_op jit(solution)/shard_map/gather | solution.py:172
  604.8 4.7 fusion.7
  609.5 1.9 select_convert_fusion
  (49 shorter events, 0.3 us)
Async XLA Ops:
  6.5 482.3 %copy-start = (bf16[1536,32]{0,1:T(8,128)(2,1)S(1)}, bf16[1536,32]{0,1:T(8,128)(2,1)}, u32[]{:S(2)}) copy-start(bf16[1536,32]{0,1:T(8,128)(2,1)} %param.24) | copy-start | bytes 294916
  6.5 86.0 %copy-start.1 = (bf16[1024,1536]{1,0:T(8,128)(2,1)S(1)}, bf16[1024,1536]{1,0:T(8,128)(2,1)}, u32[]{:S(2)}) copy-start(bf16[1024,1536]{1,0:T(8,128)(2,1)} %param.14) | copy-start | bytes 9437188
  6.5 54.3 %copy-start.7 = (f32[48,64]{1,0:T(8,128)S(1)}, f32[48,64]{1,0:T(8,128)}, u32[]{:S(2)}) copy-start(f32[48,64]{1,0:T(8,128)} %param.18) | copy-start | bytes 36868
  6.5 86.0 %copy-start.9 = (f32[1536]{0:T(1024)S(1)}, f32[1536]{0:T(1024)}, u32[]{:S(2)}) copy-start(f32[1536]{0:T(1024)} %param.16) | copy-start | bytes 18436
  9.7 162.5 %all-to-all-start = ((bf16[32,2,16,128]{3,2,1,0:T(8,128)(2,1)}), bf16[32,2,16,128]{3,2,1,0:T(8,128)(2,1)S(1)}, u32[]{:S(2)}, u32[]{:S(2)}) async-start(bf16[32,2,16,128]{3,2,1,0:T(8,128)(2,1)} %bitcast.102), calls=%async_computation | async-start | bytes 524288 | tf_op jit(solution)/shard_map/all_to_all | solution.py:67
  20.8 273.5 %reduce-scatter.2.cloned.1.call-start = ((), (), s32[]{:S(2)}) async-start(), calls=%async_computation.4 | async-start | bytes 3538944 | tf_op jit(solution)/shard_map/reduce_scatter | solution.py:115
  93.3 4.7 copy-start.8
  94.6 38.4 %copy-start.5 = (f32[192,48]{0,1:T(8,128)S(1)}, f32[192,48]{0,1:T(8,128)}, u32[]{:S(2)}) copy-start(f32[192,48]{0,1:T(8,128)} %param.20) | copy-start | bytes 110596
  177.5 12.2 %copy-start.4 = (bf16[1024,1,1,64]{0,3,2,1:T(8,128)(2,1)}, bf16[1024,1,1,64]{0,3,2,1:T(8,128)(2,1)S(1)}, u32[]{:S(2)}) copy-start(bf16[1024,1,1,64]{0,3,2,1:T(8,128)(2,1)S(1)} %copy.38) | copy-start | bytes 393220
  189.8 10.5 %copy-start.3 = (bf16[1024,64]{0,1:T(8,128)(2,1)S(1)}, bf16[1024,64]{0,1:T(8,128)(2,1)}, u32[]{:S(2)}) copy-start(bf16[1024,64]{0,1:T(8,128)(2,1)} %convolution_convert_fusion.2) | copy-start | bytes 393220
  200.2 8.2 %copy-start.11 = (f32[3,512,2048]{2,1,0:T(8,128)S(1)}, f32[3,512,2048]{2,1,0:T(8,128)}, u32[]{:S(2)}) copy-start(f32[3,512,2048]{2,1,0:T(8,128)} %get-tuple-element.16) | copy-start | bytes 37748740
  208.4 2.4 copy-start.2
  210.7 2.8 copy-start.6
  210.7 84.8 %copy-start.10 = (f32[1536]{0:T(1024)S(1)}, f32[1536]{0:T(1024)}, u32[]{:S(2)}) copy-start(f32[1536]{0:T(1024)} %param.23) | copy-start | bytes 18436
  306.1 115.2 %all-to-all-start.1 = ((bf16[32,48,1536]{2,1,0:T(8,128)(2,1)}), bf16[32,48,1536]{2,1,0:T(8,128)(2,1)}, u32[]{:S(2)}, u32[]{:S(2)}) async-start(bf16[32,48,1536]{2,1,0:T(8,128)(2,1)} %bitcast.98), calls=%async_computation.2 | async-start | bytes 9437184 | tf_op jit(solution)/shard_map/all_to_all | solution.py:142
  315.4 93.0 %all-gather.3.cloned.1.call-start = ((), (), s32[]{:S(2)}) async-start(), calls=%async_computation.5 | async-start | bytes 3538944 | tf_op jit(solution)/shard_map/all_gather | solution.py:155
  317.4 153.3 %all-gather.5.cloned.1.call-start = ((), (), s32[]{:S(2)}) async-start(), calls=%async_computation.6 | async-start | bytes 1769472 | tf_op jit(solution)/shard_map/all_gather | solution.py:156
  478.9 115.6 %all-to-all-start.2 = ((bf16[32,48,1536]{2,1,0:T(8,128)(2,1)}), bf16[32,48,1536]{2,1,0:T(8,128)(2,1)}, u32[]{:S(2)}, u32[]{:S(2)}) async-start(bf16[32,48,1536]{2,1,0:T(8,128)(2,1)} %bitcast.99), calls=%async_computation.3 | async-start | bytes 9437184 | tf_op jit(solution)/shard_map/all_to_all | solution.py:168
Sparse Core Ops, SparseCore 0:
  213.6 80.6 reduce-scatter.1
  319.2 89.1 all-gather.2
  411.3 59.3 all-gather.4
where the time goes:
time: 626 us; the launch traced here: 618 us
  waiting for transfers between devices  317 us (51%)
  blocking collectives  137 us (22%)
  matrix products  56 us (9%)
  other arithmetic  33.4 us (5%)
  starting transfers between devices  30.5 us (5%)
  local copies, waits for them, and re-layouts  30.4 us (5%)
  between operations  14.3 us (2%)
    all_to_all x1, waiting for transfers between devices, on_device(): lax.all_to_all(outgoing, 'ep', split_axis=0, concat_axis=0, tiled=True)  104 us
    all_gather x1, waiting for transfers between devices, on_device(): lax.all_gather(gate_up_local, 'tp', axis=1, tiled=True)  89.2 us
    reduce_scatter x1, waiting for transfers between devices, on_device(): lax.psum_scatter(partial_out.astype(jnp.bfloat16), 'tp', scatter_dimensio...  70.8 us
    all_gather x1, waiting for transfers between devices, on_device(): lax.all_gather(down_local, 'tp', axis=1, tiled=True)  39.7 us
    all_gather x1, blocking collectives, on_device(): lax.all_gather(q_proj.astype(jnp.bfloat16), 'ep', axis=0, tiled=True)  36.5 us
    all_gather x1, blocking collectives, on_device(): lax.all_gather(o_proj.astype(jnp.bfloat16), 'ep', axis=1, tiled=True)  35.5 us
    all_gather x1, blocking collectives, on_device(): lax.all_gather(value_projection.astype(jnp.bfloat16), 'ep', axis=0, tiled...  33.1 us
    all_gather x1, blocking collectives, on_device(): lax.all_gather(k_proj.astype(jnp.bfloat16), 'ep', axis=0, tiled=True)  31.7 us
  transfers between devices with their start and end apart: 6, of which 5 were waited for; matrix products, arithmetic and copies ran while one was open for 6% of the time, Pallas kernels for 0%

commit v1 on v0

--- a/solution.py
+++ b/solution.py
@@ -10,6 +10,13 @@
 
 
 epsilon = 1e-05
+
+Z_GROUPS = [[y * 16 + z * 2 + c for z in range(8)] for y in range(2) for c in range(2)]
+CHIP_PAIR_GROUPS = [[y * 16 + z * 2 + c for y in range(2) for c in range(2)] for z in range(8)]
+PLANE_GROUPS = [
+    [(y * 16 + z * 2 + c) * 8 + t for y in range(2) for c in range(2) for t in range(8)]
+    for z in range(8)
+]
 
 
 def rms_scale(values, norm_gain):
@@ -57,12 +64,34 @@
     tp_index = lax.axis_index("tp")
     kv_local = key_value_pages.shape[2] // (2 * HEAD_WIDTH)
     query_local = q_proj.shape[1] // HEAD_WIDTH
-    query_weight, key_matrix, value_matrix, output_weight = (
-        lax.all_gather(q_proj.astype(jnp.bfloat16), "ep", axis=0, tiled=True),
-        lax.all_gather(k_proj.astype(jnp.bfloat16), "ep", axis=0, tiled=True),
-        lax.all_gather(value_projection.astype(jnp.bfloat16), "ep", axis=0, tiled=True),
-        lax.all_gather(o_proj.astype(jnp.bfloat16), "ep", axis=1, tiled=True),
-    )
+    packed_shard = jnp.concatenate(
+        [q_proj, k_proj, value_projection, o_proj.T], axis=1
+    ).astype(jnp.bfloat16)
+    along_z = lax.all_to_all(
+        jnp.broadcast_to(packed_shard[None], (8, *packed_shard.shape)),
+        "ep", 0, 0, axis_index_groups=Z_GROUPS, tiled=True,
+    )
+    across = lax.all_to_all(
+        jnp.broadcast_to(along_z[None], (4, *along_z.shape)),
+        "ep", 0, 0, axis_index_groups=CHIP_PAIR_GROUPS, tiled=True,
+    )
+    packed = (
+        across.reshape(2, 2, 8, *packed_shard.shape)
+        .transpose(0, 2, 1, 3, 4)
+        .reshape(model_width, packed_shard.shape[1])
+    )
+    query_weight = packed[:, :192]
+    key_matrix = packed[:, 192:256]
+    value_matrix = packed[:, 256:320]
+    output_weight = packed[:, 320:].T
+    gate_up_planes = lax.all_gather(
+        gate_up_proj[0].astype(jnp.bfloat16), "ep", axis_index_groups=Z_GROUPS
+    )
+    down_planes = lax.all_gather(
+        down_proj[0].astype(jnp.bfloat16), "ep", axis_index_groups=Z_GROUPS
+    )
+    gate_up_full = lax.all_to_all(gate_up_planes, "tp", 0, 0, tiled=True).reshape(model_width, -1)
+    down_full = lax.all_to_all(down_planes, "tp", 0, 0, tiled=True).reshape(-1, model_width)
     chosen_pages = key_value_pages[page_table[:, 0, :]]
     arrived = lax.all_to_all(chosen_pages, "ep", split_axis=0, concat_axis=0, tiled=True)
     prefix_length = arrived.shape[0] * arrived.shape[1] * arrived.shape[2]
@@ -112,66 +141,52 @@
     head_outputs = jnp.concatenate(blocks, axis=1)
     attended = head_outputs.transpose(1, 0, 2).reshape(seq_len, query_local * HEAD_WIDTH)
     partial_out = jnp.dot(attended, output_weight, preferred_element_type=jnp.float32)
-    attn_sum = lax.psum_scatter(
-        partial_out.astype(jnp.bfloat16), "tp", scatter_dimension=0, tiled=True
-    ).astype(jnp.float32)
-    row_count = attn_sum.shape[0]
+    row_count = seq_len // 8
+    parts = lax.all_to_all(
+        partial_out.astype(jnp.bfloat16).reshape(8, row_count, model_width), "tp", 0, 0, tiled=True
+    )
+    attn_sum = jnp.sum(parts.astype(jnp.float32), axis=0)
     own_rows = lax.dynamic_slice_in_dim(tokens_in, tp_index * row_count, row_count, 0)
     hidden = own_rows.astype(jnp.float32) + attn_sum
     moe_in = rms_scale(hidden, moe_gain).astype(jnp.bfloat16)
     expert_count = router.shape[1]
-    choose_count = expert_ids.shape[1]
-    capacity = max(2, 3 * row_count * choose_count // (2 * expert_count))
+    capacity = 48
     logits = jnp.dot(moe_in, router, preferred_element_type=jnp.float32)
-    expert_range = jnp.arange(expert_count)
-    matches = expert_ids[:, :, None] == expert_range[None, None, :]
-    picked = jnp.sum(jnp.where(matches, logits[:, None, :], 0.0), axis=-1)
-    top_logit = jnp.max(picked, axis=-1, keepdims=True)
-    raised = jnp.exp(picked - top_logit)
+    host = jnp.arange(expert_count)
+    expert_at = (host // 16) * 16 + (host % 8) * 2 + (host // 8) % 2
+    logits = logits.reshape(row_count, 2, 8, 2).transpose(0, 1, 3, 2).reshape(row_count, expert_count)
+    chosen = jnp.any(expert_ids[:, :, None] == expert_at[None, None, :], axis=1)
+    top_logit = jnp.max(jnp.where(chosen, logits, -jnp.inf), axis=-1, keepdims=True)
+    raised = jnp.where(chosen, jnp.exp(logits - top_logit), 0.0)
     gates = raised / jnp.sum(raised, axis=-1, keepdims=True)
-    flat_ids = expert_ids.reshape(-1)
-    one_hot = (flat_ids[:, None] == expert_range[None, :]).astype(jnp.int32)
-    earlier = jnp.cumsum(one_hot, axis=0) - one_hot
-    slot_rank = jnp.sum(earlier * one_hot, axis=1)
-    destination = flat_ids * capacity + slot_rank
-    send_rows = (
-        jnp.zeros((expert_count * capacity, model_width), jnp.bfloat16)
-        .at[destination]
-        .set(jnp.repeat(moe_in, choose_count, axis=0))
-    )
+    token = jnp.arange(row_count)
+    before = (token[None, :] < token[:, None]).astype(jnp.bfloat16)
+    rank = jnp.dot(before, chosen.astype(jnp.bfloat16), preferred_element_type=jnp.float32)
+    rank = jnp.where(chosen, rank, -1.0)
+    slots = jnp.arange(capacity, dtype=jnp.float32)
+    place = (rank.T[:, None, :] == slots[None, :, None]).astype(jnp.bfloat16)
+    send_rows = jnp.dot(
+        place.reshape(expert_count * capacity, row_count), moe_in, preferred_element_type=jnp.float32
+    ).astype(jnp.bfloat16)
     received = lax.all_to_all(
-        send_rows.reshape(ep_count, -1, model_width), "ep", split_axis=0, concat_axis=0, tiled=True
-    )
-    exp_local = gate_up_proj.shape[0]
-    batch_rows = ep_count * capacity
-    batch = (
-        received.reshape(ep_count, exp_local, capacity, model_width)
-        .transpose(1, 0, 2, 3)
-        .reshape(exp_local, batch_rows, model_width)
-    )
-    gate_up_local = gate_up_proj.astype(jnp.bfloat16)
-    down_local = down_proj.astype(jnp.bfloat16)
-    gate_up_full, down_full = (
-        lax.all_gather(gate_up_local, "tp", axis=1, tiled=True),
-        lax.all_gather(down_local, "tp", axis=1, tiled=True),
-    )
-    gate_up = jnp.einsum("erd,edf->erf", batch, gate_up_full, preferred_element_type=jnp.float32)
+        send_rows.reshape(expert_count, capacity, model_width), ("ep", "tp"), 0, 0,
+        axis_index_groups=PLANE_GROUPS, tiled=True,
+    ).reshape(expert_count * capacity, model_width)
+    gate_up = jnp.dot(received, gate_up_full, preferred_element_type=jnp.float32)
     activated = (jax.nn.silu(gate_up[..., :FF]) * gate_up[..., FF:]).astype(jnp.bfloat16)
-    expert_out = jnp.einsum(
-        "erf,efd->erd", activated, down_full, preferred_element_type=jnp.float32
-    ).astype(jnp.bfloat16)
-    outgoing = (
-        expert_out.reshape(exp_local, ep_count, capacity, model_width)
-        .transpose(1, 0, 2, 3)
-        .reshape(ep_count, exp_local * capacity, model_width)
-    )
-    returned = lax.all_to_all(outgoing, "ep", split_axis=0, concat_axis=0, tiled=True).reshape(
-        expert_count * capacity, model_width
-    )
-    picked_rows = (
-        returned[destination].reshape(row_count, choose_count, model_width).astype(jnp.float32)
-    )
-    mixed = jnp.sum(picked_rows * gates[:, :, None], axis=1)
+    expert_out = jnp.dot(activated, down_full, preferred_element_type=jnp.float32).astype(jnp.bfloat16)
+    returned = lax.all_to_all(
+        expert_out.reshape(expert_count, capacity, model_width), ("ep", "tp"), 0, 0,
+        axis_index_groups=PLANE_GROUPS, tiled=True,
+    ).reshape(expert_count * capacity, model_width)
+    weigh = jnp.where(rank[:, :, None] == slots, gates[:, :, None], 0.0).reshape(row_count, -1)
+    weigh_high = weigh.astype(jnp.bfloat16)
+    weigh_low = (weigh - weigh_high.astype(jnp.float32)).astype(jnp.bfloat16)
+    mixed = jnp.dot(
+        jnp.concatenate([weigh_high, weigh_low], axis=1),
+        jnp.concatenate([returned, returned], axis=0),
+        preferred_element_type=jnp.float32,
+    )
     valid = tp_index * row_count + jnp.arange(row_count) < length_here
     return jnp.where(valid[:, None], hidden + mixed, 0.0).astype(jnp.bfloat16)
 

time: 626 us -> 396 us (0.63); the launches traced: 618 us -> 395 us
  waiting for transfers between devices: 317 us -> 199 us
  blocking collectives: 137 us -> 43.7 us
  local copies, waits for them, and re-layouts: 30.4 us -> 13.3 us
  other arithmetic: 33.4 us -> 20.5 us
  starting transfers between devices: 30.5 us -> 42.3 us
    all_gather x4 -> x0, blocking collectives: 137 us -> none  [the longest x1 36.5 us: on_device(): lax.all_gather(q_proj.astype(jnp.bfloat16), 'ep', axis=0, tiled=True)]
    all_gather x2, waiting for transfers between devices: 129 us -> 34.6 us  [the longest x1 34.6 us: on_device(): lax.all_gather(down_proj[0].astype(jnp.bfloat16), 'ep', axis_index_groups...]
    reduce_scatter x1 -> x0, waiting for transfers between devices: 70.8 us -> none  [on_device(): lax.psum_scatter(partial_out.astype(jnp.bfloat16), 'tp', scatter_dimensio...]
    all_to_all x2 -> x6, waiting for transfers between devices: 117 us -> 161 us  [the longest x1 60.7 us: on_device(): lax.all_to_all(expert_out.reshape(expert_count, capacity, model_width), (...]
    all_to_all x0 -> x1, blocking collectives: none -> 43.7 us  [on_device(): lax.all_to_all(partial_out.astype(jnp.bfloat16).reshape(8, row_count, mod...]
    all_to_all x2 -> x6, starting transfers between devices: 19.2 us -> 31.1 us  [the longest x1 7.1 us: on_device(): lax.all_to_all(send_rows.reshape(expert_count, capacity, model_width), ('...]
    gather x1 -> x0, local copies, waits for them, and re-layouts: 10.2 us -> none  [on_device(): returned[destination].reshape(row_count, choose_count, model_width)]
    dot_general x2 -> x5, matrix products: 18 us -> 27.2 us  [the longest x1 9.84 us: on_device(): jnp.dot(received, gate_up_full, preferred_element_type=jnp.float32)]
  transfers between devices with their start and end apart: 6 -> 9, of which waited for: 5 -> 8; matrix products, arithmetic and copies ran while one was open for 6% -> 20% of each run, Pallas kernels for 0% -> 0%
where the time goes in v1:
time: 396 us; the launch traced here: 395 us
  waiting for transfers between devices  199 us (50%)
  matrix products  61.3 us (15%)
  blocking collectives  43.7 us (11%)
  starting transfers between devices  42.3 us (11%)
  other arithmetic  20.5 us (5%)
  between operations  14.5 us (4%)
  local copies, waits for them, and re-layouts  13.3 us (3%)
    all_to_all x1, waiting for transfers between devices, on_device(): lax.all_to_all(expert_out.reshape(expert_count, capacity, model_width), (...  60.7 us
    all_to_all x1, blocking collectives, on_device(): lax.all_to_all(partial_out.astype(jnp.bfloat16).reshape(8, row_count, mod...  43.7 us
    all_to_all x1, waiting for transfers between devices, on_device(): lax.all_to_all(gate_up_planes, 'tp', 0, 0, tiled=True)  36.1 us
    all_gather x1, waiting for transfers between devices, on_device(): lax.all_gather(down_proj[0].astype(jnp.bfloat16), 'ep', axis_index_groups...  34.6 us
    all_to_all x1, waiting for transfers between devices, on_device(): lax.all_to_all(send_rows.reshape(expert_count, capacity, model_width), ('...  26.6 us
    all_to_all x1, waiting for transfers between devices, on_device(): lax.all_to_all(jnp.broadcast_to(packed_shard[None], (8, *packed_shard.sha...  15.4 us
    sub x2, matrix products, on_device(): weights = jnp.exp(scores - top_score)  15 us
    dot_general x2, matrix products, on_device(): jnp.einsum('gqk,kd->gqd', probs, all_values, preferred_element_type=jnp.f...  13.5 us
  transfers between devices with their start and end apart: 9, of which 8 were waited for; matrix products, arithmetic and copies ran while one was open for 20% of the time, Pallas kernels for 0%

profile of v1, /device:TPU:1, one launch (start us, length us, event | category | flops | bytes accessed | tf_op | source)
XLA Modules:
  0.0 394.7 jit_solution(7991297196806701037)
XLA Ops:
  6.5 0.7 compare_select_fusion.1
  7.3 0.1 copy.45
  7.3 0.1 reshape.487
  7.5 2.1 gather_fusion
  9.5 11.1 %all-to-all-start.2 = ((bf16[32,2,16,128]{3,2,1,0:T(8,128)(2,1)}), bf16[32,2,16,128]{3,2,1,0:T(8,128)(2,1)S(1)}, u32[]{:S(2)}, u32[]{:S(2)}) async-start(bf16[32,2,16,128]{3,2,1,0:T(8,128)(2,1)} %bitcast.8), calls=%async_computation.2 | async-start | bytes 524288 | tf_op jit(solution)/shard_map/all_to_all | solution.py:96
  20.7 2.0 convert_element_type.114
  22.7 0.8 convert.27
  23.6 0.8 convert_bitcast_fusion
  24.4 0.7 convert.28
  25.1 0.7 convert.29
  26.5 0.1 pad_maximum_fusion.1
  26.6 2.6 fusion.8
  29.2 3.4 all-to-all-done.2
  32.6 0.8 broadcast_in_dim.52
  33.4 3.5 all-to-all-start
  36.9 2.9 fusion.20
  39.8 15.4 %all-to-all-done = bf16[8,48,512]{2,1,0:T(8,128)(2,1)S(1)} async-done(((bf16[8,48,512]{2,1,0:T(8,128)(2,1)}), bf16[8,48,512]{2,1,0:T(8,128)(2,1)S(1)}, u32[]{:S(2)}, u32[]{:S(2)}) %all-to-all-start) | async-done | bytes 393248 | tf_op jit(solution)/shard_map/all_to_all | solution.py:70
  55.2 1.3 broadcast_in_dim.53
  56.5 6.5 %all-to-all-start.1 = ((bf16[4,8,48,512]{3,2,1,0:T(8,128)(2,1)}), bf16[4,8,48,512]{3,2,1,0:T(8,128)(2,1)}, u32[]{:S(2)}, u32[]{:S(2)}) async-start(bf16[4,8,48,512]{3,2,1,0:T(8,128)(2,1)} %broadcast_in_dim.53), calls=%async_computation.1 | async-start | bytes 3145728 | tf_op jit(solution)/shard_map/all_to_all | solution.py:74
  63.0 1.2 multiply_cosine_fusion.1
  64.3 2.7 fusion.10
  67.0 1.1 reshape.473
  68.0 3.1 fusion.92
  71.2 1.2 copy.53
  72.4 1.2 copy.54
  73.6 8.8 %all-to-all-done.1 = bf16[4,8,48,512]{3,2,1,0:T(8,128)(2,1)} async-done(((bf16[4,8,48,512]{3,2,1,0:T(8,128)(2,1)}), bf16[4,8,48,512]{3,2,1,0:T(8,128)(2,1)}, u32[]{:S(2)}, u32[]{:S(2)}) %all-to-all-start.1) | async-done | bytes 1572896 | tf_op jit(solution)/shard_map/all_to_all | solution.py:74
  82.3 1.5 copy.44
  83.9 1.2 fusion.40
  85.1 1.1 convolution_bitcast_fusion
  86.2 1.7 convolution_convert_fusion.3
  88.0 0.6 fusion.71
  88.6 0.1 subtract_convert_fusion.1
  88.7 8.1 %fusion.98 = (f32[3,512]{1,0:T(4,128)S(1)}, f32[3,512,2048]{2,1,0:T(8,128)}) fusion(pred[512,2048]{1,0:T(8,128)(4,1)} %get-tuple-element.11, bf16[3,1024,64]{1,2,0:T(8,128)(2,1)S(1)} %maximum_bitcast_fusion, bf16[1024,32]{0,1:T(8,128)(2,1)S(1)} %get-tuple-element.10, bf16[1024,32]{0,1:T(8,128)(2,1)S(1)} %get-tuple-element.9, bf16[1024,64]{0,1:T(8,128)(2,1)S(1)} %bitcast.105), kind=kOutput, calls=%fused_computation.139 | convolution fusion | flops 416024576 | bytes 14096384 | tf_op jit(solution)/shard_map/sub | solution.py:134
  96.8 6.7 %fusion.38 = bf16[3,512,64]{1,2,0:T(8,128)(2,1)S(1)} fusion(f32[3,512,2048]{2,1,0:T(8,128)} %get-tuple-element.18, f32[3,512]{1,0:T(4,128)S(1)} %get-tuple-element.17, bf16[1024,64]{0,1:T(8,128)(2,1)S(1)} %copy-done.9, bf16[1024,64]{0,1:T(8,128)(2,1)S(1)} %bitcast.103), kind=kOutput, calls=%fused_computation.45 | convolution fusion | flops 409567232 | bytes 13047808 | tf_op jit(solution)/shard_map/gqk,kd->gqd/dot_general | solution.py:137
  103.6 6.9 %fusion.93 = (f32[3,512]{1,0:T(4,128)S(1)}, f32[3,512,2048]{2,1,0:T(8,128)}) fusion(pred[512,2048]{1,0:T(8,128)(4,1)S(1)} %copy-done.5, bf16[3,1024,64]{1,2,0:T(8,128)(2,1)S(1)} %maximum_bitcast_fusion, bf16[1024,32]{0,1:T(8,128)(2,1)S(1)} %get-tuple-element.10, bf16[1024,32]{0,1:T(8,128)(2,1)S(1)} %get-tuple-element.9, bf16[1024,64]{0,1:T(8,128)(2,1)S(1)} %bitcast.106), kind=kOutput, calls=%fused_computation.138 | convolution fusion | flops 416024576 | bytes 14096384 | tf_op jit(solution)/shard_map/sub | solution.py:134
  110.5 6.8 %fusion.37 = bf16[3,512,64]{1,2,0:T(8,128)(2,1)S(1)} fusion(f32[3,512,2048]{2,1,0:T(8,128)} %get-tuple-element.16, f32[3,512]{1,0:T(4,128)S(1)} %get-tuple-element.15, bf16[1024,64]{0,1:T(8,128)(2,1)S(1)} %copy-done.9, bf16[1024,64]{0,1:T(8,128)(2,1)S(1)} %bitcast.104), kind=kOutput, calls=%fused_computation.44 | convolution fusion | flops 409567232 | bytes 13047808 | tf_op jit(solution)/shard_map/gqk,kd->gqd/dot_general | solution.py:137
  117.3 1.3 convolution_convert_fusion.2
  118.7 43.7 %all_to_all.40 = bf16[8,128,1536]{2,1,0:T(8,128)(2,1)S(1)} all-to-all(bf16[8,128,1536]{2,1,0:T(8,128)(2,1)S(1)} %bitcast.89), channel_id=1, replica_groups=mesh['ep'=32,'tp'=8] {'tp'}, dimensions={0} | all-to-all | bytes 6291456 | tf_op jit(solution)/shard_map/all_to_all | solution.py:145
  162.3 4.6 %all-to-all-start.5 = ((bf16[8,192,1024]{2,1,0:T(8,128)(2,1)}), bf16[8,192,1024]{2,1,0:T(8,128)(2,1)}, u32[]{:S(2)}, u32[]{:S(2)}) async-start(bf16[8,192,1024]{2,1,0:T(8,128)(2,1)} %all-gather.3.cloned.1.call-done), calls=%async_computation.5 | async-start | bytes 6291456 | tf_op jit(solution)/shard_map/all_to_all | solution.py:93
  166.9 0.1 eq.62
  167.0 0.1 compare_reduce_fusion
  167.1 0.1 convolution_select_fusion
  167.3 0.3 bitcast_compare_fusion
  167.6 0.4 convert_reduce_fusion
  168.0 1.5 multiply_reduce_fusion
  169.5 1.2 multiply_convert_fusion
  170.7 3.5 convolution_convert_fusion.1
  174.2 36.1 %all-to-all-done.5 = bf16[8,192,1024]{2,1,0:T(8,128)(2,1)} async-done(((bf16[8,192,1024]{2,1,0:T(8,128)(2,1)}), bf16[8,192,1024]{2,1,0:T(8,128)(2,1)}, u32[]{:S(2)}, u32[]{:S(2)}) %all-to-all-start.5) | async-done | bytes 3145760 | tf_op jit(solution)/shard_map/all_to_all | solution.py:93
  210.2 7.1 %all-to-all-start.4 = ((bf16[32,48,1536]{2,1,0:T(8,128)(2,1)}), bf16[32,48,1536]{2,1,0:T(8,128)(2,1)}, u32[]{:S(2)}, u32[]{:S(2)}) async-start(bf16[32,48,1536]{2,1,0:T(8,128)(2,1)} %bitcast.88), calls=%async_computation.4 | async-start | bytes 9437184 | tf_op jit(solution)/shard_map/all_to_all | solution.py:171
  217.4 0.7 convert_element_type.116
  218.1 34.6 %all-gather.5.cloned.1.call-done = bf16[8,64,1536]{2,1,0:T(8,128)(2,1)} async-done(((bf16[1,64,1536]{2,1,0:T(8,128)(2,1)}), bf16[8,64,1536]{2,1,0:T(8,128)(2,1)}) %all-gather.5.cloned.1.call-update) | async-done | bytes 1572880 | tf_op jit(solution)/shard_map/all_gather | solution.py:90
  252.7 26.6 %all-to-all-done.4 = bf16[32,48,1536]{2,1,0:T(8,128)(2,1)} async-done(((bf16[32,48,1536]{2,1,0:T(8,128)(2,1)}), bf16[32,48,1536]{2,1,0:T(8,128)(2,1)}, u32[]{:S(2)}, u32[]{:S(2)}) %all-to-all-start.4) | async-done | bytes 4718624 | tf_op jit(solution)/shard_map/all_to_all | solution.py:171
  279.3 3.6 all-to-all-start.6
  282.9 9.8 %fusion.104 = f32[1536,1024]{1,0:T(8,128)} fusion(bf16[1536,1536]{1,0:T(8,128)(2,1)} %bitcast.29, bf16[1536,1024]{1,0:T(8,128)(2,1)} %bitcast.30), kind=kOutput, calls=%fused_computation.141 | convolution fusion | flops 4831838208 | bytes 14155776 | tf_op jit(solution)/shard_map/dot_general | solution.py:175
  292.8 13.5 %all-to-all-done.6 = bf16[8,64,1536]{2,1,0:T(8,128)(2,1)S(1)} async-done(((bf16[8,64,1536]{2,1,0:T(8,128)(2,1)}), bf16[8,64,1536]{2,1,0:T(8,128)(2,1)S(1)}, u32[]{:S(2)}, u32[]{:S(2)}) %all-to-all-start.6) | async-done | bytes 1572896 | tf_op jit(solution)/shard_map/all_to_all | solution.py:94
  306.2 7.8 %convolution_convert_fusion = bf16[1536,1536]{1,0:T(8,128)(2,1)} fusion(bf16[512,1536]{1,0:T(8,128)(2,1)S(1)} %bitcast.98, f32[1536,1024]{1,0:T(8,128)} %fusion.104), kind=kOutput, calls=%fused_computation.17 | convolution fusion | flops 2422996992 | bytes 12582912 | tf_op jit(solution)/shard_map/dot_general | solution.py:177
  314.0 5.9 %all-to-all-start.7 = ((bf16[32,48,1536]{2,1,0:T(8,128)(2,1)}), bf16[32,48,1536]{2,1,0:T(8,128)(2,1)}, u32[]{:S(2)}, u32[]{:S(2)}) async-start(bf16[32,48,1536]{2,1,0:T(8,128)(2,1)} %bitcast.94), calls=%async_computation.7 | async-start | bytes 9437184 | tf_op jit(solution)/shard_map/all_to_all | solution.py:178
  320.0 0.3 copy.48
  320.3 0.2 fusion.103
  320.7 0.3 copy.52
  321.0 0.1 fusion.47
  321.1 0.1 subtract_convert_fusion
  321.2 60.7 %all-to-all-done.7 = bf16[32,48,1536]{2,1,0:T(8,128)(2,1)} async-done(((bf16[32,48,1536]{2,1,0:T(8,128)(2,1)}), bf16[32,48,1536]{2,1,0:T(8,128)(2,1)}, u32[]{:S(2)}, u32[]{:S(2)}) %all-to-all-start.7) | async-done | bytes 4718624 | tf_op jit(solution)/shard_map/all_to_all | solution.py:178
  381.9 5.9 %fusion.28 = bf16[128,1536]{1,0:T(8,128)(2,1)} fusion(bf16[1536,1536]{1,0:T(8,128)(2,1)} %bitcast.33, bf16[128,1536]{1,0:T(8,128)(2,1)S(1)} %subtract_convert_fusion, bf16[128,1536]{1,0:T(8,128)(2,1)S(1)} %fusion.47, pred[128]{0:T(512)(128)(4,1)S(1)} %add_compare_fusion, f32[128,1536]{1,0:T(8,128)S(1)} %copy-done.4, bf16[1024,1536]{1,0:T(8,128)(2,1)} %param.14, ...), kind=kOutput, calls=%fused_computation.40 | convolution fusion | flops 1229389824 | bytes 7078020 | tf_op jit(solution)/shard_map/dot_general | solution.py:185
  (50 shorter events, 0.5 us)
Async XLA Ops:
  6.5 313.8 %copy-start = (bf16[1536,32]{0,1:T(8,128)(2,1)S(1)}, bf16[1536,32]{0,1:T(8,128)(2,1)}, u32[]{:S(2)}) copy-start(bf16[1536,32]{0,1:T(8,128)(2,1)} %param.24) | copy-start | bytes 294916
  9.5 23.1 %all-to-all-start.2 = ((bf16[32,2,16,128]{3,2,1,0:T(8,128)(2,1)}), bf16[32,2,16,128]{3,2,1,0:T(8,128)(2,1)S(1)}, u32[]{:S(2)}, u32[]{:S(2)}) async-start(bf16[32,2,16,128]{3,2,1,0:T(8,128)(2,1)} %bitcast.8), calls=%async_computation.2 | async-start | bytes 524288 | tf_op jit(solution)/shard_map/all_to_all | solution.py:96
  20.7 141.6 %all-gather.3.cloned.1.call-start = ((), (), s32[]{:S(2)}) async-start(), calls=%async_computation.8 | async-start | bytes 3538944 | tf_op jit(solution)/shard_map/all_gather | solution.py:87
  29.2 35.1 %copy-start.10 = (f32[1536]{0:T(1024)S(1)}, f32[1536]{0:T(1024)}, u32[]{:S(2)}) copy-start(f32[1536]{0:T(1024)} %param.16) | copy-start | bytes 18436
  33.4 21.8 %all-to-all-start = ((bf16[8,48,512]{2,1,0:T(8,128)(2,1)}), bf16[8,48,512]{2,1,0:T(8,128)(2,1)S(1)}, u32[]{:S(2)}, u32[]{:S(2)}) async-start(bf16[8,48,512]{2,1,0:T(8,128)(2,1)} %broadcast_in_dim.52), calls=%async_computation | async-start | bytes 786432 | tf_op jit(solution)/shard_map/all_to_all | solution.py:70
  56.5 25.8 %all-to-all-start.1 = ((bf16[4,8,48,512]{3,2,1,0:T(8,128)(2,1)}), bf16[4,8,48,512]{3,2,1,0:T(8,128)(2,1)}, u32[]{:S(2)}, u32[]{:S(2)}) async-start(bf16[4,8,48,512]{3,2,1,0:T(8,128)(2,1)} %broadcast_in_dim.53), calls=%async_computation.1 | async-start | bytes 3145728 | tf_op jit(solution)/shard_map/all_to_all | solution.py:74
  83.9 4.1 %copy-start.1 = (bf16[2,8,2,48,512]{4,3,2,1,0:T(8,128)(2,1)}, bf16[2,8,2,48,512]{4,3,2,1,0:T(8,128)(2,1)S(1)}, u32[]{:S(2)}) copy-start(bf16[2,8,2,48,512]{4,3,2,1,0:T(8,128)(2,1)S(1)} %copy.44) | copy-start | bytes 4718596
  85.1 3.5 copy-start.6
  85.1 3.5 copy-start.7
  88.7 8.1 %copy-start.9 = (bf16[1024,64]{0,1:T(8,128)(2,1)S(1)}, bf16[1024,64]{0,1:T(8,128)(2,1)}, u32[]{:S(2)}) copy-start(bf16[1024,64]{0,1:T(8,128)(2,1)} %convolution_convert_fusion.3) | copy-start | bytes 393220
  96.8 6.8 %copy-start.5 = (pred[512,2048]{1,0:T(8,128)(4,1)S(1)}, pred[512,2048]{1,0:T(8,128)(4,1)}, u32[]{:S(2)}) copy-start(pred[512,2048]{1,0:T(8,128)(4,1)} %get-tuple-element.12) | copy-start | bytes 3145732
  110.5 6.8 %copy-start.2 = (bf16[2,8,2,48,512]{4,3,2,1,0:T(8,128)(2,1)S(1)}, bf16[2,8,2,48,512]{4,3,2,1,0:T(8,128)(2,1)}, u32[]{:S(2)}) copy-start(bf16[2,8,2,48,512]{4,3,2,1,0:T(8,128)(2,1)} %copy-done.1) | copy-start | bytes 4718596
  162.3 4.7 %copy-start.12 = (s32[128,8]{0,1:T(8,128)S(1)}, s32[128,8]{0,1:T(8,128)}, u32[]{:S(2)}) copy-start(s32[128,8]{0,1:T(8,128)} %param.25) | copy-start | bytes 12292
  162.3 7.2 %copy-start.11 = (f32[1536]{0:T(1024)S(1)}, f32[1536]{0:T(1024)}, u32[]{:S(2)}) copy-start(f32[1536]{0:T(1024)} %param.23) | copy-start | bytes 18436
  162.3 47.9 %all-to-all-start.5 = ((bf16[8,192,1024]{2,1,0:T(8,128)(2,1)}), bf16[8,192,1024]{2,1,0:T(8,128)(2,1)}, u32[]{:S(2)}, u32[]{:S(2)}) async-start(bf16[8,192,1024]{2,1,0:T(8,128)(2,1)} %all-gather.3.cloned.1.call-done), calls=%async_computation.5 | async-start | bytes 6291456 | tf_op jit(solution)/shard_map/all_to_all | solution.py:93
  168.0 1.5 copy-start.3
  210.2 7.2 %copy-start.8 = (f32[1,64,1536]{2,1,0:T(8,128)S(1)}, f32[1,64,1536]{2,1,0:T(8,128)}, u32[]{:S(2)}) copy-start(f32[1,64,1536]{2,1,0:T(8,128)} %param.27) | copy-start | bytes 1179652
  210.2 69.1 %all-to-all-start.4 = ((bf16[32,48,1536]{2,1,0:T(8,128)(2,1)}), bf16[32,48,1536]{2,1,0:T(8,128)(2,1)}, u32[]{:S(2)}, u32[]{:S(2)}) async-start(bf16[32,48,1536]{2,1,0:T(8,128)(2,1)} %bitcast.88), calls=%async_computation.4 | async-start | bytes 9437184 | tf_op jit(solution)/shard_map/all_to_all | solution.py:171
  217.3 35.4 %all-gather.5.cloned.1.call-start = ((), (), s32[]{:S(2)}) async-start(), calls=%async_computation.9 | async-start | bytes 1769472 | tf_op jit(solution)/shard_map/all_gather | solution.py:90
  279.3 26.9 %all-to-all-start.6 = ((bf16[8,64,1536]{2,1,0:T(8,128)(2,1)}), bf16[8,64,1536]{2,1,0:T(8,128)(2,1)S(1)}, u32[]{:S(2)}, u32[]{:S(2)}) async-start(bf16[8,64,1536]{2,1,0:T(8,128)(2,1)} %all-gather.5.cloned.1.call-done), calls=%async_computation.6 | async-start | bytes 3145728 | tf_op jit(solution)/shard_map/all_to_all | solution.py:94
  314.0 67.9 %all-to-all-start.7 = ((bf16[32,48,1536]{2,1,0:T(8,128)(2,1)}), bf16[32,48,1536]{2,1,0:T(8,128)(2,1)}, u32[]{:S(2)}, u32[]{:S(2)}) async-start(bf16[32,48,1536]{2,1,0:T(8,128)(2,1)} %bitcast.94), calls=%async_computation.7 | async-start | bytes 9437184 | tf_op jit(solution)/shard_map/all_to_all | solution.py:178
  320.0 62.0 %copy-start.4 = (f32[128,1536]{1,0:T(8,128)S(1)}, f32[128,1536]{1,0:T(8,128)}, u32[]{:S(2)}) copy-start(f32[128,1536]{1,0:T(8,128)} %copy-done.3) | copy-start | bytes 2359300
Sparse Core Ops, SparseCore 0:
  23.3 53.9 all-gather.2
  220.0 32.6 all-gather.4

commit v2 on v1

--- a/solution.py
+++ b/solution.py
@@ -3,10 +3,14 @@
 import jax
 import jax.numpy as jnp
 from jax import lax
+from jax.experimental import pallas as pl
+from jax.experimental.pallas import tpu as pltpu
 from jax.sharding import PartitionSpec as P
 
 HEAD_WIDTH = 64
 FF = 512
+CAPACITY = 48
+EXPERTS = 32
 
 
 epsilon = 1e-05
@@ -40,6 +44,108 @@
             second_half * cosine + first_half * sine_table,
         ],
         axis=-1,
+    )
+
+
+def project_body(
+    parts_ref, weight_hbm, rows_ref, gain_ref, router_ref, ids_ref,
+    hidden_ref, send_ref, high_ref, low_ref,
+    weight, attended, place, sem,
+):
+    copies = []
+    for z in range(8):
+        for y in range(2):
+            copy = pltpu.make_async_copy(
+                weight_hbm.at[z, y], weight.at[pl.ds((y * 8 + z) * 96, 96)], sem.at[z * 2 + y]
+            )
+            copy.start()
+            copies.append(copy)
+    for t in range(8):
+        attended[:, t * 192 : (t + 1) * 192] = parts_ref[t]
+    tokens = rows_ref.shape[0]
+    host = lax.broadcasted_iota(jnp.int32, (EXPERTS, tokens), 0)
+    expert_at = (host // 16) * 16 + (host % 8) * 2 + (host // 8) % 2
+    chosen = jnp.zeros((EXPERTS, tokens), jnp.float32)
+    for k in range(ids_ref.shape[0]):
+        chosen = jnp.where(ids_ref[k : k + 1, :] == expert_at, 1.0, chosen)
+    earlier = lax.broadcasted_iota(jnp.int32, (tokens, tokens), 0) < lax.broadcasted_iota(
+        jnp.int32, (tokens, tokens), 1
+    )
+    rank = jnp.dot(
+        chosen.astype(jnp.bfloat16),
+        jnp.where(earlier, 1.0, 0.0).astype(jnp.bfloat16),
+        preferred_element_type=jnp.float32,
+    )
+    rank = jnp.where(chosen > 0.0, rank, -1.0)
+    slot = lax.broadcasted_iota(jnp.int32, (CAPACITY, tokens), 0).astype(jnp.float32)
+    for g in range(EXPERTS):
+        place[g * CAPACITY : (g + 1) * CAPACITY, :] = jnp.where(
+            rank[g : g + 1, :] == slot, 1.0, 0.0
+        ).astype(jnp.bfloat16)
+    for copy in copies:
+        copy.wait()
+    for c in range(0, 1536, 256):
+        hidden_ref[:, c : c + 256] = rows_ref[:, c : c + 256].astype(jnp.float32) + lax.dot_general(
+            attended[...],
+            weight[c : c + 256, :],
+            (((1,), (1,)), ((), ())),
+            preferred_element_type=jnp.float32,
+        )
+    hidden = hidden_ref[...]
+    moe_in = rms_scale(hidden, gain_ref[...]).astype(jnp.bfloat16)
+    for c in range(0, EXPERTS * CAPACITY, 256):
+        send_ref[c : c + 256, :] = jnp.dot(
+            place[c : c + 256, :], moe_in, preferred_element_type=jnp.float32
+        ).astype(jnp.bfloat16)
+    logits = lax.dot_general(
+        router_ref[...], moe_in, (((1,), (1,)), ((), ())), preferred_element_type=jnp.float32
+    )
+    top_logit = jnp.max(jnp.where(chosen > 0.0, logits, -3e38), axis=0, keepdims=True)
+    raised = jnp.where(chosen > 0.0, jnp.exp(jnp.minimum(logits - top_logit, 0.0)), 0.0)
+    gates = raised / jnp.sum(raised, axis=0, keepdims=True)
+    for g in range(EXPERTS):
+        weigh = place[g * CAPACITY : (g + 1) * CAPACITY, :].astype(jnp.float32) * gates[g : g + 1, :]
+        high = weigh.astype(jnp.bfloat16)
+        high_ref[g * CAPACITY : (g + 1) * CAPACITY, :] = high
+        low_ref[g * CAPACITY : (g + 1) * CAPACITY, :] = (
+            weigh - high.astype(jnp.float32)
+        ).astype(jnp.bfloat16)
+
+
+def project_and_dispatch(parts, output_weight, own_rows, moe_gain, router_hosted, ids_by_choice):
+    row_count, model_width = own_rows.shape
+    slots = EXPERTS * CAPACITY
+    vmem = pl.BlockSpec(memory_space=pltpu.VMEM)
+    return pl.pallas_call(
+        project_body,
+        out_shape=(
+            jax.ShapeDtypeStruct((row_count, model_width), jnp.float32),
+            jax.ShapeDtypeStruct((slots, model_width), jnp.bfloat16),
+            jax.ShapeDtypeStruct((slots, row_count), jnp.bfloat16),
+            jax.ShapeDtypeStruct((slots, row_count), jnp.bfloat16),
+        ),
+        in_specs=[vmem, pl.BlockSpec(memory_space=pltpu.HBM), vmem, vmem, vmem, vmem],
+        out_specs=(vmem, vmem, vmem, vmem),
+        scratch_shapes=[
+            pltpu.VMEM((model_width, model_width), jnp.bfloat16),
+            pltpu.VMEM((row_count, model_width), jnp.bfloat16),
+            pltpu.VMEM((slots, row_count), jnp.bfloat16),
+            pltpu.SemaphoreType.DMA((16,)),
+        ],
+        compiler_params=pltpu.CompilerParams(vmem_limit_bytes=40 << 20),
+        cost_estimate=pl.CostEstimate(
+            flops=4 * row_count * model_width * model_width,
+            bytes_accessed=4 * model_width * model_width,
+            transcendentals=0,
+        ),
+        name="project_and_dispatch",
+    )(
+        parts,
+        output_weight.reshape(8, 2, 96, model_width),
+        own_rows,
+        moe_gain.reshape(1, model_width),
+        router_hosted,
+        ids_by_choice,
     )
 
 
@@ -65,8 +171,11 @@
     kv_local = key_value_pages.shape[2] // (2 * HEAD_WIDTH)
     query_local = q_proj.shape[1] // HEAD_WIDTH
     packed_shard = jnp.concatenate(
-        [q_proj, k_proj, value_projection, o_proj.T], axis=1
+        [q_proj, k_proj, value_projection], axis=1
     ).astype(jnp.bfloat16)
+    gate_up_planes = lax.all_gather(
+        gate_up_proj[0].astype(jnp.bfloat16), "ep", axis_index_groups=Z_GROUPS
+    )
     along_z = lax.all_to_all(
         jnp.broadcast_to(packed_shard[None], (8, *packed_shard.shape)),
         "ep", 0, 0, axis_index_groups=Z_GROUPS, tiled=True,
@@ -83,17 +192,21 @@
     query_weight = packed[:, :192]
     key_matrix = packed[:, 192:256]
     value_matrix = packed[:, 256:320]
-    output_weight = packed[:, 320:].T
-    gate_up_planes = lax.all_gather(
-        gate_up_proj[0].astype(jnp.bfloat16), "ep", axis_index_groups=Z_GROUPS
-    )
-    down_planes = lax.all_gather(
-        down_proj[0].astype(jnp.bfloat16), "ep", axis_index_groups=Z_GROUPS
-    )
+    chosen_pages = key_value_pages[page_table[:, 0, :]]
+    chosen_pages, across = lax.optimization_barrier((chosen_pages, across))
+    arrived = lax.all_to_all(chosen_pages, "ep", split_axis=0, concat_axis=0, tiled=True)
+    output_shard = o_proj.T.astype(jnp.bfloat16)
+    output_shard, arrived = lax.optimization_barrier((output_shard, arrived))
+    output_plane = lax.all_to_all(
+        jnp.broadcast_to(output_shard[None], (32, *output_shard.shape)),
+        ("ep", "tp"), 0, 0, axis_index_groups=PLANE_GROUPS, tiled=True,
+    )
+    output_plane = (
+        output_plane.reshape(4, 8, 48, 192).transpose(0, 2, 1, 3).reshape(192, model_width)
+    )
+    output_plane, gate_up_planes = lax.optimization_barrier((output_plane, gate_up_planes))
+    output_weight = lax.all_gather(output_plane, "ep", axis_index_groups=Z_GROUPS)
     gate_up_full = lax.all_to_all(gate_up_planes, "tp", 0, 0, tiled=True).reshape(model_width, -1)
-    down_full = lax.all_to_all(down_planes, "tp", 0, 0, tiled=True).reshape(-1, model_width)
-    chosen_pages = key_value_pages[page_table[:, 0, :]]
-    arrived = lax.all_to_all(chosen_pages, "ep", split_axis=0, concat_axis=0, tiled=True)
     prefix_length = arrived.shape[0] * arrived.shape[1] * arrived.shape[2]
     prefix = arrived.reshape(prefix_length, kv_local, 2, HEAD_WIDTH)
     normalized_input = rms_scale(tokens_in.astype(jnp.float32), attn_gain).astype(jnp.bfloat16)
@@ -140,51 +253,42 @@
         )
     head_outputs = jnp.concatenate(blocks, axis=1)
     attended = head_outputs.transpose(1, 0, 2).reshape(seq_len, query_local * HEAD_WIDTH)
-    partial_out = jnp.dot(attended, output_weight, preferred_element_type=jnp.float32)
+    attended, gate_up_full = lax.optimization_barrier((attended, gate_up_full))
     row_count = seq_len // 8
-    parts = lax.all_to_all(
-        partial_out.astype(jnp.bfloat16).reshape(8, row_count, model_width), "tp", 0, 0, tiled=True
-    )
-    attn_sum = jnp.sum(parts.astype(jnp.float32), axis=0)
+    attn_parts = lax.all_to_all(
+        attended.reshape(8, row_count, query_local * HEAD_WIDTH), "tp", 0, 0, tiled=True
+    )
     own_rows = lax.dynamic_slice_in_dim(tokens_in, tp_index * row_count, row_count, 0)
-    hidden = own_rows.astype(jnp.float32) + attn_sum
-    moe_in = rms_scale(hidden, moe_gain).astype(jnp.bfloat16)
-    expert_count = router.shape[1]
-    capacity = 48
-    logits = jnp.dot(moe_in, router, preferred_element_type=jnp.float32)
-    host = jnp.arange(expert_count)
-    expert_at = (host // 16) * 16 + (host % 8) * 2 + (host // 8) % 2
-    logits = logits.reshape(row_count, 2, 8, 2).transpose(0, 1, 3, 2).reshape(row_count, expert_count)
-    chosen = jnp.any(expert_ids[:, :, None] == expert_at[None, None, :], axis=1)
-    top_logit = jnp.max(jnp.where(chosen, logits, -jnp.inf), axis=-1, keepdims=True)
-    raised = jnp.where(chosen, jnp.exp(logits - top_logit), 0.0)
-    gates = raised / jnp.sum(raised, axis=-1, keepdims=True)
-    token = jnp.arange(row_count)
-    before = (token[None, :] < token[:, None]).astype(jnp.bfloat16)
-    rank = jnp.dot(before, chosen.astype(jnp.bfloat16), preferred_element_type=jnp.float32)
-    rank = jnp.where(chosen, rank, -1.0)
-    slots = jnp.arange(capacity, dtype=jnp.float32)
-    place = (rank.T[:, None, :] == slots[None, :, None]).astype(jnp.bfloat16)
-    send_rows = jnp.dot(
-        place.reshape(expert_count * capacity, row_count), moe_in, preferred_element_type=jnp.float32
-    ).astype(jnp.bfloat16)
+    router_hosted = router.T.reshape(2, 8, 2, model_width).transpose(0, 2, 1, 3)
+    hidden, send_rows, weigh_high, weigh_low = project_and_dispatch(
+        attn_parts,
+        output_weight,
+        own_rows,
+        moe_gain,
+        router_hosted.reshape(EXPERTS, model_width),
+        expert_ids.T,
+    )
     received = lax.all_to_all(
-        send_rows.reshape(expert_count, capacity, model_width), ("ep", "tp"), 0, 0,
+        send_rows.reshape(EXPERTS, CAPACITY, model_width), ("ep", "tp"), 0, 0,
         axis_index_groups=PLANE_GROUPS, tiled=True,
-    ).reshape(expert_count * capacity, model_width)
+    ).reshape(EXPERTS * CAPACITY, model_width)
+    down_shard, output_weight = lax.optimization_barrier(
+        (down_proj[0].astype(jnp.bfloat16), output_weight)
+    )
+    down_planes = lax.all_gather(down_shard, "ep", axis_index_groups=Z_GROUPS)
+    down_planes, received = lax.optimization_barrier((down_planes, received))
+    down_full = lax.all_to_all(down_planes, "tp", 0, 0, tiled=True).reshape(-1, model_width)
     gate_up = jnp.dot(received, gate_up_full, preferred_element_type=jnp.float32)
     activated = (jax.nn.silu(gate_up[..., :FF]) * gate_up[..., FF:]).astype(jnp.bfloat16)
     expert_out = jnp.dot(activated, down_full, preferred_element_type=jnp.float32).astype(jnp.bfloat16)
     returned = lax.all_to_all(
-        expert_out.reshape(expert_count, capacity, model_width), ("ep", "tp"), 0, 0,
+        expert_out.reshape(EXPERTS, CAPACITY, model_width), ("ep", "tp"), 0, 0,
         axis_index_groups=PLANE_GROUPS, tiled=True,
-    ).reshape(expert_count * capacity, model_width)
-    weigh = jnp.where(rank[:, :, None] == slots, gates[:, :, None], 0.0).reshape(row_count, -1)
-    weigh_high = weigh.astype(jnp.bfloat16)
-    weigh_low = (weigh - weigh_high.astype(jnp.float32)).astype(jnp.bfloat16)
-    mixed = jnp.dot(
-        jnp.concatenate([weigh_high, weigh_low], axis=1),
+    ).reshape(EXPERTS * CAPACITY, model_width)
+    mixed = lax.dot_general(
+        jnp.concatenate([weigh_high, weigh_low], axis=0),
         jnp.concatenate([returned, returned], axis=0),
+        (((0,), (0,)), ((), ())),
         preferred_element_type=jnp.float32,
     )
     valid = tp_index * row_count + jnp.arange(row_count) < length_here

time: 396 us -> 382 us (0.965)
  blocking collectives: 43.7 us -> 19.9 us
  local copies, waits for them, and re-layouts: 13.3 us -> 21.9 us
  other arithmetic: 20.5 us -> 13 us
  starting transfers between devices: 42.3 us -> 47.8 us
  Pallas kernels: 0 us -> 4.76 us
    all_to_all x1, blocking collectives: 43.7 us -> 19.9 us  [on_device(): lax.all_to_all(jnp.broadcast_to(packed_shard[None], (8, *packed_shard.sha...]
    all_to_all x1, waiting for transfers between devices: 36.1 us -> 20.7 us  [on_device(): lax.all_to_all(gate_up_planes, 'tp', 0, 0, tiled=True)]
    all_to_all x3 -> x4, starting transfers between devices: 16.5 us -> 27 us  [the longest x1 8.82 us: on_device(): lax.all_to_all(jnp.broadcast_to(output_shard[None], (32, *output_shard.sh...]
    all_to_all x1, waiting for transfers between devices: 3.41 us -> 11.3 us  [on_device(): lax.all_to_all(chosen_pages, 'ep', split_axis=0, concat_axis=0, tiled=True)]
    all_to_all x1, starting transfers between devices: 11.1 us -> 4.39 us  [on_device(): lax.all_to_all(chosen_pages, 'ep', split_axis=0, concat_axis=0, tiled=True)]
    all_to_all x3 -> x4, waiting for transfers between devices: 103 us -> 108 us  [the longest x1 62 us: on_device(): lax.all_to_all(expert_out.reshape(EXPERTS, CAPACITY, model_width), ('ep',...]
    reshape x0 -> x5, local copies, waits for them, and re-layouts: none -> 5.51 us  [the longest x1 2.46 us: on_device(): output_plane.reshape(4, 8, 48, 192).transpose(0, 2, 1, 3)]
    dot_general x5 -> x1, matrix products: 11.1 us -> 5.96 us  [on_device(): lax.dot_general(jnp.concatenate([weigh_high, weigh_low], axis=0), jnp.con...]
  transfers between devices with their start and end apart: 9 -> 11, of which waited for: 8 -> 9; matrix products, arithmetic and copies ran while one was open for 20% -> 19% of each run, Pallas kernels for 0% -> 0%
where the time goes in v2:
time: 382 us; the launch traced here: 381 us
  waiting for transfers between devices  201 us (53%)
  matrix products  58.7 us (15%)
  starting transfers between devices  47.8 us (13%)
  local copies, waits for them, and re-layouts  21.9 us (6%)
  blocking collectives  19.9 us (5%)
  between operations  14.2 us (4%)
  other arithmetic  13 us (3%)
  Pallas kernels  4.76 us (1%)
    all_to_all x1, waiting for transfers between devices, on_device(): lax.all_to_all(expert_out.reshape(EXPERTS, CAPACITY, model_width), ('ep',...  62 us
    all_gather x1, waiting for transfers between devices, on_device(): down_planes = lax.all_gather(down_shard, 'ep', axis_index_groups=Z_GROUPS)  34.2 us
    all_to_all x1, waiting for transfers between devices, on_device(): lax.all_to_all(send_rows.reshape(EXPERTS, CAPACITY, model_width), ('ep',...  27 us
    all_to_all x1, waiting for transfers between devices, on_device(): lax.all_to_all(gate_up_planes, 'tp', 0, 0, tiled=True)  20.7 us
    all_to_all x1, blocking collectives, on_device(): lax.all_to_all(jnp.broadcast_to(packed_shard[None], (8, *packed_shard.sha...  19.9 us
    sub x2, matrix products, on_device(): weights = jnp.exp(scores - top_score)  17.4 us
    dot_general x2, matrix products, on_device(): jnp.einsum('gqk,kd->gqd', probs, all_values, preferred_element_type=jnp.f...  13.6 us
    all_to_all x1, waiting for transfers between devices, on_device(): lax.all_to_all(jnp.broadcast_to(output_shard[None], (32, *output_shard.sh...  13.5 us
  transfers between devices with their start and end apart: 11, of which 9 were waited for; matrix products, arithmetic and copies ran while one was open for 19% of the time, Pallas kernels for 0%

profile of v2, /device:TPU:1, one launch (start us, length us, event | category | flops | bytes accessed | tf_op | source)
XLA Modules:
  0.0 381.1 jit_solution(2300850528297966072)
XLA Ops:
  6.5 0.0 all-gather.6.cloned.1.call-start
  6.6 2.1 convert_element_type.89
  8.7 0.8 convert.23
  9.5 0.7 convert.24
  10.2 0.7 convert.25
  11.0 0.1 pad_maximum_fusion.1
  11.1 19.9 %all_to_all.45 = bf16[8,48,320]{2,1,0:T(8,128)(2,1)S(1)} all-to-all(bf16[8,48,320]{2,1,0:T(8,128)(2,1)S(1)} %broadcast_in_dim.34), channel_id=1, replica_groups={{0,16,32,48,64,80,96,112},{8,24,40,56,72,88,104,120},{128,144,160,176,1..., dimensions={0} | all-to-all | bytes 491520 | tf_op jit(solution)/shard_map/all_to_all | solution.py:179
  31.0 1.1 broadcast_in_dim.35
  32.1 8.4 %all-to-all-start.1 = ((bf16[4,8,48,320]{3,2,1,0:T(8,128)(2,1)}), bf16[4,8,48,320]{3,2,1,0:T(8,128)(2,1)}, u32[]{:S(2)}, u32[]{:S(2)}) async-start(bf16[4,8,48,320]{3,2,1,0:T(8,128)(2,1)} %broadcast_in_dim.35), calls=%async_computation.1 | async-start | bytes 2359296 | tf_op jit(solution)/shard_map/all_to_all | solution.py:183
  41.3 0.1 copy.39
  41.4 0.1 reshape.390
  41.5 1.3 gather_fusion
  42.8 12.9 %all-to-all-done.1 = bf16[4,8,48,320]{3,2,1,0:T(8,128)(2,1)} async-done(((bf16[4,8,48,320]{3,2,1,0:T(8,128)(2,1)}), bf16[4,8,48,320]{3,2,1,0:T(8,128)(2,1)}, u32[]{:S(2)}, u32[]{:S(2)}) %all-to-all-start.1) | async-done | bytes 983072 | tf_op jit(solution)/shard_map/all_to_all | solution.py:183
  55.7 4.4 %all-to-all-start.2 = ((bf16[32,2,16,128]{3,2,1,0:T(8,128)(2,1)}), bf16[32,2,16,128]{3,2,1,0:T(8,128)(2,1)S(1)}, u32[]{:S(2)}, u32[]{:S(2)}) async-start(bf16[32,2,16,128]{3,2,1,0:T(8,128)(2,1)} %bitcast.96), calls=%async_computation.2 | async-start | bytes 524288 | tf_op jit(solution)/shard_map/all_to_all | solution.py:197
  60.1 0.7 fusion.8
  60.8 11.3 %all-to-all-done.2 = bf16[32,2,16,128]{3,2,1,0:T(8,128)(2,1)S(1)} async-done(((bf16[32,2,16,128]{3,2,1,0:T(8,128)(2,1)}), bf16[32,2,16,128]{3,2,1,0:T(8,128)(2,1)S(1)}, u32[]{:S(2)}, u32[]{:S(2)}) %all-to-all-start.2) | async-done | bytes 262176 | tf_op jit(solution)/shard_map/all_to_all | solution.py:197
  72.1 0.9 broadcast_in_dim.38
  73.1 8.8 %all-to-all-start.3 = ((bf16[32,48,192]{2,1,0:T(8,128)(2,1)}), bf16[32,48,192]{2,1,0:T(8,128)(2,1)}, u32[]{:S(2)}, u32[]{:S(2)}) async-start(bf16[32,48,192]{2,1,0:T(8,128)(2,1)} %broadcast_in_dim.38), calls=%async_computation.3 | async-start | bytes 1572864 | tf_op jit(solution)/shard_map/all_to_all | solution.py:200
  81.9 0.0 all-gather.8.cloned.1.call-start
  82.0 1.2 multiply_cosine_fusion.1
  83.2 13.5 %all-to-all-done.3 = bf16[32,48,192]{2,1,0:T(8,128)(2,1)} async-done(((bf16[32,48,192]{2,1,0:T(8,128)(2,1)}), bf16[32,48,192]{2,1,0:T(8,128)(2,1)}, u32[]{:S(2)}, u32[]{:S(2)}) %all-to-all-start.3) | async-done | bytes 589856 | tf_op jit(solution)/shard_map/all_to_all | solution.py:200
  96.7 2.3 copy.42
  99.0 2.5 reshape.376
  101.5 2.9 fusion.20
  104.4 0.8 fusion.10
  105.2 1.5 copy.38
  106.7 1.2 fusion.39
  107.9 0.1 subtract_convert_fusion
  108.0 0.8 maximum_bitcast_fusion
  108.8 1.1 convolution_bitcast_fusion
  109.9 0.6 fusion.69
  110.5 1.7 convolution_convert_fusion.1
  112.3 0.2 reshape.372
  112.5 0.7 fusion.80
  113.3 0.3 copy.46
  113.6 0.9 copy.47
  114.5 6.9 %fusion.86 = (f32[3,512]{1,0:T(4,128)S(1)}, f32[3,512,2048]{2,1,0:T(8,128)}) fusion(pred[512,2048]{1,0:T(8,128)(4,1)S(1)} %copy-done.7, bf16[3,1024,64]{1,2,0:T(8,128)(2,1)S(1)} %copy-done.11, bf16[1024,32]{0,1:T(8,128)(2,1)S(1)} %get-tuple-element.38, bf16[1024,32]{0,1:T(8,128)(2,1)S(1)} %get-tuple-element.37, bf16[1024,64]{0,1:T(8,128)(2,1)S(1)} %bitcast.99), kind=kOutput, calls=%fused_computation.103 | convolution fusion | flops 416024576 | bytes 14096384 | tf_op jit(solution)/shard_map/sub | solution.py:247
  121.5 4.0 %all-to-all-start.4 = ((bf16[8,192,1024]{2,1,0:T(8,128)(2,1)}), bf16[8,192,1024]{2,1,0:T(8,128)(2,1)S(1)}, u32[]{:S(2)}, u32[]{:S(2)}) async-start(bf16[8,192,1024]{2,1,0:T(8,128)(2,1)} %all-gather.6.cloned.1.call-done), calls=%async_computation.4 | async-start | bytes 6291456 | tf_op jit(solution)/shard_map/all_to_all | solution.py:209
  125.5 6.8 %fusion.38 = bf16[3,512,64]{1,2,0:T(8,128)(2,1)S(1)} fusion(f32[3,512,2048]{2,1,0:T(8,128)} %get-tuple-element.46, f32[3,512]{1,0:T(4,128)S(1)} %get-tuple-element.45, bf16[1024,64]{0,1:T(8,128)(2,1)S(1)} %copy-done.12, bf16[1024,64]{0,1:T(8,128)(2,1)} %bitcast.97), kind=kOutput, calls=%fused_computation.42 | convolution fusion | flops 409567232 | bytes 13047808 | tf_op jit(solution)/shard_map/gqk,kd->gqd/dot_general | solution.py:250
  132.3 10.5 %fusion.81 = (f32[3,512]{1,0:T(4,128)S(1)}, f32[3,512,2048]{2,1,0:T(8,128)}) fusion(pred[512,2048]{1,0:T(8,128)(4,1)} %get-tuple-element.40, bf16[3,1024,64]{1,2,0:T(8,128)(2,1)} %maximum_bitcast_fusion, bf16[1024,32]{0,1:T(8,128)(2,1)} %copy-done.15, bf16[1024,32]{0,1:T(8,128)(2,1)} %copy-done.14, bf16[1024,64]{0,1:T(8,128)(2,1)} %bitcast.100), kind=kOutput, calls=%fused_computation.102 | convolution fusion | flops 416024576 | bytes 14096384 | tf_op jit(solution)/shard_map/sub | solution.py:247
  142.8 6.8 %fusion.37 = bf16[3,512,64]{1,2,0:T(8,128)(2,1)S(1)} fusion(f32[3,512,2048]{2,1,0:T(8,128)} %get-tuple-element.44, f32[3,512]{1,0:T(4,128)S(1)} %get-tuple-element.43, bf16[1024,64]{0,1:T(8,128)(2,1)S(1)} %copy-done.12, bf16[1024,64]{0,1:T(8,128)(2,1)} %bitcast.98), kind=kOutput, calls=%fused_computation.41 | convolution fusion | flops 409567232 | bytes 13047808 | tf_op jit(solution)/shard_map/gqk,kd->gqd/dot_general | solution.py:250
  149.6 0.8 pad_maximum_fusion
  150.4 20.7 %all-to-all-done.4 = bf16[8,192,1024]{2,1,0:T(8,128)(2,1)S(1)} async-done(((bf16[8,192,1024]{2,1,0:T(8,128)(2,1)}), bf16[8,192,1024]{2,1,0:T(8,128)(2,1)S(1)}, u32[]{:S(2)}, u32[]{:S(2)}) %all-to-all-start.4) | async-done | bytes 3145760 | tf_op jit(solution)/shard_map/all_to_all | solution.py:209
  171.1 2.1 copy_bitcast_fusion
  173.2 4.9 %all-to-all-start.5 = ((bf16[8,128,192]{1,2,0:T(8,128)(2,1)}), bf16[8,128,192]{1,2,0:T(8,128)(2,1)}, u32[]{:S(2)}, u32[]{:S(2)}) async-start(bf16[8,128,192]{1,2,0:T(8,128)(2,1)} %copy_bitcast_fusion), calls=%async_computation.5 | async-start | bytes 786432 | tf_op jit(solution)/shard_map/all_to_all | solution.py:258
  178.1 0.9 reshape.381
  179.1 1.0 constant_dynamic-slice_fusion.rows_ref
  180.1 5.9 %all-to-all-done.5 = bf16[8,128,192]{1,2,0:T(8,128)(2,1)} async-done(((bf16[8,128,192]{1,2,0:T(8,128)(2,1)}), bf16[8,128,192]{1,2,0:T(8,128)(2,1)}, u32[]{:S(2)}, u32[]{:S(2)}) %all-to-all-start.5) | async-done | bytes 393248 | tf_op jit(solution)/shard_map/all_to_all | solution.py:258
  186.0 1.2 copy.45.parts_ref
  187.3 2.3 copy-done.3
  189.6 4.8 %project_and_dispatch.1 = (f32[128,1536]{1,0:T(8,128)S(1)}, bf16[1536,1536]{1,0:T(8,128)(2,1)S(1)}, bf16[1536,128]{1,0:T(8,128)(2,1)S(1)}, bf16[1536,128]{1,0:T(8,128)(2,1)S(1)}) custom-call(bf16[8,128,192]{2,1,0:T(8,128)(2,1)S(1)} %copy.45.parts_ref, bf16[8,2,96,1536]{3,2,1,0:T(8,128)(2,1)S(1)} %bitcast.84, ...), custom_call_target="tpu_custom_call" | custom-call | flops 1207959552 | bytes 9437184 | tf_op jit(solution)/shard_map/project_and_dispatch/pallas_call | solution.py:119
  194.4 2.1 copy-done.2
  196.5 7.4 %all-to-all-start.6 = ((bf16[32,48,1536]{2,1,0:T(8,128)(2,1)}), bf16[32,48,1536]{2,1,0:T(8,128)(2,1)}, u32[]{:S(2)}, u32[]{:S(2)}) async-start(bf16[32,48,1536]{2,1,0:T(8,128)(2,1)} %bitcast.83), calls=%async_computation.6 | async-start | bytes 9437184 | tf_op jit(solution)/shard_map/all_to_all | solution.py:271
  204.0 0.0 all-gather.10.cloned.1.call-start
  204.0 0.7 convert_bitcast_fusion
  204.7 34.2 %all-gather.10.cloned.1.call-done = bf16[512,1536]{1,0:T(8,128)(2,1)} async-done(((bf16[64,1536]{1,0:T(8,128)(2,1)}), bf16[512,1536]{1,0:T(8,128)(2,1)}) %all-gather.10.cloned.1.call-update) | async-done | bytes 1572880 | tf_op jit(solution)/shard_map/all_gather | solution.py:278
  239.0 27.0 %all-to-all-done.6 = bf16[32,48,1536]{2,1,0:T(8,128)(2,1)} async-done(((bf16[32,48,1536]{2,1,0:T(8,128)(2,1)}), bf16[32,48,1536]{2,1,0:T(8,128)(2,1)}, u32[]{:S(2)}, u32[]{:S(2)}) %all-to-all-start.6) | async-done | bytes 4718624 | tf_op jit(solution)/shard_map/all_to_all | solution.py:271
  265.9 3.8 all-to-all-start.7
  269.7 9.8 %fusion.91 = f32[1536,1024]{1,0:T(8,128)} fusion(bf16[1536,1536]{1,0:T(8,128)(2,1)} %bitcast.29, bf16[1536,1024]{1,0:T(8,128)(2,1)} %bitcast.91), kind=kOutput, calls=%fused_computation.104 | convolution fusion | flops 4831838208 | bytes 14155776 | tf_op jit(solution)/shard_map/dot_general | solution.py:281
  279.5 13.3 %all-to-all-done.7 = bf16[8,64,1536]{2,1,0:T(8,128)(2,1)S(1)} async-done(((bf16[8,64,1536]{2,1,0:T(8,128)(2,1)}), bf16[8,64,1536]{2,1,0:T(8,128)(2,1)S(1)}, u32[]{:S(2)}, u32[]{:S(2)}) %all-to-all-start.7) | async-done | bytes 1572896 | tf_op jit(solution)/shard_map/all_to_all | solution.py:280
  292.8 7.8 %convolution_convert_fusion = bf16[1536,1536]{1,0:T(8,128)(2,1)} fusion(bf16[512,1536]{1,0:T(8,128)(2,1)S(1)} %bitcast.94, f32[1536,1024]{1,0:T(8,128)} %fusion.91), kind=kOutput, calls=%fused_computation.17 | convolution fusion | flops 2422996992 | bytes 12582912 | tf_op jit(solution)/shard_map/dot_general | solution.py:283
  300.6 6.0 %all-to-all-start.8 = ((bf16[32,48,1536]{2,1,0:T(8,128)(2,1)}), bf16[32,48,1536]{2,1,0:T(8,128)(2,1)}, u32[]{:S(2)}, u32[]{:S(2)}) async-start(bf16[32,48,1536]{2,1,0:T(8,128)(2,1)} %bitcast.90), calls=%async_computation.8 | async-start | bytes 9437184 | tf_op jit(solution)/shard_map/all_to_all | solution.py:284
  306.6 62.0 %all-to-all-done.8 = bf16[32,48,1536]{2,1,0:T(8,128)(2,1)} async-done(((bf16[32,48,1536]{2,1,0:T(8,128)(2,1)}), bf16[32,48,1536]{2,1,0:T(8,128)(2,1)}, u32[]{:S(2)}, u32[]{:S(2)}) %all-to-all-start.8) | async-done | bytes 4718624 | tf_op jit(solution)/shard_map/all_to_all | solution.py:284
  368.6 6.0 %fusion.28 = bf16[128,1536]{1,0:T(8,128)(2,1)} fusion(f32[128,1536]{1,0:T(8,128)S(1)} %get-tuple-element.25, bf16[1536,1536]{1,0:T(8,128)(2,1)} %bitcast.32, bf16[1536,128]{1,0:T(8,128)(2,1)S(1)} %get-tuple-element.27, bf16[1536,128]{1,0:T(8,128)(2,1)S(1)} %get-tuple-element.26, pred[128]{0:T(512)(128)(4,1)S(1)} %add_compare_fusion), kind=kOutput, calls=%fused_computation.37 | convolution fusion | flops 1228996608 | bytes 6684800 | tf_op jit(solution)/shard_map/dot_general | solution.py:288
  (56 shorter events, 0.3 us)
Async XLA Ops:
  6.5 34.9 %copy-start = (bf16[8,16,128]{2,1,0:T(8,128)(2,1)S(1)}, bf16[8,16,128]{2,1,0:T(8,128)(2,1)}, u32[]{:S(2)}) copy-start(bf16[8,16,128]{2,1,0:T(8,128)(2,1)} %param.21) | copy-start | bytes 98308
  6.5 34.7 %copy-start.19 = (s32[32,1,2]{0,2,1:T(2,128)S(1)}, s32[32,1,2]{0,2,1:T(2,128)}, u32[]{:S(2)}) copy-start(s32[32,1,2]{0,2,1:T(2,128)} %param.22) | copy-start | bytes 772
  6.5 53.6 %copy-start.16 = (f32[192,48]{0,1:T(8,128)S(1)}, f32[192,48]{0,1:T(8,128)}, u32[]{:S(2)}) copy-start(f32[192,48]{0,1:T(8,128)} %param.20) | copy-start | bytes 110596
  6.5 53.6 %copy-start.5 = (bf16[1024,1536]{1,0:T(8,128)(2,1)S(1)}, bf16[1024,1536]{1,0:T(8,128)(2,1)}, u32[]{:S(2)}) copy-start(bf16[1024,1536]{1,0:T(8,128)(2,1)} %param.14) | copy-start | bytes 9437188
  6.5 94.9 %all-gather.6.cloned.1.call-start = ((), (), s32[]{:S(2)}) async-start(), calls=%async_computation.9 | async-start | bytes 3538944 | tf_op jit(solution)/shard_map/all_gather | solution.py:176
  32.1 23.6 %all-to-all-start.1 = ((bf16[4,8,48,320]{3,2,1,0:T(8,128)(2,1)}), bf16[4,8,48,320]{3,2,1,0:T(8,128)(2,1)}, u32[]{:S(2)}, u32[]{:S(2)}) async-start(bf16[4,8,48,320]{3,2,1,0:T(8,128)(2,1)} %broadcast_in_dim.35), calls=%async_computation.1 | async-start | bytes 2359296 | tf_op jit(solution)/shard_map/all_to_all | solution.py:183
  55.7 16.4 %all-to-all-start.2 = ((bf16[32,2,16,128]{3,2,1,0:T(8,128)(2,1)}), bf16[32,2,16,128]{3,2,1,0:T(8,128)(2,1)S(1)}, u32[]{:S(2)}, u32[]{:S(2)}) async-start(bf16[32,2,16,128]{3,2,1,0:T(8,128)(2,1)} %bitcast.96), calls=%async_computation.2 | async-start | bytes 524288 | tf_op jit(solution)/shard_map/all_to_all | solution.py:197
  60.8 43.6 %copy-start.17 = (f32[1536]{0:T(1024)S(1)}, f32[1536]{0:T(1024)}, u32[]{:S(2)}) copy-start(f32[1536]{0:T(1024)} %param.16) | copy-start | bytes 18436
  73.1 23.6 %all-to-all-start.3 = ((bf16[32,48,192]{2,1,0:T(8,128)(2,1)}), bf16[32,48,192]{2,1,0:T(8,128)(2,1)}, u32[]{:S(2)}, u32[]{:S(2)}) async-start(bf16[32,48,192]{2,1,0:T(8,128)(2,1)} %broadcast_in_dim.38), calls=%async_computation.3 | async-start | bytes 1572864 | tf_op jit(solution)/shard_map/all_to_all | solution.py:200
  81.9 105.4 %all-gather.8.cloned.1.call-start = ((), (), s32[]{:S(2)}) async-start(), calls=%async_computation.10 | async-start | bytes 5308416 | tf_op jit(solution)/shard_map/all_gather | solution.py:208
  105.2 2.7 copy-start.8
  105.2 2.7 copy-start.9
  109.9 4.6 %copy-start.7 = (pred[512,2048]{1,0:T(8,128)(4,1)S(1)}, pred[512,2048]{1,0:T(8,128)(4,1)}, u32[]{:S(2)}) copy-start(pred[512,2048]{1,0:T(8,128)(4,1)} %get-tuple-element.39) | copy-start | bytes 3145732
  110.5 11.0 %copy-start.14 = (bf16[1024,32]{0,1:T(8,128)(2,1)}, bf16[1024,32]{0,1:T(8,128)(2,1)S(1)}, u32[]{:S(2)}) copy-start(bf16[1024,32]{0,1:T(8,128)(2,1)S(1)} %get-tuple-element.37) | copy-start | bytes 196612
  110.5 11.0 %copy-start.15 = (bf16[1024,32]{0,1:T(8,128)(2,1)}, bf16[1024,32]{0,1:T(8,128)(2,1)S(1)}, u32[]{:S(2)}) copy-start(bf16[1024,32]{0,1:T(8,128)(2,1)S(1)} %get-tuple-element.38) | copy-start | bytes 196612
  110.5 4.0 %copy-start.11 = (bf16[3,1024,64]{1,2,0:T(8,128)(2,1)S(1)}, bf16[3,1024,64]{1,2,0:T(8,128)(2,1)}, u32[]{:S(2)}) copy-start(bf16[3,1024,64]{1,2,0:T(8,128)(2,1)} %maximum_bitcast_fusion) | copy-start | bytes 1179652
  113.6 7.9 %copy-start.13 = (bf16[1024,1,1,64]{0,3,2,1:T(8,128)(2,1)}, bf16[1024,1,1,64]{0,3,2,1:T(8,128)(2,1)S(1)}, u32[]{:S(2)}) copy-start(bf16[1024,1,1,64]{0,3,2,1:T(8,128)(2,1)S(1)} %copy.46) | copy-start | bytes 393220
  121.5 4.0 %copy-start.12 = (bf16[1024,64]{0,1:T(8,128)(2,1)S(1)}, bf16[1024,64]{0,1:T(8,128)(2,1)}, u32[]{:S(2)}) copy-start(bf16[1024,64]{0,1:T(8,128)(2,1)} %convolution_convert_fusion.1) | copy-start | bytes 393220
  121.5 49.6 %all-to-all-start.4 = ((bf16[8,192,1024]{2,1,0:T(8,128)(2,1)}), bf16[8,192,1024]{2,1,0:T(8,128)(2,1)S(1)}, u32[]{:S(2)}, u32[]{:S(2)}) async-start(bf16[8,192,1024]{2,1,0:T(8,128)(2,1)} %all-gather.6.cloned.1.call-done), calls=%async_computation.4 | async-start | bytes 6291456 | tf_op jit(solution)/shard_map/all_to_all | solution.py:209
  142.8 36.3 %copy-start.18 = (f32[1536]{0:T(1024)S(1)}, f32[1536]{0:T(1024)}, u32[]{:S(2)}) copy-start(f32[1536]{0:T(1024)} %param.23) | copy-start | bytes 18436
  142.8 44.5 %copy-start.4 = (s32[128,8]{0,1:T(8,128)S(1)}, s32[128,8]{0,1:T(8,128)}, u32[]{:S(2)}) copy-start(s32[128,8]{0,1:T(8,128)} %param.25) | copy-start | bytes 12292
  171.1 7.0 %copy-start.6 = (bf16[8,192,1024]{2,1,0:T(8,128)(2,1)}, bf16[8,192,1024]{2,1,0:T(8,128)(2,1)S(1)}, u32[]{:S(2)}) copy-start(bf16[8,192,1024]{2,1,0:T(8,128)(2,1)S(1)} %all-to-all-done.4) | copy-start | bytes 9437188
  173.2 12.8 %all-to-all-start.5 = ((bf16[8,128,192]{1,2,0:T(8,128)(2,1)}), bf16[8,128,192]{1,2,0:T(8,128)(2,1)}, u32[]{:S(2)}, u32[]{:S(2)}) async-start(bf16[8,128,192]{1,2,0:T(8,128)(2,1)} %copy_bitcast_fusion), calls=%async_computation.5 | async-start | bytes 786432 | tf_op jit(solution)/shard_map/all_to_all | solution.py:258
  187.3 2.3 copy-start.3
  194.4 2.1 copy-start.2
  196.5 7.5 %copy-start.10 = (f32[1,64,1536]{2,1,0:T(8,128)S(1)}, f32[1,64,1536]{2,1,0:T(8,128)}, u32[]{:S(2)}) copy-start(f32[1,64,1536]{2,1,0:T(8,128)} %param.27) | copy-start | bytes 1179652
  196.5 69.4 %all-to-all-start.6 = ((bf16[32,48,1536]{2,1,0:T(8,128)(2,1)}), bf16[32,48,1536]{2,1,0:T(8,128)(2,1)}, u32[]{:S(2)}, u32[]{:S(2)}) async-start(bf16[32,48,1536]{2,1,0:T(8,128)(2,1)} %bitcast.83), calls=%async_computation.6 | async-start | bytes 9437184 | tf_op jit(solution)/shard_map/all_to_all | solution.py:271
  204.0 35.0 %all-gather.10.cloned.1.call-start = ((), (), s32[]{:S(2)}) async-start(), calls=%async_computation.11 | async-start | bytes 1769472 | tf_op jit(solution)/shard_map/all_gather | solution.py:278
  265.9 26.9 %all-to-all-start.7 = ((bf16[8,64,1536]{2,1,0:T(8,128)(2,1)}), bf16[8,64,1536]{2,1,0:T(8,128)(2,1)S(1)}, u32[]{:S(2)}, u32[]{:S(2)}) async-start(bf16[8,64,1536]{2,1,0:T(8,128)(2,1)} %bitcast.93), calls=%async_computation.7 | async-start | bytes 3145728 | tf_op jit(solution)/shard_map/all_to_all | solution.py:280
  300.6 67.9 %all-to-all-start.8 = ((bf16[32,48,1536]{2,1,0:T(8,128)(2,1)}), bf16[32,48,1536]{2,1,0:T(8,128)(2,1)}, u32[]{:S(2)}, u32[]{:S(2)}) async-start(bf16[32,48,1536]{2,1,0:T(8,128)(2,1)} %bitcast.90), calls=%async_computation.8 | async-start | bytes 9437184 | tf_op jit(solution)/shard_map/all_to_all | solution.py:284
  368.6 6.0 %copy-start.1 = (bf16[8,16,128]{2,1,0:T(8,128)(2,1)S(1)}, bf16[8,16,128]{2,1,0:T(8,128)(2,1)}, u32[]{:S(2)}) copy-start(bf16[8,16,128]{2,1,0:T(8,128)(2,1)} %param.21) | copy-start | bytes 98308
Sparse Core Ops, SparseCore 0:
  9.2 50.6 all-gather.5
  101.6 52.0 all-gather.7
  206.6 32.3 all-gather.9

commit v3 on v2

v3 whole, which is shorter than its diff:
```python
import math

import jax
import jax.numpy as jnp
from jax import lax
from jax.experimental import pallas as pl
from jax.experimental.pallas import tpu as pltpu
from jax.sharding import PartitionSpec as P

HEAD_WIDTH = 64
FF = 512
CAPACITY = 48
HALF = CAPACITY // 2
EXPERTS = 32


epsilon = 1e-05

Z_GROUPS = [[y * 16 + z * 2 + c for z in range(8)] for y in range(2) for c in range(2)]
CHIP_PAIR_GROUPS = [[y * 16 + z * 2 + c for y in range(2) for c in range(2)] for z in range(8)]
PLANE_GROUPS = [
    [(y * 16 + z * 2 + c) * 8 + t for y in range(2) for c in range(2) for t in range(8)]
    for z in range(8)
]


def rms_scale(values, norm_gain):
    mean_square = jnp.mean(values * values, axis=-1, keepdims=True)
    return values * lax.rsqrt(mean_square + epsilon) * norm_gain


def rotary_tables(positions, first_position):
    lane = jnp.arange(2 * HEAD_WIDTH)
    frequency = jnp.exp(
        (lane % (HEAD_WIDTH // 2)).astype(jnp.float32) * (-2.0 * math.log(10000.0) / HEAD_WIDTH)
    )
    angles = (first_position + jnp.arange(positions)).astype(jnp.float32)[:, None] * frequency
    sign = jnp.where(lane % HEAD_WIDTH < HEAD_WIDTH // 2, -1.0, 1.0)
    return jnp.cos(angles), jnp.sin(angles) * sign


def attention_body(
    length_ref, tokens_ref, gain_ref, weight_ref, pages_ref, cosine_ref, sine_ref,
    out_ref, queries, keys, values,
):
    seq_len = tokens_ref.shape[0]
    prefix = pages_ref.shape[0]
    heads = queries.shape[0]
    chunk = 256
    lane = lax.broadcasted_iota(jnp.int32, (chunk, 256), 1)
    ones = jnp.ones((chunk, HEAD_WIDTH), jnp.bfloat16)
    for c in range(0, prefix, chunk):
        rows = pages_ref[c : c + chunk, :]
        keys[:, c : c + chunk] = rows.astype(jnp.float32).T[:HEAD_WIDTH].astype(jnp.bfloat16)
        values[c : c + chunk, :] = jnp.concatenate([rows[:, HEAD_WIDTH:], ones], axis=1)
    for c in range(0, seq_len, chunk):
        normalized = rms_scale(
            tokens_ref[c : c + chunk, :].astype(jnp.float32), gain_ref[...]
        ).astype(jnp.bfloat16)
        projected = jnp.dot(normalized, weight_ref[...], preferred_element_type=jnp.float32)
        plain = projected[:, :256]
        partner = jnp.where(
            lane % HEAD_WIDTH < HEAD_WIDTH // 2,
            pltpu.roll(plain, 256 - HEAD_WIDTH // 2, 1),
            pltpu.roll(plain, HEAD_WIDTH // 2, 1),
        )
        cosine = cosine_ref[c : c + chunk, :]
        sine = sine_ref[c : c + chunk, :]
        rotated = plain * jnp.concatenate([cosine, cosine], axis=1) + partner * jnp.concatenate(
            [sine, sine], axis=1
        )
        rounded = rotated.astype(jnp.bfloat16)
        for h in range(heads):
            queries[h, c : c + chunk, :] = (
                rounded[:, h * HEAD_WIDTH : (h + 1) * HEAD_WIDTH] * HEAD_WIDTH ** (-0.5)
            ).astype(jnp.bfloat16)
        keys[:, prefix + c : prefix + c + chunk] = (
            rotated.T[heads * HEAD_WIDTH :].astype(jnp.bfloat16)
        )
        values[prefix + c : prefix + c + chunk, :] = jnp.concatenate(
            [projected[:, 256 : 256 + HEAD_WIDTH].astype(jnp.bfloat16), ones], axis=1
        )
    block = out_ref.shape[1]
    length = length_ref[0]
    column = lax.broadcasted_iota(jnp.int32, (block, seq_len), 1)
    row = lax.broadcasted_iota(jnp.int32, (block, seq_len), 0)

    def one_block(i, carry):
        start = pl.multiple_of(i * block, block)
        allowed = (column <= row + start) & (column < length)
        outs = []
        for h in range(heads):
            query = queries[h, pl.ds(start, block), :]
            cached = jnp.dot(query, keys[:, :prefix], preferred_element_type=jnp.float32)
            own = jnp.dot(query, keys[:, prefix:], preferred_element_type=jnp.float32)
            own = jnp.where(allowed, own, -1e30)
            top = jnp.maximum(
                jnp.max(cached, axis=1, keepdims=True), jnp.max(own, axis=1, keepdims=True)
            )
            total = jnp.dot(
                jnp.exp(cached - top).astype(jnp.bfloat16),
                values[:prefix, :],
                preferred_element_type=jnp.float32,
            ) + jnp.dot(
                jnp.exp(own - top).astype(jnp.bfloat16),
                values[prefix:, :],
                preferred_element_type=jnp.float32,
            )
            outs.append(total[:, :HEAD_WIDTH] / total[:, HEAD_WIDTH : HEAD_WIDTH + 1])
        out_ref[i] = jnp.concatenate(outs, axis=1).astype(jnp.bfloat16)
        return carry

    lax.fori_loop(0, out_ref.shape[0], one_block, 0)


def attention(lengths, tokens, gain, weight, pages, cosine, sine, blocks):
    seq_len, model_width = tokens.shape
    heads = 3
    total = seq_len + pages.shape[0]
    vmem = pl.BlockSpec(memory_space=pltpu.VMEM)
    return pl.pallas_call(
        attention_body,
        out_shape=jax.ShapeDtypeStruct((blocks, seq_len // blocks, heads * HEAD_WIDTH), jnp.bfloat16),
        in_specs=[pl.BlockSpec(memory_space=pltpu.SMEM)] + [vmem] * 6,
        out_specs=vmem,
        scratch_shapes=[
            pltpu.VMEM((heads, seq_len, HEAD_WIDTH), jnp.bfloat16),
            pltpu.VMEM((HEAD_WIDTH, total), jnp.bfloat16),
            pltpu.VMEM((total, 2 * HEAD_WIDTH), jnp.bfloat16),
        ],
        compiler_params=pltpu.CompilerParams(vmem_limit_bytes=40 << 20),
        cost_estimate=pl.CostEstimate(
            flops=30_000_000_000, bytes_accessed=8 << 20, transcendentals=heads * seq_len * total
        ),
        name="attention",
    )(lengths, tokens, gain.reshape(1, model_width), weight, pages, cosine, sine)


def project_body(
    parts_ref, weight_hbm, rows_ref, gain_ref, router_ref, ids_ref,
    hidden_ref, first_ref, second_ref, high_ref, low_ref,
    weight, attended, place, sem,
):
    copies = []
    for z in range(8):
        for y in range(2):
            copy = pltpu.make_async_copy(
                weight_hbm.at[z, y], weight.at[pl.ds((y * 8 + z) * 96, 96)], sem.at[z * 2 + y]
            )
            copy.start()
            copies.append(copy)
    for t in range(8):
        attended[:, t * 192 : (t + 1) * 192] = parts_ref[t]
    tokens = rows_ref.shape[0]
    host = lax.broadcasted_iota(jnp.int32, (EXPERTS, tokens), 0)
    expert_at = (host // 16) * 16 + (host % 8) * 2 + (host // 8) % 2
    chosen = jnp.zeros((EXPERTS, tokens), jnp.float32)
    for k in range(ids_ref.shape[0]):
        chosen = jnp.where(ids_ref[k : k + 1, :] == expert_at, 1.0, chosen)
    earlier = lax.broadcasted_iota(jnp.int32, (tokens, tokens), 0) < lax.broadcasted_iota(
        jnp.int32, (tokens, tokens), 1
    )
    rank = jnp.dot(
        chosen.astype(jnp.bfloat16),
        jnp.where(earlier, 1.0, 0.0).astype(jnp.bfloat16),
        preferred_element_type=jnp.float32,
    )
    rank = jnp.where(chosen > 0.0, rank, -1.0)
    slot = lax.broadcasted_iota(jnp.int32, (HALF, tokens), 0).astype(jnp.float32)
    for half in range(2):
        for g in range(EXPERTS):
            at = (half * EXPERTS + g) * HALF
            place[at : at + HALF, :] = jnp.where(
                rank[g : g + 1, :] == slot + float(half * HALF), 1.0, 0.0
            ).astype(jnp.bfloat16)
    for copy in copies:
        copy.wait()
    for c in range(0, 1536, 256):
        hidden_ref[:, c : c + 256] = rows_ref[:, c : c + 256].astype(jnp.float32) + lax.dot_general(
            attended[...],
            weight[c : c + 256, :],
            (((1,), (1,)), ((), ())),
            preferred_element_type=jnp.float32,
        )
    hidden = hidden_ref[...]
    moe_in = rms_scale(hidden, gain_ref[...]).astype(jnp.bfloat16)
    for half, send_ref in enumerate((first_ref, second_ref)):
        for c in range(0, EXPERTS * HALF, 256):
            at = half * EXPERTS * HALF + c
            send_ref[c : c + 256, :] = jnp.dot(
                place[at : at + 256, :], moe_in, preferred_element_type=jnp.float32
            ).astype(jnp.bfloat16)
    logits = lax.dot_general(
        router_ref[...], moe_in, (((1,), (1,)), ((), ())), preferred_element_type=jnp.float32
    )
    top_logit = jnp.max(jnp.where(chosen > 0.0, logits, -3e38), axis=0, keepdims=True)
    raised = jnp.where(chosen > 0.0, jnp.exp(jnp.minimum(logits - top_logit, 0.0)), 0.0)
    gates = raised / jnp.sum(raised, axis=0, keepdims=True)
    for half in range(2):
        for g in range(EXPERTS):
            at = (half * EXPERTS + g) * HALF
            weigh = place[at : at + HALF, :].astype(jnp.float32) * gates[g : g + 1, :]
            high = weigh.astype(jnp.bfloat16)
            high_ref[at : at + HALF, :] = high
            low_ref[at : at + HALF, :] = (weigh - high.astype(jnp.float32)).astype(jnp.bfloat16)


def project_and_dispatch(parts, output_weight, own_rows, moe_gain, router_hosted, ids_by_choice):
    row_count, model_width = own_rows.shape
    slots = EXPERTS * CAPACITY
    vmem = pl.BlockSpec(memory_space=pltpu.VMEM)
    return pl.pallas_call(
        project_body,
        out_shape=(
            jax.ShapeDtypeStruct((row_count, model_width), jnp.float32),
            jax.ShapeDtypeStruct((slots // 2, model_width), jnp.bfloat16),
            jax.ShapeDtypeStruct((slots // 2, model_width), jnp.bfloat16),
            jax.ShapeDtypeStruct((slots, row_count), jnp.bfloat16),
            jax.ShapeDtypeStruct((slots, row_count), jnp.bfloat16),
        ),
        in_specs=[vmem, pl.BlockSpec(memory_space=pltpu.HBM), vmem, vmem, vmem, vmem],
        out_specs=(vmem, vmem, vmem, vmem, vmem),
        scratch_shapes=[
            pltpu.VMEM((model_width, model_width), jnp.bfloat16),
            pltpu.VMEM((row_count, model_width), jnp.bfloat16),
            pltpu.VMEM((slots, row_count), jnp.bfloat16),
            pltpu.SemaphoreType.DMA((16,)),
        ],
        compiler_params=pltpu.CompilerParams(vmem_limit_bytes=40 << 20),
        cost_estimate=pl.CostEstimate(
            flops=4 * row_count * model_width * model_width,
            bytes_accessed=4 * model_width * model_width,
            transcendentals=0,
        ),
        name="project_and_dispatch",
    )(
        parts,
        output_weight.reshape(8, 2, 96, model_width),
        own_rows,
        moe_gain.reshape(1, model_width),
        router_hosted,
        ids_by_choice,
    )


def on_device(
    tokens_in,
    lengths,
    attn_gain,
    q_proj,
    k_proj,
    value_projection,
    o_proj,
    key_value_pages,
    page_table,
    moe_gain,
    router,
    expert_ids,
    gate_up_proj,
    down_proj,
):
    seq_len, model_width = tokens_in.shape
    barrier = lax.optimization_barrier
    tp_index = lax.axis_index("tp")
    row_count = seq_len // 8

    def in_plane(rows):
        return lax.all_to_all(
            rows, ("ep", "tp"), 0, 0, axis_index_groups=PLANE_GROUPS, tiled=True
        )

    gate_up_planes = lax.all_gather(
        gate_up_proj[0].astype(jnp.bfloat16), "ep", axis_index_groups=Z_GROUPS
    )
    output_shard = o_proj.T.astype(jnp.bfloat16)
    output_plane = in_plane(jnp.broadcast_to(output_shard[None], (EXPERTS, *output_shard.shape)))
    output_plane = (
        output_plane.reshape(4, 8, 48, 192).transpose(0, 2, 1, 3).reshape(192, model_width)
    )
    output_weight = lax.all_gather(output_plane, "ep", axis_index_groups=Z_GROUPS)

    weight_shard = jnp.concatenate(
        [q_proj, k_proj, value_projection, jnp.zeros_like(k_proj)], axis=1
    ).astype(jnp.bfloat16)
    slabs = weight_shard.reshape(48, 3, 128).transpose(1, 0, 2).reshape(144, 128)
    pages = key_value_pages[page_table[:, 0, :]].reshape(2, 8, 2, 32, 128)
    payload = jnp.concatenate(
        [
            jnp.broadcast_to(slabs[None], (8, 144, 128)),
            pages.transpose(1, 0, 2, 3, 4).reshape(8, 128, 128),
        ],
        axis=1,
    )
    payload, output_plane = barrier((payload, output_plane))
    along_z = lax.all_to_all(payload, "ep", 0, 0, axis_index_groups=Z_GROUPS, tiled=True)
    payload = jnp.concatenate(
        [
            jnp.broadcast_to(along_z[None, :, :144], (4, 8, 144, 128)),
            along_z[:, 144:].reshape(8, 4, 32, 128).transpose(1, 0, 2, 3),
        ],
        axis=2,
    )
    across = lax.all_to_all(payload, "ep", 0, 0, axis_index_groups=CHIP_PAIR_GROUPS, tiled=True)
    weight = (
        across[:, :, :144]
        .reshape(2, 2, 8, 3, 48, 128)
        .transpose(0, 2, 1, 4, 3, 5)
        .reshape(model_width, 384)
    )
    prefix = across[:, :, 144:].reshape(2, 2, 8, 32, 128).transpose(0, 2, 1, 3, 4).reshape(-1, 128)
    cosine, sine = rotary_tables(seq_len, prefix.shape[0])
    weight, prefix, gate_up_planes = barrier((weight, prefix, gate_up_planes))
    gate_up_full = lax.all_to_all(gate_up_planes, "tp", 0, 0, tiled=True).reshape(model_width, -1)
    attended = attention(lengths, tokens_in, attn_gain, weight, prefix, cosine, sine, 8)
    attended, gate_up_full = barrier((attended, gate_up_full))
    attn_parts = lax.all_to_all(attended, "tp", 0, 0, tiled=True)
    own_rows = lax.dynamic_slice_in_dim(tokens_in, tp_index * row_count, row_count, 0)
    router_hosted = router.T.reshape(2, 8, 2, model_width).transpose(0, 2, 1, 3)
    hidden, send_first, send_second, weigh_high, weigh_low = project_and_dispatch(
        attn_parts,
        output_weight,
        own_rows,
        moe_gain,
        router_hosted.reshape(EXPERTS, model_width),
        expert_ids.T,
    )
    down_shard, output_plane = barrier((down_proj[0].astype(jnp.bfloat16), output_plane))
    down_planes = lax.all_gather(down_shard, "ep", axis_index_groups=Z_GROUPS)

    def experts(rows):
        rows = rows.reshape(EXPERTS * HALF, model_width)
        gate_up = jnp.dot(rows, gate_up_full, preferred_element_type=jnp.float32)
        activated = (jax.nn.silu(gate_up[..., :FF]) * gate_up[..., FF:]).astype(jnp.bfloat16)
        return (
            jnp.dot(activated, down_full, preferred_element_type=jnp.float32)
            .astype(jnp.bfloat16)
            .reshape(EXPERTS, HALF, model_width)
        )

    def mix(returned, half):
        at = slice(half * EXPERTS * HALF, (half + 1) * EXPERTS * HALF)
        rows = returned.reshape(EXPERTS * HALF, model_width)
        return lax.dot_general(
            jnp.concatenate([weigh_high[at], weigh_low[at]], axis=0),
            jnp.concatenate([rows, rows], axis=0),
            (((0,), (0,)), ((), ())),
            preferred_element_type=jnp.float32,
        )

    received_first = in_plane(send_first.reshape(EXPERTS, HALF, model_width))
    down_planes, received_first = barrier((down_planes, received_first))
    down_full = lax.all_to_all(down_planes, "tp", 0, 0, tiled=True).reshape(-1, model_width)
    send_second, down_full = barrier((send_second, down_full))
    received_second = in_plane(send_second.reshape(EXPERTS, HALF, model_width))
    out_first, received_second = barrier((experts(received_first), received_second))
    returned_first = in_plane(out_first)
    out_second, returned_first = barrier((experts(received_second), returned_first))
    returned_second = in_plane(out_second)
    mixed = hidden + mix(returned_first, 0) + mix(returned_second, 1)
    valid = tp_index * row_count + jnp.arange(row_count) < lengths[0]
    return jnp.where(valid[:, None], mixed, 0.0).astype(jnp.bfloat16)


def solution(mesh):
    in_specs = (
        P("ep", None),
        P("ep"),
        P(),
        P("ep", "tp"),
        P("ep", "tp"),
        P("ep", "tp"),
        P("tp", "ep"),
        P("ep", None, "tp"),
        P(None, "ep", None),
        P(),
        P(),
        P(("ep", "tp"), None),
        P("ep", "tp", None),
        P("ep", "tp", None),
    )
    out_specs = P(("ep", "tp"), None)
    return jax.shard_map(
        on_device, mesh=mesh, in_specs=in_specs, out_specs=out_specs, check_vma=False
    )
```

time: 382 us -> 358 us (0.937)
  blocking collectives: 19.9 us -> 81.4 us
  waiting for transfers between devices: 201 us -> 161 us
  matrix products: 58.7 us -> 23.3 us
  Pallas kernels: 4.76 us -> 22.8 us
  starting transfers between devices: 47.8 us -> 34.9 us
  local copies, waits for them, and re-layouts: 21.9 us -> 11.8 us
  other arithmetic: 13 us -> 6.77 us
    all_to_all x1 -> x3, blocking collectives: 19.9 us -> 81.4 us  [the longest x1 32.3 us: on_device(): lax.all_to_all(payload, 'ep', 0, 0, axis_index_groups=Z_GROUPS, tiled=True)]
    all_gather x1, waiting for transfers between devices: 34.2 us -> 0.02 us  [on_device(): down_planes = lax.all_gather(down_shard, 'ep', axis_index_groups=Z_GROUPS)]
    dot_general x8 -> x6, matrix products: 41.2 us -> 23.3 us  [the longest x2 10.4 us: experts(): gate_up = jnp.dot(rows, gate_up_full, preferred_element_type=jnp.float32)]
    sub x2 -> x0, matrix products: 17.4 us -> none  [on_device(): weights = jnp.exp(scores - top_score)]
    pallas_call x0 -> x1, Pallas kernels: none -> 16.7 us  [attention(): pl.pallas_call(attention_body, out_shape=jax.ShapeDtypeStruct((blocks, se...]
    all_to_all x7 -> x6, starting transfers between devices: 43.7 us -> 30.4 us  [the longest x4 21.8 us: in_plane(): lax.all_to_all(rows, ('ep', 'tp'), 0, 0, axis_index_groups=PLANE_GROUPS,...]
    all_to_all x7 -> x6, waiting for transfers between devices: 146 us -> 135 us  [the longest x4 114 us: in_plane(): lax.all_to_all(rows, ('ep', 'tp'), 0, 0, axis_index_groups=PLANE_GROUPS,...]
    all_to_all x1, waiting for transfers between devices: 20.7 us -> 26.3 us  [on_device(): lax.all_to_all(gate_up_planes, 'tp', 0, 0, tiled=True)]
  transfers between devices with their start and end apart: 11 -> 10, of which waited for: 9 -> 7; matrix products, arithmetic and copies ran while one was open for 19% -> 9% of each run, Pallas kernels for 0% -> 6%
where the time goes in v3:
time: 358 us; the launch traced here: 357 us
  waiting for transfers between devices  161 us (45%)
  blocking collectives  81.4 us (23%)
  starting transfers between devices  34.9 us (10%)
  matrix products  23.3 us (7%)
  Pallas kernels  22.8 us (6%)
  between operations  14.2 us (4%)
  local copies, waits for them, and re-layouts  11.8 us (3%)
  other arithmetic  6.77 us (2%)
    all_to_all x4, waiting for transfers between devices, in_plane(): lax.all_to_all(rows, ('ep', 'tp'), 0, 0, axis_index_groups=PLANE_GROUPS,...  114 us
    all_to_all x1, blocking collectives, on_device(): lax.all_to_all(payload, 'ep', 0, 0, axis_index_groups=Z_GROUPS, tiled=True)  32.3 us
    all_to_all x1, waiting for transfers between devices, on_device(): lax.all_to_all(gate_up_planes, 'tp', 0, 0, tiled=True)  26.3 us
    all_to_all x1, blocking collectives, on_device(): lax.all_to_all(down_planes, 'tp', 0, 0, tiled=True).reshape(-1, model_width)  25.9 us
    all_to_all x1, blocking collectives, in_plane(): lax.all_to_all(rows, ('ep', 'tp'), 0, 0, axis_index_groups=PLANE_GROUPS,...  23.2 us
    all_to_all x4, starting transfers between devices, in_plane(): lax.all_to_all(rows, ('ep', 'tp'), 0, 0, axis_index_groups=PLANE_GROUPS,...  21.8 us
    pallas_call x1, Pallas kernels, attention(): pl.pallas_call(attention_body, out_shape=jax.ShapeDtypeStruct((blocks, se...  16.7 us
    all_to_all x1, waiting for transfers between devices, on_device(): lax.all_to_all(payload, 'ep', 0, 0, axis_index_groups=CHIP_PAIR_GROUPS, t...  14.6 us
  transfers between devices with their start and end apart: 10, of which 7 were waited for; matrix products, arithmetic and copies ran while one was open for 9% of the time, Pallas kernels for 6%

profile of v3, /device:TPU:1, one launch (start us, length us, event | category | flops | bytes accessed | tf_op | source)
XLA Modules:
  0.0 356.7 jit_solution(12383408742974394930)
XLA Ops:
  6.5 0.0 copy-start
  6.5 1.9 convert_element_type.55
  8.5 0.0 all-gather.5.cloned.1.call-update
  8.5 0.0 all-gather.7.cloned.1.call-start
  8.6 0.8 convert_bitcast_fusion.1
  9.4 0.1 broadcast_in_dim.54
  9.4 0.0 copy-start.12
  9.4 23.2 %all_to_all.50 = bf16[32,48,192]{2,1,0:T(8,128)(2,1)S(1)} all-to-all(bf16[32,48,192]{2,1,0:T(8,128)(2,1)S(1)} %broadcast_in_dim.54), channel_id=1, replica_groups={{0,1,2,3,4,5,6,7,8,9,10,11,12,13,14,15,128,129,130,131,132,133,134,135,..., dimensions={0} | all-to-all | bytes 1179648 | tf_op jit(solution)/shard_map/all_to_all | solution.py:268
  32.6 0.3 copy.38
  32.9 1.5 all_gather_reshape.3
  34.4 0.0 all-gather.7.cloned.1.call-update
  34.4 0.1 copy.32
  34.5 0.1 reshape.163
  34.7 0.6 gather_fusion
  35.4 0.0 copy-done.9
  35.4 0.1 pad.15.clone
  35.5 0.1 maximum_maximum_fusion
  35.7 32.3 %all_to_all.51 = bf16[8,272,128]{2,1,0:T(8,128)(2,1)S(1)} all-to-all(bf16[8,272,128]{2,1,0:T(8,128)(2,1)S(1)} %pad_maximum_fusion.1), channel_id=1, replica_groups={{0,16,32,48,64,80,96,112},{8,24,40,56,72,88,104,120},{128,144,160,176,1..., dimensions={0} | all-to-all | bytes 1114112 | tf_op jit(solution)/shard_map/all_to_all | solution.py:295
  68.1 0.2 broadcast_in_dim.51
  68.3 0.0 copy-start.5
  68.3 1.3 pad_maximum_fusion
  69.5 4.6 %all-to-all-start.1 = ((bf16[4,8,176,128]{3,2,1,0:T(8,128)(2,1)}), bf16[4,8,176,128]{3,2,1,0:T(8,128)(2,1)S(1)}, u32[]{:S(2)}, u32[]{:S(2)}) async-start(bf16[4,8,176,128]{3,2,1,0:T(8,128)(2,1)} %pad_maximum_fusion), calls=%async_computation.1 | async-start | bytes 2883584 | tf_op jit(solution)/shard_map/all_to_all | solution.py:303
  74.2 0.0 all-gather.9.cloned.1.call-start
  74.2 0.7 convert_bitcast_fusion
  74.9 0.0 all-gather.9.cloned.1.call-update
  75.6 1.9 fusion.26
  77.5 14.6 %all-to-all-done.1 = bf16[4,8,176,128]{3,2,1,0:T(8,128)(2,1)S(1)} async-done(((bf16[4,8,176,128]{3,2,1,0:T(8,128)(2,1)}), bf16[4,8,176,128]{3,2,1,0:T(8,128)(2,1)S(1)}, u32[]{:S(2)}, u32[]{:S(2)}) %all-to-all-start.1) | async-done | bytes 1441824 | tf_op jit(solution)/shard_map/all_to_all | solution.py:303
  92.1 0.1 slice.52
  92.2 0.8 copy.35
  92.9 0.3 copy-done.4
  93.2 0.2 copy.45
  93.4 0.7 slice-done
  94.2 0.0 all-gather.5.cloned.1.call-done
  94.2 4.5 %all-to-all-start.2 = ((bf16[8,192,1024]{2,1,0:T(8,128)(2,1)}), bf16[8,192,1024]{2,1,0:T(8,128)(2,1)}, u32[]{:S(2)}, u32[]{:S(2)}) async-start(bf16[8,192,1024]{2,1,0:T(8,128)(2,1)} %all-gather.5.cloned.1.call-done), calls=%async_computation.2 | async-start | bytes 6291456 | tf_op jit(solution)/shard_map/all_to_all | solution.py:313
  98.7 0.0 copy-start.2
  98.8 1.9 copy-done.2
  100.7 16.7 %attention.1 = bf16[8,128,192]{2,1,0:T(8,128)(2,1)S(1)} custom-call(s32[1]{0:T(128)} %copy.46.length_ref, bf16[1024,1536]{1,0:T(8,128)(2,1)S(1)} %copy-done.2, f32[1,1536]{1,0:T(1,128)S(1)} %reshape.138.gain_ref, bf16[1536,384]{1,0:T(8,128)(2,1)S(1)} %bitcast.60, bf16[1024,128]{1,0:T(8,128)(2,1)S(1)} %bitcast.62, ...), custom_call_target="tpu_custom_call" | custom-call | flops 30000001024 | bytes 8388608 | tf_op jit(solution)/shard_map/attention/pallas_call | solution.py:121
  117.4 0.0 copy-start.3
  117.4 26.3 %all-to-all-done.2 = bf16[8,192,1024]{2,1,0:T(8,128)(2,1)} async-done(((bf16[8,192,1024]{2,1,0:T(8,128)(2,1)}), bf16[8,192,1024]{2,1,0:T(8,128)(2,1)}, u32[]{:S(2)}, u32[]{:S(2)}) %all-to-all-start.2) | async-done | bytes 3145760 | tf_op jit(solution)/shard_map/all_to_all | solution.py:313
  143.7 1.0 copy.37
  144.6 3.9 %all-to-all-start.3 = ((bf16[8,128,192]{1,2,0:T(8,128)(2,1)}), bf16[8,128,192]{1,2,0:T(8,128)(2,1)S(1)}, u32[]{:S(2)}, u32[]{:S(2)}) async-start(bf16[8,128,192]{1,2,0:T(8,128)(2,1)} %copy.37), calls=%async_computation.3 | async-start | bytes 786432 | tf_op jit(solution)/shard_map/all_to_all | solution.py:316
  148.6 0.0 copy-done.6
  148.7 1.0 constant_dynamic-slice_fusion.rows_ref
  149.7 6.7 %all-to-all-done.3 = bf16[8,128,192]{1,2,0:T(8,128)(2,1)S(1)} async-done(((bf16[8,128,192]{1,2,0:T(8,128)(2,1)}), bf16[8,128,192]{1,2,0:T(8,128)(2,1)S(1)}, u32[]{:S(2)}, u32[]{:S(2)}) %all-to-all-start.3) | async-done | bytes 393248 | tf_op jit(solution)/shard_map/all_to_all | solution.py:316
  156.4 0.2 copy.40.parts_ref
  156.6 0.0 all-gather.7.cloned.1.call-done
  156.6 2.3 copy-done.1
  159.0 6.1 %project_and_dispatch.1 = (f32[128,1536]{1,0:T(8,128)S(1)}, bf16[768,1536]{1,0:T(8,128)(2,1)}, bf16[768,1536]{1,0:T(8,128)(2,1)}, bf16[1536,128]{1,0:T(8,128)(2,1)S(1)}, bf16[1536,128]{1,0:T(8,128)(2,1)S(1)}) custom-call(bf16[8,128,192]{2,1,0:T(8,128)(2,1)S(1)} %copy.40.parts_ref, bf16[8,2,96,1536]{3,2,1,0:T(8,128)(2,1)S(1)} %bitcast.59, ...), custom_call_target="tpu_custom_call" | custom-call | flops 1207959552 | bytes 9437184 | tf_op jit(solution)/shard_map/project_and_dispatch/pallas_call | solution.py:212
  165.1 7.5 %all-to-all-start.5 = ((bf16[32,24,1536]{2,1,0:T(8,128)(2,1)}), bf16[32,24,1536]{2,1,0:T(8,128)(2,1)}, u32[]{:S(2)}, u32[]{:S(2)}) async-start(bf16[32,24,1536]{2,1,0:T(8,128)(2,1)} %bitcast.25), calls=%async_computation.5 | async-start | bytes 4718592 | tf_op jit(solution)/shard_map/all_to_all | solution.py:268
  172.7 0.0 all-gather.9.cloned.1.call-done
  172.7 33.5 %all-to-all-done.5 = bf16[32,24,1536]{2,1,0:T(8,128)(2,1)} async-done(((bf16[32,24,1536]{2,1,0:T(8,128)(2,1)}), bf16[32,24,1536]{2,1,0:T(8,128)(2,1)}, u32[]{:S(2)}, u32[]{:S(2)}) %all-to-all-start.5) | async-done | bytes 2359328 | tf_op jit(solution)/shard_map/all_to_all | solution.py:268
  206.2 25.9 %all_to_all.52 = bf16[8,64,1536]{2,1,0:T(8,128)(2,1)S(1)} all-to-all(bf16[8,64,1536]{2,1,0:T(8,128)(2,1)} %bitcast.70), channel_id=1, replica_groups=mesh['ep'=32,'tp'=8] {'tp'}, dimensions={0} | all-to-all | bytes 3145728 | tf_op jit(solution)/shard_map/all_to_all | solution.py:352
  232.1 5.1 %all-to-all-start.7 = ((bf16[32,24,1536]{2,1,0:T(8,128)(2,1)}), bf16[32,24,1536]{2,1,0:T(8,128)(2,1)}, u32[]{:S(2)}, u32[]{:S(2)}) async-start(bf16[32,24,1536]{2,1,0:T(8,128)(2,1)} %bitcast.29), calls=%async_computation.7 | async-start | bytes 4718592 | tf_op jit(solution)/shard_map/all_to_all | solution.py:268
  237.2 5.2 %fusion.42 = f32[768,1024]{1,0:T(8,128)S(1)} fusion(bf16[768,1536]{1,0:T(8,128)(2,1)} %bitcast.26, bf16[1536,1024]{1,0:T(8,128)(2,1)} %bitcast.14), kind=kOutput, calls=%fused_computation.53 | convolution fusion | flops 2415919104 | bytes 8650752 | tf_op jit(solution)/shard_map/dot_general | solution.py:332
  242.4 2.9 convolution_convert_fusion.1
  245.3 25.4 %all-to-all-done.7 = bf16[32,24,1536]{2,1,0:T(8,128)(2,1)} async-done(((bf16[32,24,1536]{2,1,0:T(8,128)(2,1)}), bf16[32,24,1536]{2,1,0:T(8,128)(2,1)}, u32[]{:S(2)}, u32[]{:S(2)}) %all-to-all-start.7) | async-done | bytes 2359328 | tf_op jit(solution)/shard_map/all_to_all | solution.py:268
  270.7 4.6 %all-to-all-start.8 = ((bf16[32,24,1536]{2,1,0:T(8,128)(2,1)}), bf16[32,24,1536]{2,1,0:T(8,128)(2,1)}, u32[]{:S(2)}, u32[]{:S(2)}) async-start(bf16[32,24,1536]{2,1,0:T(8,128)(2,1)} %bitcast.69), calls=%async_computation.8 | async-start | bytes 4718592 | tf_op jit(solution)/shard_map/all_to_all | solution.py:268
  275.3 5.2 %fusion.43 = f32[768,1024]{1,0:T(8,128)S(1)} fusion(bf16[768,1536]{1,0:T(8,128)(2,1)} %bitcast.30, bf16[1536,1024]{1,0:T(8,128)(2,1)} %bitcast.14), kind=kOutput, calls=%fused_computation.54 | convolution fusion | flops 2415919104 | bytes 8650752 | tf_op jit(solution)/shard_map/dot_general | solution.py:332
  280.5 2.9 convolution_convert_fusion
  283.4 25.1 %all-to-all-done.8 = bf16[32,24,1536]{2,1,0:T(8,128)(2,1)} async-done(((bf16[32,24,1536]{2,1,0:T(8,128)(2,1)}), bf16[32,24,1536]{2,1,0:T(8,128)(2,1)}, u32[]{:S(2)}, u32[]{:S(2)}) %all-to-all-start.8) | async-done | bytes 2359328 | tf_op jit(solution)/shard_map/all_to_all | solution.py:268
  308.5 4.6 %all-to-all-start.9 = ((bf16[32,24,1536]{2,1,0:T(8,128)(2,1)}), bf16[32,24,1536]{2,1,0:T(8,128)(2,1)}, u32[]{:S(2)}, u32[]{:S(2)}) async-start(bf16[32,24,1536]{2,1,0:T(8,128)(2,1)} %bitcast.68), calls=%async_computation.9 | async-start | bytes 4718592 | tf_op jit(solution)/shard_map/all_to_all | solution.py:268
  313.2 3.2 fusion.11
  316.4 29.8 %all-to-all-done.9 = bf16[32,24,1536]{2,1,0:T(8,128)(2,1)} async-done(((bf16[32,24,1536]{2,1,0:T(8,128)(2,1)}), bf16[32,24,1536]{2,1,0:T(8,128)(2,1)}, u32[]{:S(2)}, u32[]{:S(2)}) %all-to-all-start.9) | async-done | bytes 2359328 | tf_op jit(solution)/shard_map/all_to_all | solution.py:268
  346.2 3.9 %fusion.17 = bf16[128,1536]{1,0:T(8,128)(2,1)} fusion(f32[128,1536]{1,0:T(8,128)S(1)} %fusion.11, bf16[768,1536]{1,0:T(8,128)(2,1)} %bitcast.33, bf16[768,128]{1,0:T(8,128)(2,1)S(1)} %get-tuple-element.43, bf16[768,128]{1,0:T(8,128)(2,1)S(1)} %get-tuple-element.41, pred[128]{0:T(512)(128)(4,1)S(1)} %add_compare_fusion), kind=kOutput, calls=%fused_computation.14 | convolution fusion | flops 614793216 | bytes 3932288 | tf_op jit(solution)/shard_map/dot_general | solution.py:343
  (41 shorter events, 0.4 us)
Async XLA Ops:
  6.5 28.1 %copy-start = (bf16[8,16,128]{2,1,0:T(8,128)(2,1)S(1)}, bf16[8,16,128]{2,1,0:T(8,128)(2,1)}, u32[]{:S(2)}) copy-start(bf16[8,16,128]{2,1,0:T(8,128)(2,1)} %param.21) | copy-start | bytes 98308
  6.5 87.7 %all-gather.5.cloned.1.call-start = ((), (), s32[]{:S(2)}) async-start(), calls=%async_computation.10 | async-start | bytes 3538944 | tf_op jit(solution)/shard_map/all_gather | solution.py:272
  8.5 148.1 %all-gather.7.cloned.1.call-start = ((), (), s32[]{:S(2)}) async-start(), calls=%async_computation.11 | async-start | bytes 5308416 | tf_op jit(solution)/shard_map/all_gather | solution.py:280
  9.4 25.0 %copy-start.12 = (s32[32,1,2]{0,2,1:T(2,128)S(1)}, s32[32,1,2]{0,2,1:T(2,128)}, u32[]{:S(2)}) copy-start(s32[32,1,2]{0,2,1:T(2,128)} %param.22) | copy-start | bytes 772
  32.6 2.7 copy-start.7
  32.6 2.8 copy-start.8
  32.6 2.8 copy-start.9
  68.3 5.9 %copy-start.5 = (f32[1,64,1536]{2,1,0:T(8,128)S(1)}, f32[1,64,1536]{2,1,0:T(8,128)}, u32[]{:S(2)}) copy-start(f32[1,64,1536]{2,1,0:T(8,128)} %param.27) | copy-start | bytes 1179652
  69.5 6.0 %copy-start.10 = (f32[1536]{0:T(1024)S(1)}, f32[1536]{0:T(1024)}, u32[]{:S(2)}) copy-start(f32[1536]{0:T(1024)} %param.16) | copy-start | bytes 18436
  69.5 22.6 %all-to-all-start.1 = ((bf16[4,8,176,128]{3,2,1,0:T(8,128)(2,1)}), bf16[4,8,176,128]{3,2,1,0:T(8,128)(2,1)S(1)}, u32[]{:S(2)}, u32[]{:S(2)}) async-start(bf16[4,8,176,128]{3,2,1,0:T(8,128)(2,1)} %pad_maximum_fusion), calls=%async_computation.1 | async-start | bytes 2883584 | tf_op jit(solution)/shard_map/all_to_all | solution.py:303
  74.2 98.5 %all-gather.9.cloned.1.call-start = ((), (), s32[]{:S(2)}) async-start(), calls=%async_computation.12 | async-start | bytes 1769472 | tf_op jit(solution)/shard_map/all_gather | solution.py:328
  92.1 1.2 copy-start.4
  93.2 0.9 slice-start
  94.2 49.4 %all-to-all-start.2 = ((bf16[8,192,1024]{2,1,0:T(8,128)(2,1)}), bf16[8,192,1024]{2,1,0:T(8,128)(2,1)}, u32[]{:S(2)}, u32[]{:S(2)}) async-start(bf16[8,192,1024]{2,1,0:T(8,128)(2,1)} %all-gather.5.cloned.1.call-done), calls=%async_computation.2 | async-start | bytes 6291456 | tf_op jit(solution)/shard_map/all_to_all | solution.py:313
  98.7 1.9 copy-start.2
  100.7 47.9 %copy-start.6 = (bf16[1536,32]{0,1:T(8,128)(2,1)S(1)}, bf16[1536,32]{0,1:T(8,128)(2,1)}, u32[]{:S(2)}) copy-start(bf16[1536,32]{0,1:T(8,128)(2,1)} %param.24) | copy-start | bytes 294916
  100.7 48.0 %copy-start.11 = (f32[1536]{0:T(1024)S(1)}, f32[1536]{0:T(1024)}, u32[]{:S(2)}) copy-start(f32[1536]{0:T(1024)} %param.23) | copy-start | bytes 18436
  117.4 39.2 %copy-start.3 = (s32[128,8]{0,1:T(8,128)S(1)}, s32[128,8]{0,1:T(8,128)}, u32[]{:S(2)}) copy-start(s32[128,8]{0,1:T(8,128)} %param.25) | copy-start | bytes 12292
  144.6 11.8 %all-to-all-start.3 = ((bf16[8,128,192]{1,2,0:T(8,128)(2,1)}), bf16[8,128,192]{1,2,0:T(8,128)(2,1)S(1)}, u32[]{:S(2)}, u32[]{:S(2)}) async-start(bf16[8,128,192]{1,2,0:T(8,128)(2,1)} %copy.37), calls=%async_computation.3 | async-start | bytes 786432 | tf_op jit(solution)/shard_map/all_to_all | solution.py:316
  156.6 2.4 copy-start.1
  165.1 41.1 %all-to-all-start.5 = ((bf16[32,24,1536]{2,1,0:T(8,128)(2,1)}), bf16[32,24,1536]{2,1,0:T(8,128)(2,1)}, u32[]{:S(2)}, u32[]{:S(2)}) async-start(bf16[32,24,1536]{2,1,0:T(8,128)(2,1)} %bitcast.25), calls=%async_computation.5 | async-start | bytes 4718592 | tf_op jit(solution)/shard_map/all_to_all | solution.py:268
  232.1 38.6 %all-to-all-start.7 = ((bf16[32,24,1536]{2,1,0:T(8,128)(2,1)}), bf16[32,24,1536]{2,1,0:T(8,128)(2,1)}, u32[]{:S(2)}, u32[]{:S(2)}) async-start(bf16[32,24,1536]{2,1,0:T(8,128)(2,1)} %bitcast.29), calls=%async_computation.7 | async-start | bytes 4718592 | tf_op jit(solution)/shard_map/all_to_all | solution.py:268
  270.7 37.7 %all-to-all-start.8 = ((bf16[32,24,1536]{2,1,0:T(8,128)(2,1)}), bf16[32,24,1536]{2,1,0:T(8,128)(2,1)}, u32[]{:S(2)}, u32[]{:S(2)}) async-start(bf16[32,24,1536]{2,1,0:T(8,128)(2,1)} %bitcast.69), calls=%async_computation.8 | async-start | bytes 4718592 | tf_op jit(solution)/shard_map/all_to_all | solution.py:268
  308.5 37.7 %all-to-all-start.9 = ((bf16[32,24,1536]{2,1,0:T(8,128)(2,1)}), bf16[32,24,1536]{2,1,0:T(8,128)(2,1)}, u32[]{:S(2)}, u32[]{:S(2)}) async-start(bf16[32,24,1536]{2,1,0:T(8,128)(2,1)} %bitcast.68), calls=%async_computation.9 | async-start | bytes 4718592 | tf_op jit(solution)/shard_map/all_to_all | solution.py:268
Sparse Core Ops, SparseCore 0:
  9.1 60.4 all-gather.4
  71.5 58.5 all-gather.6
  131.9 34.7 all-gather.8

commit v4 on v3

--- a/solution.py
+++ b/solution.py
@@ -10,7 +10,6 @@
 HEAD_WIDTH = 64
 FF = 512
 CAPACITY = 48
-HALF = CAPACITY // 2
 EXPERTS = 32
 
 
@@ -138,7 +137,7 @@
 
 def project_body(
     parts_ref, weight_hbm, rows_ref, gain_ref, router_ref, ids_ref,
-    hidden_ref, first_ref, second_ref, high_ref, low_ref,
+    hidden_ref, send_ref, rank_ref, gates_ref,
     weight, attended, place, sem,
 ):
     copies = []
@@ -166,13 +165,12 @@
         preferred_element_type=jnp.float32,
     )
     rank = jnp.where(chosen > 0.0, rank, -1.0)
-    slot = lax.broadcasted_iota(jnp.int32, (HALF, tokens), 0).astype(jnp.float32)
-    for half in range(2):
-        for g in range(EXPERTS):
-            at = (half * EXPERTS + g) * HALF
-            place[at : at + HALF, :] = jnp.where(
-                rank[g : g + 1, :] == slot + float(half * HALF), 1.0, 0.0
-            ).astype(jnp.bfloat16)
+    rank_ref[...] = rank
+    slot = lax.broadcasted_iota(jnp.int32, (CAPACITY, tokens), 0).astype(jnp.float32)
+    for g in range(EXPERTS):
+        place[g * CAPACITY : (g + 1) * CAPACITY, :] = jnp.where(
+            rank[g : g + 1, :] == slot, 1.0, 0.0
+        ).astype(jnp.bfloat16)
     for copy in copies:
         copy.wait()
     for c in range(0, 1536, 256):
@@ -184,25 +182,16 @@
         )
     hidden = hidden_ref[...]
     moe_in = rms_scale(hidden, gain_ref[...]).astype(jnp.bfloat16)
-    for half, send_ref in enumerate((first_ref, second_ref)):
-        for c in range(0, EXPERTS * HALF, 256):
-            at = half * EXPERTS * HALF + c
-            send_ref[c : c + 256, :] = jnp.dot(
-                place[at : at + 256, :], moe_in, preferred_element_type=jnp.float32
-            ).astype(jnp.bfloat16)
+    for c in range(0, EXPERTS * CAPACITY, 256):
+        send_ref[c : c + 256, :] = jnp.dot(
+            place[c : c + 256, :], moe_in, preferred_element_type=jnp.float32
+        ).astype(jnp.bfloat16)
     logits = lax.dot_general(
         router_ref[...], moe_in, (((1,), (1,)), ((), ())), preferred_element_type=jnp.float32
     )
     top_logit = jnp.max(jnp.where(chosen > 0.0, logits, -3e38), axis=0, keepdims=True)
     raised = jnp.where(chosen > 0.0, jnp.exp(jnp.minimum(logits - top_logit, 0.0)), 0.0)
-    gates = raised / jnp.sum(raised, axis=0, keepdims=True)
-    for half in range(2):
-        for g in range(EXPERTS):
-            at = (half * EXPERTS + g) * HALF
-            weigh = place[at : at + HALF, :].astype(jnp.float32) * gates[g : g + 1, :]
-            high = weigh.astype(jnp.bfloat16)
-            high_ref[at : at + HALF, :] = high
-            low_ref[at : at + HALF, :] = (weigh - high.astype(jnp.float32)).astype(jnp.bfloat16)
+    gates_ref[...] = raised / jnp.sum(raised, axis=0, keepdims=True)
 
 
 def project_and_dispatch(parts, output_weight, own_rows, moe_gain, router_hosted, ids_by_choice):
@@ -213,13 +202,12 @@
         project_body,
         out_shape=(
             jax.ShapeDtypeStruct((row_count, model_width), jnp.float32),
-            jax.ShapeDtypeStruct((slots // 2, model_width), jnp.bfloat16),
-            jax.ShapeDtypeStruct((slots // 2, model_width), jnp.bfloat16),
-            jax.ShapeDtypeStruct((slots, row_count), jnp.bfloat16),
-            jax.ShapeDtypeStruct((slots, row_count), jnp.bfloat16),
+            jax.ShapeDtypeStruct((slots, model_width), jnp.bfloat16),
+            jax.ShapeDtypeStruct((EXPERTS, row_count), jnp.float32),
+            jax.ShapeDtypeStruct((EXPERTS, row_count), jnp.float32),
         ),
         in_specs=[vmem, pl.BlockSpec(memory_space=pltpu.HBM), vmem, vmem, vmem, vmem],
-        out_specs=(vmem, vmem, vmem, vmem, vmem),
+        out_specs=(vmem, vmem, vmem, vmem),
         scratch_shapes=[
             pltpu.VMEM((model_width, model_width), jnp.bfloat16),
             pltpu.VMEM((row_count, model_width), jnp.bfloat16),
@@ -241,6 +229,102 @@
         router_hosted,
         ids_by_choice,
     )
+
+
+def weigh_body(rank_ref, gates_ref, high_ref, low_ref, weigh):
+    tokens = rank_ref.shape[1]
+    slot = lax.broadcasted_iota(jnp.int32, (CAPACITY, tokens), 0).astype(jnp.float32)
+    for g in range(EXPERTS):
+        weigh[g * CAPACITY : (g + 1) * CAPACITY, :] = jnp.where(
+            rank_ref[g : g + 1, :] == slot, gates_ref[g : g + 1, :], 0.0
+        )
+    for c in range(0, EXPERTS * CAPACITY, 128):
+        by_token = weigh[c : c + 128, :].T
+        high = by_token.astype(jnp.bfloat16)
+        high_ref[:, c : c + 128] = high
+        low_ref[:, c : c + 128] = (by_token - high.astype(jnp.float32)).astype(jnp.bfloat16)
+
+
+def weighing(rank, gates):
+    row_count = rank.shape[1]
+    slots = EXPERTS * CAPACITY
+    vmem = pl.BlockSpec(memory_space=pltpu.VMEM)
+    shape = jax.ShapeDtypeStruct((row_count, slots), jnp.bfloat16)
+    return pl.pallas_call(
+        weigh_body,
+        out_shape=(shape, shape),
+        in_specs=[vmem, vmem],
+        out_specs=(vmem, vmem),
+        scratch_shapes=[pltpu.VMEM((slots, row_count), jnp.float32)],
+        cost_estimate=pl.CostEstimate(flops=1 << 20, bytes_accessed=1 << 20, transcendentals=0),
+        name="weighing",
+    )(rank, gates)
+
+
+def expert_body(rows_ref, gate_up_ref, down_ref, out_ref):
+    gate_up = jnp.dot(rows_ref[...], gate_up_ref[...], preferred_element_type=jnp.float32)
+    activated = (jax.nn.silu(gate_up[:, :FF]) * gate_up[:, FF:]).astype(jnp.bfloat16)
+    out_ref[...] = jnp.dot(activated, down_ref[...], preferred_element_type=jnp.float32).astype(
+        jnp.bfloat16
+    )
+
+
+def experts(rows, gate_up, down):
+    count, model_width = rows.shape
+    tile = 256
+    return pl.pallas_call(
+        expert_body,
+        out_shape=jax.ShapeDtypeStruct((count, model_width), jnp.bfloat16),
+        grid=(count // tile,),
+        in_specs=[
+            pl.BlockSpec((tile, model_width), lambda i: (i, 0)),
+            pl.BlockSpec(gate_up.shape, lambda i: (0, 0)),
+            pl.BlockSpec(down.shape, lambda i: (0, 0)),
+        ],
+        out_specs=pl.BlockSpec((tile, model_width), lambda i: (i, 0)),
+        compiler_params=pltpu.CompilerParams(vmem_limit_bytes=40 << 20),
+        cost_estimate=pl.CostEstimate(
+            flops=2 * count * model_width * 3 * FF,
+            bytes_accessed=4 * count * model_width + 6 * model_width * FF,
+            transcendentals=count * FF,
+        ),
+        name="experts",
+    )(rows, gate_up, down)
+
+
+def combine_body(live_ref, high_ref, low_ref, returned_ref, hidden_ref, out_ref):
+    mixed = jnp.dot(high_ref[...], returned_ref[...], preferred_element_type=jnp.float32) + jnp.dot(
+        low_ref[...], returned_ref[...], preferred_element_type=jnp.float32
+    )
+    row = lax.broadcasted_iota(jnp.int32, mixed.shape, 0)
+    out_ref[...] = jnp.where(row < live_ref[0], hidden_ref[...] + mixed, 0.0).astype(jnp.bfloat16)
+
+
+def combine(live, high, low, returned, hidden):
+    row_count, model_width = hidden.shape
+    slots = returned.shape[0]
+    tile = 256
+    whole = pl.BlockSpec((row_count, slots), lambda i: (0, 0))
+    column = pl.BlockSpec((row_count, tile), lambda i: (0, i))
+    return pl.pallas_call(
+        combine_body,
+        out_shape=jax.ShapeDtypeStruct((row_count, model_width), jnp.bfloat16),
+        grid=(model_width // tile,),
+        in_specs=[
+            pl.BlockSpec(memory_space=pltpu.SMEM),
+            whole,
+            whole,
+            pl.BlockSpec((slots, tile), lambda i: (0, i)),
+            column,
+        ],
+        out_specs=column,
+        cost_estimate=pl.CostEstimate(
+            flops=4 * row_count * slots * model_width,
+            bytes_accessed=2 * slots * model_width + 6 * row_count * model_width,
+            transcendentals=0,
+        ),
+        name="combine",
+    )(live, high, low, returned, hidden)
 
 
 def on_device(
@@ -269,15 +353,11 @@
             rows, ("ep", "tp"), 0, 0, axis_index_groups=PLANE_GROUPS, tiled=True
         )
 
-    gate_up_planes = lax.all_gather(
-        gate_up_proj[0].astype(jnp.bfloat16), "ep", axis_index_groups=Z_GROUPS
-    )
     output_shard = o_proj.T.astype(jnp.bfloat16)
     output_plane = in_plane(jnp.broadcast_to(output_shard[None], (EXPERTS, *output_shard.shape)))
     output_plane = (
         output_plane.reshape(4, 8, 48, 192).transpose(0, 2, 1, 3).reshape(192, model_width)
     )
-    output_weight = lax.all_gather(output_plane, "ep", axis_index_groups=Z_GROUPS)
 
     weight_shard = jnp.concatenate(
         [q_proj, k_proj, value_projection, jnp.zeros_like(k_proj)], axis=1
@@ -293,6 +373,8 @@
     )
     payload, output_plane = barrier((payload, output_plane))
     along_z = lax.all_to_all(payload, "ep", 0, 0, axis_index_groups=Z_GROUPS, tiled=True)
+    output_plane, along_z = barrier((output_plane, along_z))
+    output_weight = lax.all_gather(output_plane, "ep", axis_index_groups=Z_GROUPS)
     payload = jnp.concatenate(
         [
             jnp.broadcast_to(along_z[None, :, :144], (4, 8, 144, 128)),
@@ -309,14 +391,23 @@
     )
     prefix = across[:, :, 144:].reshape(2, 2, 8, 32, 128).transpose(0, 2, 1, 3, 4).reshape(-1, 128)
     cosine, sine = rotary_tables(seq_len, prefix.shape[0])
-    weight, prefix, gate_up_planes = barrier((weight, prefix, gate_up_planes))
-    gate_up_full = lax.all_to_all(gate_up_planes, "tp", 0, 0, tiled=True).reshape(model_width, -1)
+    eighths = jnp.concatenate(
+        [
+            gate_up_proj.astype(jnp.bfloat16).reshape(8, 24, 2, 512).transpose(0, 2, 1, 3).reshape(8, 48, 512),
+            down_proj.astype(jnp.bfloat16).reshape(8, 8, 3, 512).transpose(0, 2, 1, 3).reshape(8, 24, 512),
+        ],
+        axis=1,
+    )
+    eighths, weight, prefix = barrier((eighths, weight, prefix))
+    by_expert = lax.all_to_all(eighths, "ep", 0, 0, axis_index_groups=Z_GROUPS, tiled=True)
     attended = attention(lengths, tokens_in, attn_gain, weight, prefix, cosine, sine, 8)
-    attended, gate_up_full = barrier((attended, gate_up_full))
+    attended, by_expert = barrier((attended, by_expert))
     attn_parts = lax.all_to_all(attended, "tp", 0, 0, tiled=True)
+    attn_parts, by_expert = barrier((attn_parts, by_expert))
+    hosted = lax.all_to_all(by_expert, "tp", 0, 0, tiled=True)
     own_rows = lax.dynamic_slice_in_dim(tokens_in, tp_index * row_count, row_count, 0)
     router_hosted = router.T.reshape(2, 8, 2, model_width).transpose(0, 2, 1, 3)
-    hidden, send_first, send_second, weigh_high, weigh_low = project_and_dispatch(
+    hidden, send_rows, rank, gates = project_and_dispatch(
         attn_parts,
         output_weight,
         own_rows,
@@ -324,41 +415,20 @@
         router_hosted.reshape(EXPERTS, model_width),
         expert_ids.T,
     )
-    down_shard, output_plane = barrier((down_proj[0].astype(jnp.bfloat16), output_plane))
-    down_planes = lax.all_gather(down_shard, "ep", axis_index_groups=Z_GROUPS)
-
-    def experts(rows):
-        rows = rows.reshape(EXPERTS * HALF, model_width)
-        gate_up = jnp.dot(rows, gate_up_full, preferred_element_type=jnp.float32)
-        activated = (jax.nn.silu(gate_up[..., :FF]) * gate_up[..., FF:]).astype(jnp.bfloat16)
-        return (
-            jnp.dot(activated, down_full, preferred_element_type=jnp.float32)
-            .astype(jnp.bfloat16)
-            .reshape(EXPERTS, HALF, model_width)
-        )
-
-    def mix(returned, half):
-        at = slice(half * EXPERTS * HALF, (half + 1) * EXPERTS * HALF)
-        rows = returned.reshape(EXPERTS * HALF, model_width)
-        return lax.dot_general(
-            jnp.concatenate([weigh_high[at], weigh_low[at]], axis=0),
-            jnp.concatenate([rows, rows], axis=0),
-            (((0,), (0,)), ((), ())),
-            preferred_element_type=jnp.float32,
-        )
-
-    received_first = in_plane(send_first.reshape(EXPERTS, HALF, model_width))
-    down_planes, received_first = barrier((down_planes, received_first))
-    down_full = lax.all_to_all(down_planes, "tp", 0, 0, tiled=True).reshape(-1, model_width)
-    send_second, down_full = barrier((send_second, down_full))
-    received_second = in_plane(send_second.reshape(EXPERTS, HALF, model_width))
-    out_first, received_second = barrier((experts(received_first), received_second))
-    returned_first = in_plane(out_first)
-    out_second, returned_first = barrier((experts(received_second), returned_first))
-    returned_second = in_plane(out_second)
-    mixed = hidden + mix(returned_first, 0) + mix(returned_second, 1)
-    valid = tp_index * row_count + jnp.arange(row_count) < lengths[0]
-    return jnp.where(valid[:, None], mixed, 0.0).astype(jnp.bfloat16)
+    send_rows, hosted = barrier((send_rows, hosted))
+    planes = lax.all_gather(hosted, "ep", axis_index_groups=Z_GROUPS)
+    gate_up_full = (
+        planes[:, :, :48].reshape(8, 8, 2, 24, 512).transpose(1, 0, 3, 2, 4).reshape(model_width, 2 * FF)
+    )
+    down_full = (
+        planes[:, :, 48:].reshape(8, 8, 3, 8, 512).transpose(1, 0, 3, 2, 4).reshape(FF, model_width)
+    )
+    received = in_plane(send_rows.reshape(EXPERTS, CAPACITY, model_width))
+    high, low = weighing(rank, gates)
+    expert_out = experts(received.reshape(-1, model_width), gate_up_full, down_full)
+    returned = in_plane(expert_out.reshape(EXPERTS, CAPACITY, model_width))
+    live = lengths - tp_index * row_count
+    return combine(live, high, low, returned.reshape(-1, model_width), hidden)
 
 
 def solution(mesh):

time: 358 us -> 308 us (0.86)
  blocking collectives: 81.4 us -> 37.1 us
  matrix products: 23.3 us -> 0 us
  Pallas kernels: 22.8 us -> 39.4 us
  local copies, waits for them, and re-layouts: 11.8 us -> 27.8 us
  waiting for transfers between devices: 161 us -> 147 us
    all_gather x2 -> x1, waiting for transfers between devices: 0.04 us -> 48.7 us  [on_device(): planes = lax.all_gather(hosted, 'ep', axis_index_groups=Z_GROUPS)]
    all_to_all x2 -> x1, blocking collectives: 49.1 us -> 10.8 us  [on_device(): attn_parts = lax.all_to_all(attended, 'tp', 0, 0, tiled=True)]
    all_to_all x4 -> x3, waiting for transfers between devices: 114 us -> 77.5 us  [in_plane(): lax.all_to_all(rows, ('ep', 'tp'), 0, 0, axis_index_groups=PLANE_GROUPS,...]
    all_to_all x2, waiting for transfers between devices: 33 us -> 6.72 us  [the longest x1 6.72 us: on_device(): lax.all_to_all(eighths, 'ep', 0, 0, axis_index_groups=Z_GROUPS, tiled=True)]
    dot_general x6 -> x0, matrix products: 23.3 us -> none  [the longest x2 10.4 us: experts(): gate_up = jnp.dot(rows, gate_up_full, preferred_element_type=jnp.float32)]
    pallas_call x0 -> x3, Pallas kernels: none -> 18.3 us  [the longest x1 10 us: experts(): pl.pallas_call(expert_body, out_shape=jax.ShapeDtypeStruct((count, model_...]
    unnamed x27 -> x44, local copies, waits for them, and re-layouts: 4.8 us -> 12.7 us
    all_to_all x1, blocking collectives: 32.3 us -> 26.3 us  [on_device(): lax.all_to_all(payload, 'ep', 0, 0, axis_index_groups=Z_GROUPS, tiled=True)]
  transfers between devices with their start and end apart: 10 -> 8, of which waited for: 7 -> 6; matrix products, arithmetic and copies ran while one was open for 9% -> 6% of each run, Pallas kernels for 6% -> 8%
where the time goes in v4:
time: 308 us; the launch traced here: 307 us
  waiting for transfers between devices  147 us (48%)
  Pallas kernels  39.4 us (13%)
  blocking collectives  37.1 us (12%)
  starting transfers between devices  35.9 us (12%)
  local copies, waits for them, and re-layouts  27.8 us (9%)
  between operations  14.6 us (5%)
  other arithmetic  5.1 us (2%)
    all_to_all x3, waiting for transfers between devices, in_plane(): lax.all_to_all(rows, ('ep', 'tp'), 0, 0, axis_index_groups=PLANE_GROUPS,...  77.5 us
    all_gather x1, waiting for transfers between devices, on_device(): planes = lax.all_gather(hosted, 'ep', axis_index_groups=Z_GROUPS)  48.7 us
    all_to_all x1, blocking collectives, on_device(): lax.all_to_all(payload, 'ep', 0, 0, axis_index_groups=Z_GROUPS, tiled=True)  26.3 us
    all_to_all x3, starting transfers between devices, in_plane(): lax.all_to_all(rows, ('ep', 'tp'), 0, 0, axis_index_groups=PLANE_GROUPS,...  23.3 us
    pallas_call x1, Pallas kernels, attention(): pl.pallas_call(attention_body, out_shape=jax.ShapeDtypeStruct((blocks, se...  16.5 us
    all_to_all x1, waiting for transfers between devices, on_device(): lax.all_to_all(payload, 'ep', 0, 0, axis_index_groups=CHIP_PAIR_GROUPS, t...  14 us
    unnamed x44, local copies, waits for them, and re-layouts  12.7 us
    all_to_all x1, blocking collectives, on_device(): attn_parts = lax.all_to_all(attended, 'tp', 0, 0, tiled=True)  10.8 us
  transfers between devices with their start and end apart: 8, of which 6 were waited for; matrix products, arithmetic and copies ran while one was open for 6% of the time, Pallas kernels for 8%

profile of v4, /device:TPU:1, one launch (start us, length us, event | category | flops | bytes accessed | tf_op | source)
XLA Modules:
  0.0 306.8 jit_solution(12148616570862167079)
XLA Ops:
  6.5 0.8 convert_bitcast_fusion
  7.4 1.0 broadcast_in_dim.37
  8.4 8.6 %all-to-all-start = ((bf16[32,48,192]{2,1,0:T(8,128)(2,1)}), bf16[32,48,192]{2,1,0:T(8,128)(2,1)S(1)}, u32[]{:S(2)}, u32[]{:S(2)}) async-start(bf16[32,48,192]{2,1,0:T(8,128)(2,1)} %broadcast_in_dim.37), calls=%async_computation | async-start | bytes 1572864 | tf_op jit(solution)/shard_map/all_to_all | solution.py:352
  17.0 0.0 all-gather.5.cloned.1.call-start
  17.1 0.1 copy.38
  17.2 0.1 reshape.168
  17.3 0.0 copy-done.15
  17.3 0.1 pad.7.clone
  17.4 0.1 maximum_maximum_fusion
  17.5 0.0 copy-done
  17.5 0.6 gather_fusion
  18.3 13.4 %all-to-all-done = bf16[32,48,192]{2,1,0:T(8,128)(2,1)S(1)} async-done(((bf16[32,48,192]{2,1,0:T(8,128)(2,1)}), bf16[32,48,192]{2,1,0:T(8,128)(2,1)S(1)}, u32[]{:S(2)}, u32[]{:S(2)}) %all-to-all-start) | async-done | bytes 589856 | tf_op jit(solution)/shard_map/all_to_all | solution.py:352
  31.7 0.3 copy.40
  32.0 1.5 reshape.148
  33.5 26.3 %all_to_all.40 = bf16[8,272,128]{2,1,0:T(8,128)(2,1)S(1)} all-to-all(bf16[8,272,128]{2,1,0:T(8,128)(2,1)S(1)} %pad_maximum_fusion.2), channel_id=1, replica_groups={{0,16,32,48,64,80,96,112},{8,24,40,56,72,88,104,120},{128,144,160,176,1..., dimensions={0} | all-to-all | bytes 1114112 | tf_op jit(solution)/shard_map/all_to_all | solution.py:375
  59.8 0.0 all-gather.5.cloned.1.call-update
  59.9 0.2 broadcast_in_dim.38
  60.0 1.3 pad_maximum_fusion
  61.3 4.5 %all-to-all-start.2 = ((bf16[4,8,176,128]{3,2,1,0:T(8,128)(2,1)}), bf16[4,8,176,128]{3,2,1,0:T(8,128)(2,1)S(1)}, u32[]{:S(2)}, u32[]{:S(2)}) async-start(bf16[4,8,176,128]{3,2,1,0:T(8,128)(2,1)} %pad_maximum_fusion), calls=%async_computation.2 | async-start | bytes 2883584 | tf_op jit(solution)/shard_map/all_to_all | solution.py:385
  66.5 0.0 copy-done.18
  66.5 0.1 convert_element_type.35
  66.6 0.3 reshape.141
  67.0 0.9 pad_maximum_fusion.1
  67.8 1.9 fusion
  69.7 14.0 %all-to-all-done.2 = bf16[4,8,176,128]{3,2,1,0:T(8,128)(2,1)S(1)} async-done(((bf16[4,8,176,128]{3,2,1,0:T(8,128)(2,1)}), bf16[4,8,176,128]{3,2,1,0:T(8,128)(2,1)S(1)}, u32[]{:S(2)}, u32[]{:S(2)}) %all-to-all-start.2) | async-done | bytes 1441824 | tf_op jit(solution)/shard_map/all_to_all | solution.py:385
  83.8 0.1 slice.26
  83.9 0.8 copy.42
  84.6 0.2 copy.54
  84.9 4.2 %all-to-all-start.3 = ((bf16[8,72,512]{2,1,0:T(8,128)(2,1)}), bf16[8,72,512]{2,1,0:T(8,128)(2,1)}, u32[]{:S(2)}, u32[]{:S(2)}) async-start(bf16[8,72,512]{2,1,0:T(8,128)(2,1)} %pad_maximum_fusion.1), calls=%async_computation.3 | async-start | bytes 1179648 | tf_op jit(solution)/shard_map/all_to_all | solution.py:402
  89.1 0.0 copy-start.7
  89.1 1.9 copy-done.7
  91.0 16.5 %attention.1 = bf16[8,128,192]{2,1,0:T(8,128)(2,1)S(1)} custom-call(s32[1]{0:T(128)S(6)} %copy.55.length_ref, bf16[1024,1536]{1,0:T(8,128)(2,1)S(1)} %copy-done.7, f32[1,1536]{1,0:T(1,128)S(1)} %reshape.140.gain_ref, bf16[1536,384]{1,0:T(8,128)(2,1)S(1)} %bitcast.67, bf16[1024,128]{1,0:T(8,128)(2,1)S(1)} %bitcast.69, ...), custom_call_target="tpu_custom_call" | custom-call | flops 30000001024 | bytes 8388608 | tf_op jit(solution)/shard_map/attention/pallas_call | solution.py:120
  107.5 0.0 copy-start.19
  107.5 0.0 copy-start.14
  107.5 6.7 %all-to-all-done.3 = bf16[8,72,512]{2,1,0:T(8,128)(2,1)} async-done(((bf16[8,72,512]{2,1,0:T(8,128)(2,1)}), bf16[8,72,512]{2,1,0:T(8,128)(2,1)}, u32[]{:S(2)}, u32[]{:S(2)}) %all-to-all-start.3) | async-done | bytes 589856 | tf_op jit(solution)/shard_map/all_to_all | solution.py:402
  114.3 0.3 copy.44
  114.5 10.8 %all_to_all.41 = bf16[8,128,192]{1,2,0:T(8,128)(2,1)S(1)} all-to-all(bf16[8,128,192]{1,2,0:T(8,128)(2,1)S(1)} %copy.44), channel_id=1, replica_groups=mesh['ep'=32,'tp'=8] {'tp'}, dimensions={0} | all-to-all | bytes 786432 | tf_op jit(solution)/shard_map/all_to_all | solution.py:405
  125.3 3.7 %all-to-all-start.5 = ((bf16[8,72,512]{2,1,0:T(8,128)(2,1)}), bf16[8,72,512]{2,1,0:T(8,128)(2,1)S(1)}, u32[]{:S(2)}, u32[]{:S(2)}) async-start(bf16[8,72,512]{2,1,0:T(8,128)(2,1)} %all-to-all-done.3), calls=%async_computation.5 | async-start | bytes 1179648 | tf_op jit(solution)/shard_map/all_to_all | solution.py:407
  129.0 0.2 all-gather.7.cloned.1.call-start
  129.3 1.0 constant_dynamic-slice_fusion.rows_ref
  130.4 0.2 copy.46.parts_ref
  130.6 0.0 all-gather.5.cloned.1.call-done
  130.6 2.3 copy-done.4
  133.0 4.6 %project_and_dispatch.1 = (f32[128,1536]{1,0:T(8,128)S(1)}, bf16[1536,1536]{1,0:T(8,128)(2,1)S(1)}, f32[32,128]{1,0:T(8,128)S(1)}, f32[32,128]{1,0:T(8,128)S(1)}) custom-call(bf16[8,128,192]{2,1,0:T(8,128)(2,1)S(1)} %copy.46.parts_ref, bf16[8,2,96,1536]{3,2,1,0:T(8,128)(2,1)S(1)} %bitcast.64, bf16[128,1536]{1,0:T(8,128)(2,1)S(1)} %constant_dynamic-slice_fusion.rows_ref, ...), custom_call_target="tpu_custom_call" | custom-call | flops 1207959552 | bytes 9437184 | tf_op jit(solution)/shard_map/project_and_dispatch/pallas_call | solution.py:201
  137.6 2.1 copy-done.2
  139.8 0.9 copy-done.6
  140.6 0.0 all-to-all-done.5
  140.7 0.8 copy-done.11
  141.5 0.0 all-gather.7.cloned.1.call-update
  141.5 9.7 %all-to-all-start.6 = ((bf16[32,48,1536]{2,1,0:T(8,128)(2,1)}), bf16[32,48,1536]{2,1,0:T(8,128)(2,1)}, u32[]{:S(2)}, u32[]{:S(2)}) async-start(bf16[32,48,1536]{2,1,0:T(8,128)(2,1)} %bitcast.62), calls=%async_computation.6 | async-start | bytes 9437184 | tf_op jit(solution)/shard_map/all_to_all | solution.py:352
  151.2 48.7 %all-gather.7.cloned.1.call-done = bf16[64,72,512]{2,1,0:T(8,128)(2,1)} async-done(((bf16[8,72,512]{2,1,0:T(8,128)(2,1)}), bf16[64,72,512]{2,1,0:T(8,128)(2,1)}) %all-gather.7.cloned.1.call-update) | async-done | bytes 4718608 | tf_op jit(solution)/shard_map/all_gather | solution.py:419
  199.9 2.2 slice.28
  202.1 3.3 %copy.47 = bf16[8,8,24,2,512]{4,3,2,1,0:T(2,128)(2,1)S(1)} copy(bf16[8,8,24,2,512]{4,2,3,0,1:T(8,128)(2,1)S(1)} %bitcast.72) | data formatting | bytes 6291456 | tf_op jit(solution)/shard_map/transpose | solution.py:421
  205.4 0.9 copy.50
  206.3 1.5 slice_bitcast_fusion
  207.8 1.3 copy.48
  209.1 4.0 %all-to-all-done.6 = bf16[32,48,1536]{2,1,0:T(8,128)(2,1)} async-done(((bf16[32,48,1536]{2,1,0:T(8,128)(2,1)}), bf16[32,48,1536]{2,1,0:T(8,128)(2,1)}, u32[]{:S(2)}, u32[]{:S(2)}) %all-to-all-start.6) | async-done | bytes 4718624 | tf_op jit(solution)/shard_map/all_to_all | solution.py:352
  213.1 1.4 copy-done.5
  214.5 10.0 %experts.1 = bf16[1536,1536]{1,0:T(8,128)(2,1)S(1)} custom-call(bf16[1536,1536]{1,0:T(8,128)(2,1)} %bitcast.28.rows_ref, bf16[1536,1024]{1,0:T(8,128)(2,1)S(1)} %bitcast.65, bf16[512,1536]{1,0:T(8,128)(2,1)S(1)} %bitcast.66), custom_call_target="tpu_custom_call" | custom-call | flops 7247757312 | bytes 14155776 | tf_op jit(solution)/shard_map/experts/pallas_call | solution.py:275
  224.6 2.1 copy-done.3
  226.7 5.0 %all-to-all-start.7 = ((bf16[32,48,1536]{2,1,0:T(8,128)(2,1)}), bf16[32,48,1536]{2,1,0:T(8,128)(2,1)}, u32[]{:S(2)}, u32[]{:S(2)}) async-start(bf16[32,48,1536]{2,1,0:T(8,128)(2,1)} %bitcast.63), calls=%async_computation.7 | async-start | bytes 9437184 | tf_op jit(solution)/shard_map/all_to_all | solution.py:352
  231.7 1.9 weighing.1
  233.7 60.1 %all-to-all-done.7 = bf16[32,48,1536]{2,1,0:T(8,128)(2,1)} async-done(((bf16[32,48,1536]{2,1,0:T(8,128)(2,1)}), bf16[32,48,1536]{2,1,0:T(8,128)(2,1)}, u32[]{:S(2)}, u32[]{:S(2)}) %all-to-all-start.7) | async-done | bytes 4718624 | tf_op jit(solution)/shard_map/all_to_all | solution.py:352
  293.7 6.3 %combine.1 = bf16[128,1536]{1,0:T(8,128)(2,1)} custom-call(s32[1]{0:T(128)S(6)} %sub.7.live_ref, bf16[128,1536]{1,0:T(8,128)(2,1)} %get-tuple-element.36.high_ref, bf16[128,1536]{1,0:T(8,128)(2,1)} %get-tuple-element.37.low_ref, bf16[1536,1536]{1,0:T(8,128)(2,1)} %bitcast.36.returned_ref, f32[128,1536]{1,0:T(8,128)} %copy-done.6), custom_call_target="tpu_custom_call" | custom-call | flops 1207959552 | bytes 5898240 | tf_op jit(solution)/shard_map/combine/pallas_call | solution.py:309
  (52 shorter events, 0.4 us)
Async XLA Ops:
  6.5 11.0 %copy-start = (bf16[8,16,128]{2,1,0:T(8,128)(2,1)S(1)}, bf16[8,16,128]{2,1,0:T(8,128)(2,1)}, u32[]{:S(2)}) copy-start(bf16[8,16,128]{2,1,0:T(8,128)(2,1)} %param.21) | copy-start | bytes 98308
  6.5 10.5 %copy-start.20 = (s32[32,1,2]{0,2,1:T(2,128)S(1)}, s32[32,1,2]{0,2,1:T(2,128)}, u32[]{:S(2)}) copy-start(s32[32,1,2]{0,2,1:T(2,128)} %param.22) | copy-start | bytes 772
  6.5 10.5 %copy-start.16 = (f32[48,64]{1,0:T(8,128)S(1)}, f32[48,64]{1,0:T(8,128)}, u32[]{:S(2)}) copy-start(f32[48,64]{1,0:T(8,128)} %param.18) | copy-start | bytes 36868
  6.5 10.5 %copy-start.17 = (f32[48,64]{1,0:T(8,128)S(1)}, f32[48,64]{1,0:T(8,128)}, u32[]{:S(2)}) copy-start(f32[48,64]{1,0:T(8,128)} %param.19) | copy-start | bytes 36868
  6.5 10.7 %copy-start.15 = (f32[48,192]{1,0:T(8,128)S(1)}, f32[48,192]{1,0:T(8,128)}, u32[]{:S(2)}) copy-start(f32[48,192]{1,0:T(8,128)} %param.17) | copy-start | bytes 110596
  8.4 23.4 %all-to-all-start = ((bf16[32,48,192]{2,1,0:T(8,128)(2,1)}), bf16[32,48,192]{2,1,0:T(8,128)(2,1)S(1)}, u32[]{:S(2)}, u32[]{:S(2)}) async-start(bf16[32,48,192]{2,1,0:T(8,128)(2,1)} %broadcast_in_dim.37), calls=%async_computation | async-start | bytes 1572864 | tf_op jit(solution)/shard_map/all_to_all | solution.py:352
  17.0 113.7 %all-gather.5.cloned.1.call-start = ((), (), s32[]{:S(2)}) async-start(), calls=%async_computation.8 | async-start | bytes 5308416 | tf_op jit(solution)/shard_map/all_gather | solution.py:377
  61.3 5.2 %copy-start.18 = (f32[1536]{0:T(1024)S(1)}, f32[1536]{0:T(1024)}, u32[]{:S(2)}) copy-start(f32[1536]{0:T(1024)} %param.16) | copy-start | bytes 18436
  61.3 5.2 %copy-start.13 = (f32[1,64,1536]{2,1,0:T(8,128)S(1)}, f32[1,64,1536]{2,1,0:T(8,128)}, u32[]{:S(2)}) copy-start(f32[1,64,1536]{2,1,0:T(8,128)} %param.27) | copy-start | bytes 1179652
  61.3 5.3 %copy-start.12 = (f32[1,192,1024]{2,1,0:T(8,128)S(1)}, f32[1,192,1024]{2,1,0:T(8,128)}, u32[]{:S(2)}) copy-start(f32[1,192,1024]{2,1,0:T(8,128)} %param.26) | copy-start | bytes 2359300
  61.3 22.4 %all-to-all-start.2 = ((bf16[4,8,176,128]{3,2,1,0:T(8,128)(2,1)}), bf16[4,8,176,128]{3,2,1,0:T(8,128)(2,1)S(1)}, u32[]{:S(2)}, u32[]{:S(2)}) async-start(bf16[4,8,176,128]{3,2,1,0:T(8,128)(2,1)} %pad_maximum_fusion), calls=%async_computation.2 | async-start | bytes 2883584 | tf_op jit(solution)/shard_map/all_to_all | solution.py:385
  84.9 29.4 %all-to-all-start.3 = ((bf16[8,72,512]{2,1,0:T(8,128)(2,1)}), bf16[8,72,512]{2,1,0:T(8,128)(2,1)}, u32[]{:S(2)}, u32[]{:S(2)}) async-start(bf16[8,72,512]{2,1,0:T(8,128)(2,1)} %pad_maximum_fusion.1), calls=%async_computation.3 | async-start | bytes 1179648 | tf_op jit(solution)/shard_map/all_to_all | solution.py:402
  89.1 1.9 copy-start.7
  107.5 21.7 %copy-start.19 = (f32[1536]{0:T(1024)S(1)}, f32[1536]{0:T(1024)}, u32[]{:S(2)}) copy-start(f32[1536]{0:T(1024)} %param.23) | copy-start | bytes 18436
  107.5 21.7 %copy-start.14 = (bf16[1536,32]{0,1:T(8,128)(2,1)S(1)}, bf16[1536,32]{0,1:T(8,128)(2,1)}, u32[]{:S(2)}) copy-start(bf16[1536,32]{0,1:T(8,128)(2,1)} %param.24) | copy-start | bytes 294916
  125.3 5.3 %copy-start.10 = (s32[128,8]{0,1:T(8,128)S(1)}, s32[128,8]{0,1:T(8,128)}, u32[]{:S(2)}) copy-start(s32[128,8]{0,1:T(8,128)} %param.25) | copy-start | bytes 12292
  125.3 15.3 %all-to-all-start.5 = ((bf16[8,72,512]{2,1,0:T(8,128)(2,1)}), bf16[8,72,512]{2,1,0:T(8,128)(2,1)S(1)}, u32[]{:S(2)}, u32[]{:S(2)}) async-start(bf16[8,72,512]{2,1,0:T(8,128)(2,1)} %all-to-all-done.3), calls=%async_computation.5 | async-start | bytes 1179648 | tf_op jit(solution)/shard_map/all_to_all | solution.py:407
  129.0 70.9 %all-gather.7.cloned.1.call-start = ((), (), s32[]{:S(2)}) async-start(), calls=%async_computation.9 | async-start | bytes 5308416 | tf_op jit(solution)/shard_map/all_gather | solution.py:419
  130.6 2.3 copy-start.4
  137.6 2.1 copy-start.2
  139.8 0.9 copy-start.6
  140.6 0.9 copy-start.8
  140.6 0.9 copy-start.9
  140.6 0.8 copy-start.11
  141.5 71.6 %all-to-all-start.6 = ((bf16[32,48,1536]{2,1,0:T(8,128)(2,1)}), bf16[32,48,1536]{2,1,0:T(8,128)(2,1)}, u32[]{:S(2)}, u32[]{:S(2)}) async-start(bf16[32,48,1536]{2,1,0:T(8,128)(2,1)} %bitcast.62), calls=%async_computation.6 | async-start | bytes 9437184 | tf_op jit(solution)/shard_map/all_to_all | solution.py:352
  213.1 1.4 copy-start.5
  224.6 2.2 copy-start.3
  226.7 67.0 %all-to-all-start.7 = ((bf16[32,48,1536]{2,1,0:T(8,128)(2,1)}), bf16[32,48,1536]{2,1,0:T(8,128)(2,1)}, u32[]{:S(2)}, u32[]{:S(2)}) async-start(bf16[32,48,1536]{2,1,0:T(8,128)(2,1)} %bitcast.63), calls=%async_computation.7 | async-start | bytes 9437184 | tf_op jit(solution)/shard_map/all_to_all | solution.py:352
  293.7 6.3 %copy-start.1 = (bf16[8,16,128]{2,1,0:T(8,128)(2,1)S(1)}, bf16[8,16,128]{2,1,0:T(8,128)(2,1)}, u32[]{:S(2)}) copy-start(bf16[8,16,128]{2,1,0:T(8,128)(2,1)} %param.21) | copy-start | bytes 98308
Sparse Core Ops, SparseCore 0:
  59.9 64.8 all-gather.4
  141.6 58.2 all-gather.6

commit v5 on v4

--- a/solution.py
+++ b/solution.py
@@ -39,10 +39,10 @@
 
 
 def attention_body(
-    length_ref, tokens_ref, gain_ref, weight_ref, pages_ref, cosine_ref, sine_ref,
+    length_ref, normalized_ref, weight_ref, pages_ref, cosine_ref, sine_ref,
     out_ref, queries, keys, values,
 ):
-    seq_len = tokens_ref.shape[0]
+    seq_len = normalized_ref.shape[0]
     prefix = pages_ref.shape[0]
     heads = queries.shape[0]
     chunk = 256
@@ -53,10 +53,9 @@
         keys[:, c : c + chunk] = rows.astype(jnp.float32).T[:HEAD_WIDTH].astype(jnp.bfloat16)
         values[c : c + chunk, :] = jnp.concatenate([rows[:, HEAD_WIDTH:], ones], axis=1)
     for c in range(0, seq_len, chunk):
-        normalized = rms_scale(
-            tokens_ref[c : c + chunk, :].astype(jnp.float32), gain_ref[...]
-        ).astype(jnp.bfloat16)
-        projected = jnp.dot(normalized, weight_ref[...], preferred_element_type=jnp.float32)
+        projected = jnp.dot(
+            normalized_ref[c : c + chunk, :], weight_ref[...], preferred_element_type=jnp.float32
+        )
         plain = projected[:, :256]
         partner = jnp.where(
             lane % HEAD_WIDTH < HEAD_WIDTH // 2,
@@ -79,19 +78,17 @@
         values[prefix + c : prefix + c + chunk, :] = jnp.concatenate(
             [projected[:, 256 : 256 + HEAD_WIDTH].astype(jnp.bfloat16), ones], axis=1
         )
-    block = out_ref.shape[1]
     length = length_ref[0]
-    column = lax.broadcasted_iota(jnp.int32, (block, seq_len), 1)
-    row = lax.broadcasted_iota(jnp.int32, (block, seq_len), 0)
-
-    def one_block(i, carry):
-        start = pl.multiple_of(i * block, block)
+    for start in range(0, seq_len, chunk):
+        seen = start + chunk
+        column = lax.broadcasted_iota(jnp.int32, (chunk, seen), 1)
+        row = lax.broadcasted_iota(jnp.int32, (chunk, seen), 0)
         allowed = (column <= row + start) & (column < length)
         outs = []
         for h in range(heads):
-            query = queries[h, pl.ds(start, block), :]
+            query = queries[h, start:seen, :]
             cached = jnp.dot(query, keys[:, :prefix], preferred_element_type=jnp.float32)
-            own = jnp.dot(query, keys[:, prefix:], preferred_element_type=jnp.float32)
+            own = jnp.dot(query, keys[:, prefix : prefix + seen], preferred_element_type=jnp.float32)
             own = jnp.where(allowed, own, -1e30)
             top = jnp.maximum(
                 jnp.max(cached, axis=1, keepdims=True), jnp.max(own, axis=1, keepdims=True)
@@ -102,43 +99,40 @@
                 preferred_element_type=jnp.float32,
             ) + jnp.dot(
                 jnp.exp(own - top).astype(jnp.bfloat16),
-                values[prefix:, :],
+                values[prefix : prefix + seen, :],
                 preferred_element_type=jnp.float32,
             )
             outs.append(total[:, :HEAD_WIDTH] / total[:, HEAD_WIDTH : HEAD_WIDTH + 1])
-        out_ref[i] = jnp.concatenate(outs, axis=1).astype(jnp.bfloat16)
-        return carry
-
-    lax.fori_loop(0, out_ref.shape[0], one_block, 0)
-
-
-def attention(lengths, tokens, gain, weight, pages, cosine, sine, blocks):
-    seq_len, model_width = tokens.shape
+        out_ref[start:seen, :] = jnp.concatenate(outs, axis=1).astype(jnp.bfloat16)
+
+
+def attention(lengths, normalized, weight, pages, cosine, sine):
+    seq_len, model_width = normalized.shape
     heads = 3
     total = seq_len + pages.shape[0]
     vmem = pl.BlockSpec(memory_space=pltpu.VMEM)
     return pl.pallas_call(
         attention_body,
-        out_shape=jax.ShapeDtypeStruct((blocks, seq_len // blocks, heads * HEAD_WIDTH), jnp.bfloat16),
-        in_specs=[pl.BlockSpec(memory_space=pltpu.SMEM)] + [vmem] * 6,
+        out_shape=jax.ShapeDtypeStruct((seq_len, heads * HEAD_WIDTH), jnp.bfloat16),
+        in_specs=[pl.BlockSpec(memory_space=pltpu.SMEM)] + [vmem] * 5,
         out_specs=vmem,
         scratch_shapes=[
             pltpu.VMEM((heads, seq_len, HEAD_WIDTH), jnp.bfloat16),
             pltpu.VMEM((HEAD_WIDTH, total), jnp.bfloat16),
             pltpu.VMEM((total, 2 * HEAD_WIDTH), jnp.bfloat16),
         ],
-        compiler_params=pltpu.CompilerParams(vmem_limit_bytes=40 << 20),
+        compiler_params=pltpu.CompilerParams(vmem_limit_bytes=48 << 20),
         cost_estimate=pl.CostEstimate(
-            flops=30_000_000_000, bytes_accessed=8 << 20, transcendentals=heads * seq_len * total
+            flops=12_000_000_000, bytes_accessed=8 << 20, transcendentals=heads * seq_len * total
         ),
         name="attention",
-    )(lengths, tokens, gain.reshape(1, model_width), weight, pages, cosine, sine)
+    )(lengths, normalized, weight, pages, cosine, sine)
 
 
 def project_body(
     parts_ref, weight_hbm, rows_ref, gain_ref, router_ref, ids_ref,
     hidden_ref, send_ref, rank_ref, gates_ref,
-    weight, attended, place, sem,
+    weight, attended, place, staged, sem, out_sem,
 ):
     copies = []
     for z in range(8):
@@ -183,15 +177,22 @@
     hidden = hidden_ref[...]
     moe_in = rms_scale(hidden, gain_ref[...]).astype(jnp.bfloat16)
     for c in range(0, EXPERTS * CAPACITY, 256):
-        send_ref[c : c + 256, :] = jnp.dot(
+        staged[c : c + 256, :] = jnp.dot(
             place[c : c + 256, :], moe_in, preferred_element_type=jnp.float32
         ).astype(jnp.bfloat16)
+        pltpu.make_async_copy(
+            staged.at[pl.ds(c, 256)], send_ref.at[pl.ds(c, 256)], out_sem.at[c // 256]
+        ).start()
     logits = lax.dot_general(
         router_ref[...], moe_in, (((1,), (1,)), ((), ())), preferred_element_type=jnp.float32
     )
     top_logit = jnp.max(jnp.where(chosen > 0.0, logits, -3e38), axis=0, keepdims=True)
     raised = jnp.where(chosen > 0.0, jnp.exp(jnp.minimum(logits - top_logit, 0.0)), 0.0)
     gates_ref[...] = raised / jnp.sum(raised, axis=0, keepdims=True)
+    for c in range(0, EXPERTS * CAPACITY, 256):
+        pltpu.make_async_copy(
+            staged.at[pl.ds(c, 256)], send_ref.at[pl.ds(c, 256)], out_sem.at[c // 256]
+        ).wait()
 
 
 def project_and_dispatch(parts, output_weight, own_rows, moe_gain, router_hosted, ids_by_choice):
@@ -202,17 +203,19 @@
         project_body,
         out_shape=(
             jax.ShapeDtypeStruct((row_count, model_width), jnp.float32),
-            jax.ShapeDtypeStruct((slots, model_width), jnp.bfloat16),
+            pltpu.HBM((slots, model_width), jnp.bfloat16),
             jax.ShapeDtypeStruct((EXPERTS, row_count), jnp.float32),
             jax.ShapeDtypeStruct((EXPERTS, row_count), jnp.float32),
         ),
         in_specs=[vmem, pl.BlockSpec(memory_space=pltpu.HBM), vmem, vmem, vmem, vmem],
-        out_specs=(vmem, vmem, vmem, vmem),
+        out_specs=(vmem, pl.BlockSpec(memory_space=pltpu.HBM), vmem, vmem),
         scratch_shapes=[
             pltpu.VMEM((model_width, model_width), jnp.bfloat16),
             pltpu.VMEM((row_count, model_width), jnp.bfloat16),
             pltpu.VMEM((slots, row_count), jnp.bfloat16),
+            pltpu.VMEM((slots, model_width), jnp.bfloat16),
             pltpu.SemaphoreType.DMA((16,)),
+            pltpu.SemaphoreType.DMA((6,)),
         ],
         compiler_params=pltpu.CompilerParams(vmem_limit_bytes=40 << 20),
         cost_estimate=pl.CostEstimate(
@@ -223,7 +226,7 @@
         name="project_and_dispatch",
     )(
         parts,
-        output_weight.reshape(8, 2, 96, model_width),
+        pltpu.with_memory_space_constraint(output_weight.reshape(8, 2, 96, model_width), pltpu.HBM),
         own_rows,
         moe_gain.reshape(1, model_width),
         router_hosted,
@@ -231,7 +234,7 @@
     )
 
 
-def weigh_body(rank_ref, gates_ref, high_ref, low_ref, weigh):
+def weigh_body(rank_ref, gates_ref, both_ref, weigh):
     tokens = rank_ref.shape[1]
     slot = lax.broadcasted_iota(jnp.int32, (CAPACITY, tokens), 0).astype(jnp.float32)
     for g in range(EXPERTS):
@@ -241,20 +244,19 @@
     for c in range(0, EXPERTS * CAPACITY, 128):
         by_token = weigh[c : c + 128, :].T
         high = by_token.astype(jnp.bfloat16)
-        high_ref[:, c : c + 128] = high
-        low_ref[:, c : c + 128] = (by_token - high.astype(jnp.float32)).astype(jnp.bfloat16)
+        both_ref[:tokens, c : c + 128] = high
+        both_ref[tokens:, c : c + 128] = (by_token - high.astype(jnp.float32)).astype(jnp.bfloat16)
 
 
 def weighing(rank, gates):
     row_count = rank.shape[1]
     slots = EXPERTS * CAPACITY
     vmem = pl.BlockSpec(memory_space=pltpu.VMEM)
-    shape = jax.ShapeDtypeStruct((row_count, slots), jnp.bfloat16)
     return pl.pallas_call(
         weigh_body,
-        out_shape=(shape, shape),
+        out_shape=jax.ShapeDtypeStruct((2 * row_count, slots), jnp.bfloat16),
         in_specs=[vmem, vmem],
-        out_specs=(vmem, vmem),
+        out_specs=vmem,
         scratch_shapes=[pltpu.VMEM((slots, row_count), jnp.float32)],
         cost_estimate=pl.CostEstimate(flops=1 << 20, bytes_accessed=1 << 20, transcendentals=0),
         name="weighing",
@@ -271,10 +273,10 @@
 
 def experts(rows, gate_up, down):
     count, model_width = rows.shape
-    tile = 256
+    tile = 512
     return pl.pallas_call(
         expert_body,
-        out_shape=jax.ShapeDtypeStruct((count, model_width), jnp.bfloat16),
+        out_shape=pltpu.HBM((count, model_width), jnp.bfloat16),
         grid=(count // tile,),
         in_specs=[
             pl.BlockSpec((tile, model_width), lambda i: (i, 0)),
@@ -292,39 +294,48 @@
     )(rows, gate_up, down)
 
 
-def combine_body(live_ref, high_ref, low_ref, returned_ref, hidden_ref, out_ref):
-    mixed = jnp.dot(high_ref[...], returned_ref[...], preferred_element_type=jnp.float32) + jnp.dot(
-        low_ref[...], returned_ref[...], preferred_element_type=jnp.float32
-    )
-    row = lax.broadcasted_iota(jnp.int32, mixed.shape, 0)
-    out_ref[...] = jnp.where(row < live_ref[0], hidden_ref[...] + mixed, 0.0).astype(jnp.bfloat16)
-
-
-def combine(live, high, low, returned, hidden):
+def combine_body(live_ref, both_ref, returned_ref, hidden_ref, out_ref, total):
+    step = pl.program_id(0)
+    tokens = hidden_ref.shape[0]
+
+    @pl.when(step == 0)
+    def _():
+        total[...] = hidden_ref[...]
+
+    mixed = jnp.dot(both_ref[...], returned_ref[...], preferred_element_type=jnp.float32)
+    total[...] += mixed[:tokens] + mixed[tokens:]
+
+    @pl.when(step == pl.num_programs(0) - 1)
+    def _():
+        row = lax.broadcasted_iota(jnp.int32, total.shape, 0)
+        out_ref[...] = jnp.where(row < live_ref[0], total[...], 0.0).astype(jnp.bfloat16)
+
+
+def combine(live, both, returned, hidden):
     row_count, model_width = hidden.shape
     slots = returned.shape[0]
-    tile = 256
-    whole = pl.BlockSpec((row_count, slots), lambda i: (0, 0))
-    column = pl.BlockSpec((row_count, tile), lambda i: (0, i))
+    tile = slots // 2
+    whole = pl.BlockSpec((row_count, model_width), lambda i: (0, 0))
     return pl.pallas_call(
         combine_body,
         out_shape=jax.ShapeDtypeStruct((row_count, model_width), jnp.bfloat16),
-        grid=(model_width // tile,),
+        grid=(slots // tile,),
         in_specs=[
             pl.BlockSpec(memory_space=pltpu.SMEM),
+            pl.BlockSpec((2 * row_count, tile), lambda i: (0, i)),
+            pl.BlockSpec((tile, model_width), lambda i: (i, 0)),
             whole,
-            whole,
-            pl.BlockSpec((slots, tile), lambda i: (0, i)),
-            column,
-        ],
-        out_specs=column,
+        ],
+        out_specs=whole,
+        scratch_shapes=[pltpu.VMEM((row_count, model_width), jnp.float32)],
+        compiler_params=pltpu.CompilerParams(vmem_limit_bytes=24 << 20),
         cost_estimate=pl.CostEstimate(
             flops=4 * row_count * slots * model_width,
             bytes_accessed=2 * slots * model_width + 6 * row_count * model_width,
             transcendentals=0,
         ),
         name="combine",
-    )(live, high, low, returned, hidden)
+    )(live, both, returned, hidden)
 
 
 def on_device(
@@ -364,10 +375,14 @@
     ).astype(jnp.bfloat16)
     slabs = weight_shard.reshape(48, 3, 128).transpose(1, 0, 2).reshape(144, 128)
     pages = key_value_pages[page_table[:, 0, :]].reshape(2, 8, 2, 32, 128)
+    gate_up_slabs = gate_up_proj.astype(jnp.bfloat16).reshape(8, 24, 8, 128).transpose(0, 2, 1, 3)
+    down_slabs = down_proj.astype(jnp.bfloat16).reshape(8, 8, 12, 128).transpose(0, 2, 1, 3)
     payload = jnp.concatenate(
         [
             jnp.broadcast_to(slabs[None], (8, 144, 128)),
             pages.transpose(1, 0, 2, 3, 4).reshape(8, 128, 128),
+            gate_up_slabs.reshape(8, 192, 128),
+            down_slabs.reshape(8, 96, 128),
         ],
         axis=1,
     )
@@ -378,7 +393,7 @@
     payload = jnp.concatenate(
         [
             jnp.broadcast_to(along_z[None, :, :144], (4, 8, 144, 128)),
-            along_z[:, 144:].reshape(8, 4, 32, 128).transpose(1, 0, 2, 3),
+            along_z[:, 144:272].reshape(8, 4, 32, 128).transpose(1, 0, 2, 3),
         ],
         axis=2,
     )
@@ -391,20 +406,15 @@
     )
     prefix = across[:, :, 144:].reshape(2, 2, 8, 32, 128).transpose(0, 2, 1, 3, 4).reshape(-1, 128)
     cosine, sine = rotary_tables(seq_len, prefix.shape[0])
-    eighths = jnp.concatenate(
-        [
-            gate_up_proj.astype(jnp.bfloat16).reshape(8, 24, 2, 512).transpose(0, 2, 1, 3).reshape(8, 48, 512),
-            down_proj.astype(jnp.bfloat16).reshape(8, 8, 3, 512).transpose(0, 2, 1, 3).reshape(8, 24, 512),
-        ],
-        axis=1,
-    )
-    eighths, weight, prefix = barrier((eighths, weight, prefix))
-    by_expert = lax.all_to_all(eighths, "ep", 0, 0, axis_index_groups=Z_GROUPS, tiled=True)
-    attended = attention(lengths, tokens_in, attn_gain, weight, prefix, cosine, sine, 8)
-    attended, by_expert = barrier((attended, by_expert))
-    attn_parts = lax.all_to_all(attended, "tp", 0, 0, tiled=True)
-    attn_parts, by_expert = barrier((attn_parts, by_expert))
+    normalized = rms_scale(tokens_in.astype(jnp.float32), attn_gain).astype(jnp.bfloat16)
+    by_expert, weight, prefix = barrier((along_z[:, 272:], weight, prefix))
     hosted = lax.all_to_all(by_expert, "tp", 0, 0, tiled=True)
+    attended = attention(lengths, normalized, weight, prefix, cosine, sine)
+    attended, hosted = barrier((attended, hosted))
+    attn_parts = lax.all_to_all(
+        attended.reshape(8, row_count, attended.shape[1]), "tp", 0, 0, tiled=True
+    )
+    planes = lax.all_gather(hosted, "ep", axis_index_groups=Z_GROUPS)
     own_rows = lax.dynamic_slice_in_dim(tokens_in, tp_index * row_count, row_count, 0)
     router_hosted = router.T.reshape(2, 8, 2, model_width).transpose(0, 2, 1, 3)
     hidden, send_rows, rank, gates = project_and_dispatch(
@@ -415,20 +425,18 @@
         router_hosted.reshape(EXPERTS, model_width),
         expert_ids.T,
     )
-    send_rows, hosted = barrier((send_rows, hosted))
-    planes = lax.all_gather(hosted, "ep", axis_index_groups=Z_GROUPS)
     gate_up_full = (
-        planes[:, :, :48].reshape(8, 8, 2, 24, 512).transpose(1, 0, 3, 2, 4).reshape(model_width, 2 * FF)
+        planes[:, :, :192].reshape(8, 8, 8, 24, 128).transpose(1, 0, 3, 2, 4).reshape(model_width, 2 * FF)
     )
     down_full = (
-        planes[:, :, 48:].reshape(8, 8, 3, 8, 512).transpose(1, 0, 3, 2, 4).reshape(FF, model_width)
+        planes[:, :, 192:].reshape(8, 8, 12, 8, 128).transpose(1, 0, 3, 2, 4).reshape(FF, model_width)
     )
     received = in_plane(send_rows.reshape(EXPERTS, CAPACITY, model_width))
-    high, low = weighing(rank, gates)
+    both = weighing(rank, gates)
     expert_out = experts(received.reshape(-1, model_width), gate_up_full, down_full)
     returned = in_plane(expert_out.reshape(EXPERTS, CAPACITY, model_width))
     live = lengths - tp_index * row_count
-    return combine(live, high, low, returned.reshape(-1, model_width), hidden)
+    return combine(live, both, returned.reshape(-1, model_width), hidden)
 
 
 def solution(mesh):

time: 308 us -> 311 us (level)
  Pallas kernels: 39.4 us -> 33.3 us
  other arithmetic: 5.1 us -> 9.98 us
    all_to_all x3, waiting for transfers between devices: 77.5 us -> 97 us  [in_plane(): lax.all_to_all(rows, ('ep', 'tp'), 0, 0, axis_index_groups=PLANE_GROUPS,...]
    all_gather x1, waiting for transfers between devices: 48.7 us -> 30.3 us  [on_device(): planes = lax.all_gather(hosted, 'ep', axis_index_groups=Z_GROUPS)]
    all_to_all x1, blocking collectives: 26.3 us -> 39.6 us  [on_device(): lax.all_to_all(payload, 'ep', 0, 0, axis_index_groups=Z_GROUPS, tiled=True)]
    all_to_all x1 -> x0, blocking collectives: 10.8 us -> none  [on_device(): attn_parts = lax.all_to_all(attended, 'tp', 0, 0, tiled=True)]
    pallas_call x3, Pallas kernels: 28.5 us -> 22.3 us  [the longest x1 10.5 us: experts(): pl.pallas_call(expert_body, out_shape=pltpu.HBM((count, model_width), jnp...]
    unnamed x44 -> x51, local copies, waits for them, and re-layouts: 12.7 us -> 11.1 us
  transfers between devices with their start and end apart: 8 -> 8, of which waited for: 6 -> 6; matrix products, arithmetic and copies ran while one was open for 6% -> 8% of each run, Pallas kernels for 8% -> 6%
where the time goes in v5:
time: 311 us; the launch traced here: 310 us
  waiting for transfers between devices  145 us (47%)
  blocking collectives  39.6 us (13%)
  starting transfers between devices  37.1 us (12%)
  Pallas kernels  33.3 us (11%)
  local copies, waits for them, and re-layouts  30.5 us (10%)
  between operations  14.6 us (5%)
  other arithmetic  9.98 us (3%)
    all_to_all x3, waiting for transfers between devices, in_plane(): lax.all_to_all(rows, ('ep', 'tp'), 0, 0, axis_index_groups=PLANE_GROUPS,...  97 us
    all_to_all x1, blocking collectives, on_device(): lax.all_to_all(payload, 'ep', 0, 0, axis_index_groups=Z_GROUPS, tiled=True)  39.6 us
    all_gather x1, waiting for transfers between devices, on_device(): planes = lax.all_gather(hosted, 'ep', axis_index_groups=Z_GROUPS)  30.3 us
    all_to_all x3, starting transfers between devices, in_plane(): lax.all_to_all(rows, ('ep', 'tp'), 0, 0, axis_index_groups=PLANE_GROUPS,...  21.5 us
    unnamed x51, local copies, waits for them, and re-layouts  11.1 us
    all_to_all x1, waiting for transfers between devices, on_device(): lax.all_to_all(payload, 'ep', 0, 0, axis_index_groups=CHIP_PAIR_GROUPS, t...  11.1 us
    pallas_call x1, Pallas kernels, experts(): pl.pallas_call(expert_body, out_shape=pltpu.HBM((count, model_width), jnp...  10.5 us
    pallas_call x1, Pallas kernels, attention(): pl.pallas_call(attention_body, out_shape=jax.ShapeDtypeStruct((seq_len, h...  9.91 us
  transfers between devices with their start and end apart: 8, of which 6 were waited for; matrix products, arithmetic and copies ran while one was open for 8% of the time, Pallas kernels for 6%

profile of v5, /device:TPU:1, one launch (start us, length us, event | category | flops | bytes accessed | tf_op | source)
XLA Modules:
  0.0 310.2 jit_solution(11342264932518798341)
XLA Ops:
  6.6 0.9 convert_bitcast_fusion.2
  7.4 0.9 broadcast_in_dim.21
  8.4 8.6 %all-to-all-start = ((bf16[32,48,192]{2,1,0:T(8,128)(2,1)}), bf16[32,48,192]{2,1,0:T(8,128)(2,1)S(1)}, u32[]{:S(2)}, u32[]{:S(2)}) async-start(bf16[32,48,192]{2,1,0:T(8,128)(2,1)} %broadcast_in_dim.21), calls=%async_computation | async-start | bytes 1572864 | tf_op jit(solution)/shard_map/all_to_all | solution.py:363
  17.0 0.0 all-gather.5.cloned.1.call-start
  17.1 0.1 copy.38
  17.2 0.1 reshape.177
  17.3 0.1 pad.9.clone
  17.4 0.1 maximum_maximum_fusion
  17.5 0.6 gather_fusion
  18.2 0.1 convert_bitcast_fusion
  18.3 0.1 copy.50
  18.4 0.1 copy.40
  18.5 0.1 copy-done.16
  18.6 1.1 pad_maximum_fusion.1
  19.7 12.0 %all-to-all-done = bf16[32,48,192]{2,1,0:T(8,128)(2,1)S(1)} async-done(((bf16[32,48,192]{2,1,0:T(8,128)(2,1)}), bf16[32,48,192]{2,1,0:T(8,128)(2,1)S(1)}, u32[]{:S(2)}, u32[]{:S(2)}) %all-to-all-start) | async-done | bytes 589856 | tf_op jit(solution)/shard_map/all_to_all | solution.py:363
  31.7 1.1 copy.41
  32.9 2.6 reshape.156
  35.5 39.6 %all_to_all.35 = bf16[8,560,128]{2,1,0:T(8,128)(2,1)} all-to-all(bf16[8,560,128]{2,1,0:T(8,128)(2,1)} %pad_maximum_fusion.1), channel_id=1, replica_groups={{0,16,32,48,64,80,96,112},{8,24,40,56,72,88,104,120},{128,144,160,176,1..., dimensions={0} | all-to-all | bytes 2293760 | tf_op jit(solution)/shard_map/all_to_all | solution.py:390
  75.1 0.0 all-gather.5.cloned.1.call-update
  75.8 0.7 fusion
  76.6 0.3 slice-done.1
  76.8 0.2 broadcast_in_dim.40
  77.0 1.2 pad_maximum_fusion
  78.2 4.9 %all-to-all-start.2 = ((bf16[4,8,176,128]{3,2,1,0:T(8,128)(2,1)}), bf16[4,8,176,128]{3,2,1,0:T(8,128)(2,1)}, u32[]{:S(2)}, u32[]{:S(2)}) async-start(bf16[4,8,176,128]{3,2,1,0:T(8,128)(2,1)} %pad_maximum_fusion), calls=%async_computation.2 | async-start | bytes 2883584 | tf_op jit(solution)/shard_map/all_to_all | solution.py:400
  83.1 3.1 fusion.3
  86.2 2.8 fusion.2.normalized_ref
  89.0 0.9 slice.21
  89.9 11.1 %all-to-all-done.2 = bf16[4,8,176,128]{3,2,1,0:T(8,128)(2,1)} async-done(((bf16[4,8,176,128]{3,2,1,0:T(8,128)(2,1)}), bf16[4,8,176,128]{3,2,1,0:T(8,128)(2,1)}, u32[]{:S(2)}, u32[]{:S(2)}) %all-to-all-start.2) | async-done | bytes 1441824 | tf_op jit(solution)/shard_map/all_to_all | solution.py:400
  101.0 1.0 slice.31
  102.0 1.4 slice.30
  103.4 0.8 copy.43
  104.2 1.3 copy.57
  105.4 4.2 %all-to-all-start.3 = ((bf16[8,288,128]{2,1,0:T(8,128)(2,1)}), bf16[8,288,128]{2,1,0:T(8,128)(2,1)}, u32[]{:S(2)}, u32[]{:S(2)}) async-start(bf16[8,288,128]{2,1,0:T(8,128)(2,1)} %slice.21), calls=%async_computation.3 | async-start | bytes 1179648 | tf_op jit(solution)/shard_map/all_to_all | solution.py:411
  109.6 0.2 all-gather.7.cloned.1.call-start
  109.9 1.3 copy-done.4
  111.2 1.1 copy-done.7
  112.2 1.0 copy-done.8
  113.3 9.9 %attention.1 = bf16[1024,192]{1,0:T(8,128)(2,1)S(1)} custom-call(s32[1]{0:T(128)S(6)} %copy.59.length_ref, bf16[1024,1536]{1,0:T(8,128)(2,1)S(1)} %fusion.2.normalized_ref, bf16[1536,384]{1,0:T(8,128)(2,1)S(1)} %bitcast.77, bf16[1024,128]{1,0:T(8,128)(2,1)S(1)} %bitcast.80, f32[1024,128]{1,0:T(8,128)S(1)} %copy-done.8, f32[1024,128]{1,0:T(8,128)S(1)} %copy-done.7), custom_call_target="tpu_custom_call" | custom-call | flops 12000000000 | bytes 8388608 | tf_op jit(solution)/shard_map/attention/pallas_call | solution.py:114
  123.2 0.8 copy-done.9
  124.0 2.0 copy.45
  126.1 6.3 %all-to-all-start.4 = ((bf16[8,128,192]{1,2,0:T(8,128)(2,1)}), bf16[8,128,192]{1,2,0:T(8,128)(2,1)S(1)}, u32[]{:S(2)}, u32[]{:S(2)}) async-start(bf16[8,128,192]{1,2,0:T(8,128)(2,1)} %copy.45), calls=%async_computation.4 | async-start | bytes 786432 | tf_op jit(solution)/shard_map/all_to_all | solution.py:414
  132.5 1.0 constant_dynamic-slice_fusion.rows_ref
  133.5 6.7 %all-to-all-done.4 = bf16[8,128,192]{1,2,0:T(8,128)(2,1)S(1)} async-done(((bf16[8,128,192]{1,2,0:T(8,128)(2,1)}), bf16[8,128,192]{1,2,0:T(8,128)(2,1)S(1)}, u32[]{:S(2)}, u32[]{:S(2)}) %all-to-all-start.4) | async-done | bytes 393248 | tf_op jit(solution)/shard_map/all_to_all | solution.py:414
  140.2 0.2 copy.47.parts_ref
  140.4 0.0 all-gather.5.cloned.1.call-done
  140.4 6.8 %project_and_dispatch.1 = (f32[128,1536]{1,0:T(8,128)S(1)}, bf16[1536,1536]{1,0:T(8,128)(2,1)}, f32[32,128]{1,0:T(8,128)S(1)}, f32[32,128]{1,0:T(8,128)S(1)}) custom-call(bf16[8,128,192]{2,1,0:T(8,128)(2,1)S(1)} %copy.47.parts_ref, bf16[8,2,96,1536]{3,2,1,0:T(8,128)(2,1)} %bitcast.89, bf16[128,1536]{1,0:T(8,128)(2,1)S(1)} %constant_dynamic-slice_fusion.rows_ref, ...), custom_call_target="tpu_custom_call" | custom-call | flops 1207959552 | bytes 9437184 | tf_op jit(solution)/shard_map/project_and_dispatch/pallas_call | solution.py:202
  147.3 0.9 copy-done.5
  148.2 0.6 copy-done.10
  148.8 0.6 copy-done.11
  149.4 7.6 %all-to-all-start.5 = ((bf16[32,48,1536]{2,1,0:T(8,128)(2,1)}), bf16[32,48,1536]{2,1,0:T(8,128)(2,1)}, u32[]{:S(2)}, u32[]{:S(2)}) async-start(bf16[32,48,1536]{2,1,0:T(8,128)(2,1)} %bitcast.87), calls=%async_computation.5 | async-start | bytes 9437184 | tf_op jit(solution)/shard_map/all_to_all | solution.py:363
  157.0 30.3 %all-gather.7.cloned.1.call-done = bf16[64,288,128]{2,1,0:T(8,128)(2,1)} async-done(((bf16[8,288,128]{2,1,0:T(8,128)(2,1)}), bf16[64,288,128]{2,1,0:T(8,128)(2,1)}) %all-gather.7.cloned.1.call-update) | async-done | bytes 4718608 | tf_op jit(solution)/shard_map/all_gather | solution.py:417
  187.3 2.1 slice.32
  189.4 0.9 copy.48
  190.3 0.8 copy.56
  191.1 1.5 slice_bitcast_fusion
  192.7 1.3 copy.49
  194.0 25.0 %all-to-all-done.5 = bf16[32,48,1536]{2,1,0:T(8,128)(2,1)} async-done(((bf16[32,48,1536]{2,1,0:T(8,128)(2,1)}), bf16[32,48,1536]{2,1,0:T(8,128)(2,1)}, u32[]{:S(2)}, u32[]{:S(2)}) %all-to-all-start.5) | async-done | bytes 4718624 | tf_op jit(solution)/shard_map/all_to_all | solution.py:363
  219.0 1.4 copy-done.3
  220.4 10.5 %experts.1 = bf16[1536,1536]{1,0:T(8,128)(2,1)} custom-call(bf16[1536,1536]{1,0:T(8,128)(2,1)} %bitcast.29.rows_ref, bf16[1536,1024]{1,0:T(8,128)(2,1)S(1)} %bitcast.75, bf16[512,1536]{1,0:T(8,128)(2,1)S(1)} %bitcast.76), custom_call_target="tpu_custom_call" | custom-call | flops 7247757312 | bytes 14155776 | tf_op jit(solution)/shard_map/experts/pallas_call | solution.py:277
  230.9 5.3 %all-to-all-start.6 = ((bf16[32,48,1536]{2,1,0:T(8,128)(2,1)}), bf16[32,48,1536]{2,1,0:T(8,128)(2,1)}, u32[]{:S(2)}, u32[]{:S(2)}) async-start(bf16[32,48,1536]{2,1,0:T(8,128)(2,1)} %bitcast.88), calls=%async_computation.6 | async-start | bytes 9437184 | tf_op jit(solution)/shard_map/all_to_all | solution.py:363
  236.2 1.9 weighing.1.both_ref
  238.1 60.1 %all-to-all-done.6 = bf16[32,48,1536]{2,1,0:T(8,128)(2,1)} async-done(((bf16[32,48,1536]{2,1,0:T(8,128)(2,1)}), bf16[32,48,1536]{2,1,0:T(8,128)(2,1)}, u32[]{:S(2)}, u32[]{:S(2)}) %all-to-all-start.6) | async-done | bytes 4718624 | tf_op jit(solution)/shard_map/all_to_all | solution.py:363
  298.2 1.1 copy-done.2
  299.3 4.1 %combine.1 = bf16[128,1536]{1,0:T(8,128)(2,1)} custom-call(s32[1]{0:T(128)S(6)} %sub.7.live_ref, bf16[256,1536]{1,0:T(8,128)(2,1)S(1)} %copy-done.2, bf16[1536,1536]{1,0:T(8,128)(2,1)} %bitcast.37.returned_ref, f32[128,1536]{1,0:T(8,128)S(1)} %copy-done.6), custom_call_target="tpu_custom_call" | custom-call | flops 1207959552 | bytes 5898240 | tf_op jit(solution)/shard_map/combine/pallas_call | solution.py:319
  (63 shorter events, 0.4 us)
Async XLA Ops:
  6.5 11.0 %copy-start = (bf16[8,16,128]{2,1,0:T(8,128)(2,1)S(1)}, bf16[8,16,128]{2,1,0:T(8,128)(2,1)}, u32[]{:S(2)}) copy-start(bf16[8,16,128]{2,1,0:T(8,128)(2,1)} %param.21) | copy-start | bytes 98308
  6.5 10.5 %copy-start.23 = (s32[32,1,2]{0,2,1:T(2,128)S(1)}, s32[32,1,2]{0,2,1:T(2,128)}, u32[]{:S(2)}) copy-start(s32[32,1,2]{0,2,1:T(2,128)} %param.22) | copy-start | bytes 772
  6.5 10.5 %copy-start.19 = (f32[48,64]{1,0:T(8,128)S(1)}, f32[48,64]{1,0:T(8,128)}, u32[]{:S(2)}) copy-start(f32[48,64]{1,0:T(8,128)} %param.18) | copy-start | bytes 36868
  6.5 10.5 %copy-start.20 = (f32[48,64]{1,0:T(8,128)S(1)}, f32[48,64]{1,0:T(8,128)}, u32[]{:S(2)}) copy-start(f32[48,64]{1,0:T(8,128)} %param.19) | copy-start | bytes 36868
  6.5 10.7 %copy-start.18 = (f32[48,192]{1,0:T(8,128)S(1)}, f32[48,192]{1,0:T(8,128)}, u32[]{:S(2)}) copy-start(f32[48,192]{1,0:T(8,128)} %param.17) | copy-start | bytes 110596
  6.5 11.7 %copy-start.15 = (f32[1,192,1024]{2,1,0:T(8,128)S(1)}, f32[1,192,1024]{2,1,0:T(8,128)}, u32[]{:S(2)}) copy-start(f32[1,192,1024]{2,1,0:T(8,128)} %param.26) | copy-start | bytes 2359300
  8.4 23.4 %all-to-all-start = ((bf16[32,48,192]{2,1,0:T(8,128)(2,1)}), bf16[32,48,192]{2,1,0:T(8,128)(2,1)S(1)}, u32[]{:S(2)}, u32[]{:S(2)}) async-start(bf16[32,48,192]{2,1,0:T(8,128)(2,1)} %broadcast_in_dim.21), calls=%async_computation | async-start | bytes 1572864 | tf_op jit(solution)/shard_map/all_to_all | solution.py:363
  17.0 123.5 %all-gather.5.cloned.1.call-start = ((), (), s32[]{:S(2)}) async-start(), calls=%async_computation.7 | async-start | bytes 5308416 | tf_op jit(solution)/shard_map/all_gather | solution.py:392
  17.5 1.0 copy-start.16
  32.9 43.0 %copy-start.13 = (bf16[1024,1536]{1,0:T(8,128)(2,1)S(1)}, bf16[1024,1536]{1,0:T(8,128)(2,1)}, u32[]{:S(2)}) copy-start(bf16[1024,1536]{1,0:T(8,128)(2,1)} %param.14) | copy-start | bytes 9437188
  75.1 1.4 slice-start
  75.8 1.0 slice-start.1
  78.2 8.0 %copy-start.21 = (f32[1536]{0:T(1024)S(1)}, f32[1536]{0:T(1024)}, u32[]{:S(2)}) copy-start(f32[1536]{0:T(1024)} %param.16) | copy-start | bytes 18436
  78.2 22.8 %all-to-all-start.2 = ((bf16[4,8,176,128]{3,2,1,0:T(8,128)(2,1)}), bf16[4,8,176,128]{3,2,1,0:T(8,128)(2,1)}, u32[]{:S(2)}, u32[]{:S(2)}) async-start(bf16[4,8,176,128]{3,2,1,0:T(8,128)(2,1)} %pad_maximum_fusion), calls=%async_computation.2 | async-start | bytes 2883584 | tf_op jit(solution)/shard_map/all_to_all | solution.py:400
  86.2 2.8 copy-start.14
  105.4 18.6 %all-to-all-start.3 = ((bf16[8,288,128]{2,1,0:T(8,128)(2,1)}), bf16[8,288,128]{2,1,0:T(8,128)(2,1)}, u32[]{:S(2)}, u32[]{:S(2)}) async-start(bf16[8,288,128]{2,1,0:T(8,128)(2,1)} %slice.21), calls=%async_computation.3 | async-start | bytes 1179648 | tf_op jit(solution)/shard_map/all_to_all | solution.py:411
  109.6 77.6 %all-gather.7.cloned.1.call-start = ((), (), s32[]{:S(2)}) async-start(), calls=%async_computation.8 | async-start | bytes 5308416 | tf_op jit(solution)/shard_map/all_gather | solution.py:417
  109.9 1.3 copy-start.4
  111.2 1.1 copy-start.7
  112.2 1.0 copy-start.8
  123.2 0.8 copy-start.9
  124.0 8.4 %copy-start.22 = (f32[1536]{0:T(1024)S(1)}, f32[1536]{0:T(1024)}, u32[]{:S(2)}) copy-start(f32[1536]{0:T(1024)} %param.23) | copy-start | bytes 18436
  124.0 8.4 %copy-start.17 = (bf16[1536,32]{0,1:T(8,128)(2,1)S(1)}, bf16[1536,32]{0,1:T(8,128)(2,1)}, u32[]{:S(2)}) copy-start(bf16[1536,32]{0,1:T(8,128)(2,1)} %param.24) | copy-start | bytes 294916
  124.0 16.4 %copy-start.12 = (s32[128,8]{0,1:T(8,128)S(1)}, s32[128,8]{0,1:T(8,128)}, u32[]{:S(2)}) copy-start(s32[128,8]{0,1:T(8,128)} %param.25) | copy-start | bytes 12292
  126.1 14.1 %all-to-all-start.4 = ((bf16[8,128,192]{1,2,0:T(8,128)(2,1)}), bf16[8,128,192]{1,2,0:T(8,128)(2,1)S(1)}, u32[]{:S(2)}, u32[]{:S(2)}) async-start(bf16[8,128,192]{1,2,0:T(8,128)(2,1)} %copy.45), calls=%async_computation.4 | async-start | bytes 786432 | tf_op jit(solution)/shard_map/all_to_all | solution.py:414
  147.3 0.9 copy-start.5
  148.2 0.6 copy-start.10
  148.8 0.6 copy-start.11
  149.4 69.6 %all-to-all-start.5 = ((bf16[32,48,1536]{2,1,0:T(8,128)(2,1)}), bf16[32,48,1536]{2,1,0:T(8,128)(2,1)}, u32[]{:S(2)}, u32[]{:S(2)}) async-start(bf16[32,48,1536]{2,1,0:T(8,128)(2,1)} %bitcast.87), calls=%async_computation.5 | async-start | bytes 9437184 | tf_op jit(solution)/shard_map/all_to_all | solution.py:363
  219.0 1.4 copy-start.3
  230.9 67.3 %copy-start.6 = (f32[128,1536]{1,0:T(8,128)S(1)}, f32[128,1536]{1,0:T(8,128)}, u32[]{:S(2)}) copy-start(f32[128,1536]{1,0:T(8,128)} %copy-done.5) | copy-start | bytes 2359300
  230.9 67.3 %all-to-all-start.6 = ((bf16[32,48,1536]{2,1,0:T(8,128)(2,1)}), bf16[32,48,1536]{2,1,0:T(8,128)(2,1)}, u32[]{:S(2)}, u32[]{:S(2)}) async-start(bf16[32,48,1536]{2,1,0:T(8,128)(2,1)} %bitcast.88), calls=%async_computation.6 | async-start | bytes 9437184 | tf_op jit(solution)/shard_map/all_to_all | solution.py:363
  298.2 5.3 %copy-start.1 = (bf16[8,16,128]{2,1,0:T(8,128)(2,1)S(1)}, bf16[8,16,128]{2,1,0:T(8,128)(2,1)}, u32[]{:S(2)}) copy-start(bf16[8,16,128]{2,1,0:T(8,128)(2,1)} %param.21) | copy-start | bytes 98308
  298.2 1.1 copy-start.2
Sparse Core Ops, SparseCore 0:
  75.2 51.8 all-gather.4
  128.9 58.3 all-gather.6

commit v6 on v5

--- a/solution.py
+++ b/solution.py
@@ -28,33 +28,45 @@
     return values * lax.rsqrt(mean_square + epsilon) * norm_gain
 
 
-def rotary_tables(positions, first_position):
+def rotary_table(positions, first_position):
     lane = jnp.arange(2 * HEAD_WIDTH)
     frequency = jnp.exp(
         (lane % (HEAD_WIDTH // 2)).astype(jnp.float32) * (-2.0 * math.log(10000.0) / HEAD_WIDTH)
     )
     angles = (first_position + jnp.arange(positions)).astype(jnp.float32)[:, None] * frequency
     sign = jnp.where(lane % HEAD_WIDTH < HEAD_WIDTH // 2, -1.0, 1.0)
-    return jnp.cos(angles), jnp.sin(angles) * sign
+    return jnp.where(lane < HEAD_WIDTH, jnp.cos(angles), jnp.sin(angles) * sign)
 
 
 def attention_body(
-    length_ref, normalized_ref, weight_ref, pages_ref, cosine_ref, sine_ref,
-    out_ref, queries, keys, values,
+    length_ref, normalized_ref, across_ref, table_ref,
+    out_ref, queries, keys, values, weight,
 ):
     seq_len = normalized_ref.shape[0]
-    prefix = pages_ref.shape[0]
     heads = queries.shape[0]
+    prefix = keys.shape[1] - seq_len
     chunk = 256
     lane = lax.broadcasted_iota(jnp.int32, (chunk, 256), 1)
     ones = jnp.ones((chunk, HEAD_WIDTH), jnp.bfloat16)
+    for e in range(32):
+        pair, z = (e // 16) * 2 + e % 2, (e // 2) % 8
+        for j in range(3):
+            weight[e * 48 : (e + 1) * 48, j * 128 : (j + 1) * 128] = across_ref[
+                pair, z, j * 48 : (j + 1) * 48, :
+            ]
     for c in range(0, prefix, chunk):
-        rows = pages_ref[c : c + chunk, :]
+        rows = jnp.concatenate(
+            [
+                across_ref[(e // 16) * 2 + e % 2, (e // 2) % 8, 144:176, :]
+                for e in range(c // 32, (c + chunk) // 32)
+            ],
+            axis=0,
+        )
         keys[:, c : c + chunk] = rows.astype(jnp.float32).T[:HEAD_WIDTH].astype(jnp.bfloat16)
         values[c : c + chunk, :] = jnp.concatenate([rows[:, HEAD_WIDTH:], ones], axis=1)
     for c in range(0, seq_len, chunk):
         projected = jnp.dot(
-            normalized_ref[c : c + chunk, :], weight_ref[...], preferred_element_type=jnp.float32
+            normalized_ref[c : c + chunk, :], weight[...], preferred_element_type=jnp.float32
         )
         plain = projected[:, :256]
         partner = jnp.where(
@@ -62,10 +74,10 @@
             pltpu.roll(plain, 256 - HEAD_WIDTH // 2, 1),
             pltpu.roll(plain, HEAD_WIDTH // 2, 1),
         )
-        cosine = cosine_ref[c : c + chunk, :]
-        sine = sine_ref[c : c + chunk, :]
-        rotated = plain * jnp.concatenate([cosine, cosine], axis=1) + partner * jnp.concatenate(
-            [sine, sine], axis=1
+        cosine = table_ref[c : c + chunk, :HEAD_WIDTH]
+        sine = table_ref[c : c + chunk, HEAD_WIDTH:]
+        rotated = plain * jnp.concatenate([cosine] * 4, axis=1) + partner * jnp.concatenate(
+            [sine] * 4, axis=1
         )
         rounded = rotated.astype(jnp.bfloat16)
         for h in range(heads):
@@ -103,36 +115,80 @@
                 preferred_element_type=jnp.float32,
             )
             outs.append(total[:, :HEAD_WIDTH] / total[:, HEAD_WIDTH : HEAD_WIDTH + 1])
-        out_ref[start:seen, :] = jnp.concatenate(outs, axis=1).astype(jnp.bfloat16)
-
-
-def attention(lengths, normalized, weight, pages, cosine, sine):
+        for t in range(0, chunk, 128):
+            block = (start + t) // 128
+            low, high = outs[2][t : t + 64], outs[2][t + 64 : t + 128]
+            out_ref[block, :128, :] = jnp.concatenate(
+                [outs[0][t : t + 128], outs[1][t : t + 128]], axis=1
+            ).astype(jnp.bfloat16)
+            out_ref[block, 128:, :] = jnp.concatenate([low, high], axis=1).astype(jnp.bfloat16)
+
+
+def attention(lengths, normalized, across, table):
     seq_len, model_width = normalized.shape
     heads = 3
-    total = seq_len + pages.shape[0]
+    total = 2 * seq_len
     vmem = pl.BlockSpec(memory_space=pltpu.VMEM)
     return pl.pallas_call(
         attention_body,
-        out_shape=jax.ShapeDtypeStruct((seq_len, heads * HEAD_WIDTH), jnp.bfloat16),
-        in_specs=[pl.BlockSpec(memory_space=pltpu.SMEM)] + [vmem] * 5,
+        out_shape=pltpu.HBM((seq_len // 128, 192, 128), jnp.bfloat16),
+        in_specs=[pl.BlockSpec(memory_space=pltpu.SMEM)] + [vmem] * 3,
         out_specs=vmem,
         scratch_shapes=[
             pltpu.VMEM((heads, seq_len, HEAD_WIDTH), jnp.bfloat16),
             pltpu.VMEM((HEAD_WIDTH, total), jnp.bfloat16),
             pltpu.VMEM((total, 2 * HEAD_WIDTH), jnp.bfloat16),
+            pltpu.VMEM((model_width, 384), jnp.bfloat16),
         ],
         compiler_params=pltpu.CompilerParams(vmem_limit_bytes=48 << 20),
         cost_estimate=pl.CostEstimate(
             flops=12_000_000_000, bytes_accessed=8 << 20, transcendentals=heads * seq_len * total
         ),
         name="attention",
-    )(lengths, normalized, weight, pages, cosine, sine)
+    )(lengths, normalized, across, table)
+
+
+def relay_body(along_ref, payload_ref, expert_ref, sem):
+    copies = [pltpu.make_async_copy(along_ref.at[:, 272:], expert_ref, sem.at[8])]
+    for d in range(4):
+        copies.append(
+            pltpu.make_async_copy(
+                along_ref.at[:, :144], payload_ref.at[d, :, pl.ds(0, 144)], sem.at[2 * d]
+            )
+        )
+        copies.append(
+            pltpu.make_async_copy(
+                along_ref.at[:, pl.ds(144 + 32 * d, 32)],
+                payload_ref.at[d, :, pl.ds(144, 32)],
+                sem.at[2 * d + 1],
+            )
+        )
+    for copy in copies:
+        copy.start()
+    for copy in copies:
+        copy.wait()
+
+
+def relay(along_z):
+    hbm = pl.BlockSpec(memory_space=pltpu.HBM)
+    return pl.pallas_call(
+        relay_body,
+        out_shape=(
+            pltpu.HBM((4, 8, 176, 128), jnp.bfloat16),
+            pltpu.HBM((8, 288, 128), jnp.bfloat16),
+        ),
+        in_specs=[hbm],
+        out_specs=(hbm, hbm),
+        scratch_shapes=[pltpu.SemaphoreType.DMA((9,))],
+        cost_estimate=pl.CostEstimate(flops=0, bytes_accessed=4 << 20, transcendentals=0),
+        name="relay",
+    )(pltpu.with_memory_space_constraint(along_z, pltpu.HBM))
 
 
 def project_body(
     parts_ref, weight_hbm, rows_ref, gain_ref, router_ref, ids_ref,
-    hidden_ref, send_ref, rank_ref, gates_ref,
-    weight, attended, place, staged, sem, out_sem,
+    hidden_out, send_ref, rank_gates_out,
+    weight, attended, place, staged, hidden_ref, rank_gates, sem, out_sem,
 ):
     copies = []
     for z in range(8):
@@ -143,7 +199,10 @@
             copy.start()
             copies.append(copy)
     for t in range(8):
-        attended[:, t * 192 : (t + 1) * 192] = parts_ref[t]
+        at = t * 192
+        attended[:, at : at + 128] = parts_ref[t, :128, :]
+        attended[:64, at + 128 : at + 192] = parts_ref[t, 128:, :64]
+        attended[64:, at + 128 : at + 192] = parts_ref[t, 128:, 64:]
     tokens = rows_ref.shape[0]
     host = lax.broadcasted_iota(jnp.int32, (EXPERTS, tokens), 0)
     expert_at = (host // 16) * 16 + (host % 8) * 2 + (host // 8) % 2
@@ -159,7 +218,7 @@
         preferred_element_type=jnp.float32,
     )
     rank = jnp.where(chosen > 0.0, rank, -1.0)
-    rank_ref[...] = rank
+    rank_gates[:EXPERTS, :] = rank
     slot = lax.broadcasted_iota(jnp.int32, (CAPACITY, tokens), 0).astype(jnp.float32)
     for g in range(EXPERTS):
         place[g * CAPACITY : (g + 1) * CAPACITY, :] = jnp.where(
@@ -174,6 +233,8 @@
             (((1,), (1,)), ((), ())),
             preferred_element_type=jnp.float32,
         )
+    keep = pltpu.make_async_copy(hidden_ref, hidden_out, out_sem.at[6])
+    keep.start()
     hidden = hidden_ref[...]
     moe_in = rms_scale(hidden, gain_ref[...]).astype(jnp.bfloat16)
     for c in range(0, EXPERTS * CAPACITY, 256):
@@ -188,11 +249,15 @@
     )
     top_logit = jnp.max(jnp.where(chosen > 0.0, logits, -3e38), axis=0, keepdims=True)
     raised = jnp.where(chosen > 0.0, jnp.exp(jnp.minimum(logits - top_logit, 0.0)), 0.0)
-    gates_ref[...] = raised / jnp.sum(raised, axis=0, keepdims=True)
+    rank_gates[EXPERTS:, :] = raised / jnp.sum(raised, axis=0, keepdims=True)
+    last = pltpu.make_async_copy(rank_gates, rank_gates_out, out_sem.at[7])
+    last.start()
     for c in range(0, EXPERTS * CAPACITY, 256):
         pltpu.make_async_copy(
             staged.at[pl.ds(c, 256)], send_ref.at[pl.ds(c, 256)], out_sem.at[c // 256]
         ).wait()
+    keep.wait()
+    last.wait()
 
 
 def project_and_dispatch(parts, output_weight, own_rows, moe_gain, router_hosted, ids_by_choice):
@@ -202,20 +267,21 @@
     return pl.pallas_call(
         project_body,
         out_shape=(
-            jax.ShapeDtypeStruct((row_count, model_width), jnp.float32),
+            pltpu.HBM((row_count, model_width), jnp.float32),
             pltpu.HBM((slots, model_width), jnp.bfloat16),
-            jax.ShapeDtypeStruct((EXPERTS, row_count), jnp.float32),
-            jax.ShapeDtypeStruct((EXPERTS, row_count), jnp.float32),
+            pltpu.HBM((2 * EXPERTS, row_count), jnp.float32),
         ),
         in_specs=[vmem, pl.BlockSpec(memory_space=pltpu.HBM), vmem, vmem, vmem, vmem],
-        out_specs=(vmem, pl.BlockSpec(memory_space=pltpu.HBM), vmem, vmem),
+        out_specs=(pl.BlockSpec(memory_space=pltpu.HBM),) * 3,
         scratch_shapes=[
             pltpu.VMEM((model_width, model_width), jnp.bfloat16),
             pltpu.VMEM((row_count, model_width), jnp.bfloat16),
             pltpu.VMEM((slots, row_count), jnp.bfloat16),
             pltpu.VMEM((slots, model_width), jnp.bfloat16),
+            pltpu.VMEM((row_count, model_width), jnp.float32),
+            pltpu.VMEM((2 * EXPERTS, row_count), jnp.float32),
             pltpu.SemaphoreType.DMA((16,)),
-            pltpu.SemaphoreType.DMA((6,)),
+            pltpu.SemaphoreType.DMA((8,)),
         ],
         compiler_params=pltpu.CompilerParams(vmem_limit_bytes=40 << 20),
         cost_estimate=pl.CostEstimate(
@@ -234,12 +300,14 @@
     )
 
 
-def weigh_body(rank_ref, gates_ref, both_ref, weigh):
-    tokens = rank_ref.shape[1]
+def weigh_body(rank_gates_ref, both_ref, weigh):
+    tokens = rank_gates_ref.shape[1]
     slot = lax.broadcasted_iota(jnp.int32, (CAPACITY, tokens), 0).astype(jnp.float32)
     for g in range(EXPERTS):
         weigh[g * CAPACITY : (g + 1) * CAPACITY, :] = jnp.where(
-            rank_ref[g : g + 1, :] == slot, gates_ref[g : g + 1, :], 0.0
+            rank_gates_ref[g : g + 1, :] == slot,
+            rank_gates_ref[EXPERTS + g : EXPERTS + g + 1, :],
+            0.0,
         )
     for c in range(0, EXPERTS * CAPACITY, 128):
         by_token = weigh[c : c + 128, :].T
@@ -248,19 +316,19 @@
         both_ref[tokens:, c : c + 128] = (by_token - high.astype(jnp.float32)).astype(jnp.bfloat16)
 
 
-def weighing(rank, gates):
-    row_count = rank.shape[1]
+def weighing(rank_gates):
+    row_count = rank_gates.shape[1]
     slots = EXPERTS * CAPACITY
     vmem = pl.BlockSpec(memory_space=pltpu.VMEM)
     return pl.pallas_call(
         weigh_body,
         out_shape=jax.ShapeDtypeStruct((2 * row_count, slots), jnp.bfloat16),
-        in_specs=[vmem, vmem],
+        in_specs=[vmem],
         out_specs=vmem,
         scratch_shapes=[pltpu.VMEM((slots, row_count), jnp.float32)],
         cost_estimate=pl.CostEstimate(flops=1 << 20, bytes_accessed=1 << 20, transcendentals=0),
         name="weighing",
-    )(rank, gates)
+    )(rank_gates)
 
 
 def expert_body(rows_ref, gate_up_ref, down_ref, out_ref):
@@ -366,9 +434,6 @@
 
     output_shard = o_proj.T.astype(jnp.bfloat16)
     output_plane = in_plane(jnp.broadcast_to(output_shard[None], (EXPERTS, *output_shard.shape)))
-    output_plane = (
-        output_plane.reshape(4, 8, 48, 192).transpose(0, 2, 1, 3).reshape(192, model_width)
-    )
 
     weight_shard = jnp.concatenate(
         [q_proj, k_proj, value_projection, jnp.zeros_like(k_proj)], axis=1
@@ -386,38 +451,26 @@
         ],
         axis=1,
     )
-    payload, output_plane = barrier((payload, output_plane))
+    normalized = rms_scale(tokens_in.astype(jnp.float32), attn_gain).astype(jnp.bfloat16)
+    payload, output_plane, normalized = barrier((payload, output_plane, normalized))
     along_z = lax.all_to_all(payload, "ep", 0, 0, axis_index_groups=Z_GROUPS, tiled=True)
+    output_plane = (
+        output_plane.reshape(4, 8, 48, 192).transpose(0, 2, 1, 3).reshape(192, model_width)
+    )
     output_plane, along_z = barrier((output_plane, along_z))
     output_weight = lax.all_gather(output_plane, "ep", axis_index_groups=Z_GROUPS)
-    payload = jnp.concatenate(
-        [
-            jnp.broadcast_to(along_z[None, :, :144], (4, 8, 144, 128)),
-            along_z[:, 144:272].reshape(8, 4, 32, 128).transpose(1, 0, 2, 3),
-        ],
-        axis=2,
-    )
+    payload, by_expert = relay(along_z)
     across = lax.all_to_all(payload, "ep", 0, 0, axis_index_groups=CHIP_PAIR_GROUPS, tiled=True)
-    weight = (
-        across[:, :, :144]
-        .reshape(2, 2, 8, 3, 48, 128)
-        .transpose(0, 2, 1, 4, 3, 5)
-        .reshape(model_width, 384)
-    )
-    prefix = across[:, :, 144:].reshape(2, 2, 8, 32, 128).transpose(0, 2, 1, 3, 4).reshape(-1, 128)
-    cosine, sine = rotary_tables(seq_len, prefix.shape[0])
-    normalized = rms_scale(tokens_in.astype(jnp.float32), attn_gain).astype(jnp.bfloat16)
-    by_expert, weight, prefix = barrier((along_z[:, 272:], weight, prefix))
+    table = rotary_table(seq_len, 32 * 32)
+    by_expert, across = barrier((by_expert, across))
     hosted = lax.all_to_all(by_expert, "tp", 0, 0, tiled=True)
-    attended = attention(lengths, normalized, weight, prefix, cosine, sine)
+    attended = attention(lengths, normalized, across, table)
     attended, hosted = barrier((attended, hosted))
-    attn_parts = lax.all_to_all(
-        attended.reshape(8, row_count, attended.shape[1]), "tp", 0, 0, tiled=True
-    )
+    attn_parts = lax.all_to_all(attended, "tp", 0, 0, tiled=True)
     planes = lax.all_gather(hosted, "ep", axis_index_groups=Z_GROUPS)
     own_rows = lax.dynamic_slice_in_dim(tokens_in, tp_index * row_count, row_count, 0)
     router_hosted = router.T.reshape(2, 8, 2, model_width).transpose(0, 2, 1, 3)
-    hidden, send_rows, rank, gates = project_and_dispatch(
+    hidden, send_rows, rank_gates = project_and_dispatch(
         attn_parts,
         output_weight,
         own_rows,
@@ -432,7 +485,7 @@
         planes[:, :, 192:].reshape(8, 8, 12, 8, 128).transpose(1, 0, 3, 2, 4).reshape(FF, model_width)
     )
     received = in_plane(send_rows.reshape(EXPERTS, CAPACITY, model_width))
-    both = weighing(rank, gates)
+    both = weighing(rank_gates)
     expert_out = experts(received.reshape(-1, model_width), gate_up_full, down_full)
     returned = in_plane(expert_out.reshape(EXPERTS, CAPACITY, model_width))
     live = lengths - tp_index * row_count

time: 311 us -> 358 us (1.15)
  Pallas kernels: 33.3 us -> 98.4 us
  blocking collectives: 39.6 us -> 0 us
  waiting for transfers between devices: 145 us -> 170 us
  local copies, waits for them, and re-layouts: 30.5 us -> 19.1 us
  starting transfers between devices: 37.1 us -> 45.4 us
    pallas_call x2 -> x3, Pallas kernels: 16.8 us -> 81.8 us  [the longest x1 62.7 us: relay(): pl.pallas_call(relay_body, out_shape=(pltpu.HBM((4, 8, 176, 128), jnp.bfl...]
    all_to_all x1 -> x0, blocking collectives: 39.6 us -> none  [on_device(): lax.all_to_all(payload, 'ep', 0, 0, axis_index_groups=Z_GROUPS, tiled=True)]
    all_to_all x1 -> x2, waiting for transfers between devices: 6.69 us -> 33.4 us  [the longest x1 26.7 us: on_device(): lax.all_to_all(payload, 'ep', 0, 0, axis_index_groups=Z_GROUPS, tiled=True)]
    all_to_all x1 -> x2, starting transfers between devices: 6.31 us -> 14.5 us  [the longest x1 8.19 us: on_device(): lax.all_to_all(payload, 'ep', 0, 0, axis_index_groups=Z_GROUPS, tiled=True)]
    unnamed x51 -> x32, local copies, waits for them, and re-layouts: 11.1 us -> 5.42 us
  transfers between devices with their start and end apart: 8 -> 9, of which waited for: 6 -> 7; matrix products, arithmetic and copies ran while one was open for 8% -> 6% of each run, Pallas kernels for 6% -> 23%
where the time goes in v6:
time: 358 us; the launch traced here: 357 us
  waiting for transfers between devices  170 us (47%)
  Pallas kernels  98.4 us (27%)
  starting transfers between devices  45.4 us (13%)
  local copies, waits for them, and re-layouts  19.1 us (5%)
  between operations  14.4 us (4%)
  other arithmetic  9.2 us (3%)
    all_to_all x3, waiting for transfers between devices, in_plane(): lax.all_to_all(rows, ('ep', 'tp'), 0, 0, axis_index_groups=PLANE_GROUPS,...  94.9 us
    pallas_call x1, Pallas kernels, relay(): pl.pallas_call(relay_body, out_shape=(pltpu.HBM((4, 8, 176, 128), jnp.bfl...  62.7 us
    all_gather x1, waiting for transfers between devices, on_device(): planes = lax.all_gather(hosted, 'ep', axis_index_groups=Z_GROUPS)  27.7 us
    all_to_all x1, waiting for transfers between devices, on_device(): lax.all_to_all(payload, 'ep', 0, 0, axis_index_groups=Z_GROUPS, tiled=True)  26.7 us
    all_to_all x3, starting transfers between devices, in_plane(): lax.all_to_all(rows, ('ep', 'tp'), 0, 0, axis_index_groups=PLANE_GROUPS,...  21.7 us
    all_to_all x1, waiting for transfers between devices, on_device(): lax.all_to_all(payload, 'ep', 0, 0, axis_index_groups=CHIP_PAIR_GROUPS, t...  14.2 us
    pallas_call x1, Pallas kernels, attention(): pl.pallas_call(attention_body, out_shape=pltpu.HBM((seq_len // 128, 192,...  12.2 us
    pallas_call x1, Pallas kernels, experts(): pl.pallas_call(expert_body, out_shape=pltpu.HBM((count, model_width), jnp...  10.5 us
  transfers between devices with their start and end apart: 9, of which 7 were waited for; matrix products, arithmetic and copies ran while one was open for 6% of the time, Pallas kernels for 23%

profile of v6, /device:TPU:1, one launch (start us, length us, event | category | flops | bytes accessed | tf_op | source)
XLA Modules:
  0.0 356.7 jit_solution(1490010674582704809)
XLA Ops:
  6.5 0.0 copy-start
  6.5 0.9 convert_bitcast_fusion.2
  7.4 0.9 broadcast_in_dim.37
  8.3 8.8 %all-to-all-start = ((bf16[32,48,192]{2,1,0:T(8,128)(2,1)}), bf16[32,48,192]{2,1,0:T(8,128)(2,1)}, u32[]{:S(2)}, u32[]{:S(2)}) async-start(bf16[32,48,192]{2,1,0:T(8,128)(2,1)} %broadcast_in_dim.37), calls=%async_computation | async-start | bytes 1572864 | tf_op jit(solution)/shard_map/all_to_all | solution.py:431
  17.1 0.7 compare_select_fusion
  17.8 2.6 fusion
  20.4 0.0 copy-done.11
  20.4 0.0 copy-done.12
  20.4 0.1 copy.36
  20.5 0.1 reshape.152
  20.6 0.0 copy-done.10
  20.7 0.1 pad.7.clone
  20.7 0.1 maximum_maximum_fusion
  20.9 0.0 copy-done.8
  20.9 0.0 copy-done
  20.9 0.0 copy-start.13
  20.9 0.6 gather_fusion
  21.6 0.0 copy-start.6
  21.6 0.0 copy-done.7
  21.6 0.1 convert_bitcast_fusion
  21.7 0.1 copy.43
  21.8 0.1 copy.38
  21.9 1.1 pad_maximum_fusion
  23.0 0.0 copy-done.13
  23.0 0.9 copy-done.6
  23.9 0.8 fusion.2.normalized_ref
  24.7 7.3 %all-to-all-done = bf16[32,48,192]{2,1,0:T(8,128)(2,1)} async-done(((bf16[32,48,192]{2,1,0:T(8,128)(2,1)}), bf16[32,48,192]{2,1,0:T(8,128)(2,1)}, u32[]{:S(2)}, u32[]{:S(2)}) %all-to-all-start) | async-done | bytes 589856 | tf_op jit(solution)/shard_map/all_to_all | solution.py:431
  31.9 8.2 %all-to-all-start.1 = ((bf16[8,560,128]{2,1,0:T(8,128)(2,1)}), bf16[8,560,128]{2,1,0:T(8,128)(2,1)}, u32[]{:S(2)}, u32[]{:S(2)}) async-start(bf16[8,560,128]{2,1,0:T(8,128)(2,1)} %pad_maximum_fusion), calls=%async_computation.1 | async-start | bytes 2293760 | tf_op jit(solution)/shard_map/all_to_all | solution.py:456
  40.1 0.0 all-gather.5.cloned.1.call-start
  40.2 2.3 copy.39
  42.4 2.4 reshape.137
  44.9 26.7 %all-to-all-done.1.along_ref = bf16[8,560,128]{2,1,0:T(8,128)(2,1)} async-done(((bf16[8,560,128]{2,1,0:T(8,128)(2,1)}), bf16[8,560,128]{2,1,0:T(8,128)(2,1)}, u32[]{:S(2)}, u32[]{:S(2)}) %all-to-all-start.1) | async-done | bytes 1146912 | tf_op jit(solution)/shard_map/all_to_all | solution.py:456
  71.6 0.0 all-gather.5.cloned.1.call-update
  71.6 62.7 %relay.1 = (bf16[4,8,176,128]{3,2,1,0:T(8,128)(2,1)}, bf16[8,288,128]{2,1,0:T(8,128)(2,1)}) custom-call(bf16[8,560,128]{2,1,0:T(8,128)(2,1)} %all-to-all-done.1.along_ref), custom_call_target="tpu_custom_call" | custom-call | bytes 4194304 | tf_op jit(solution)/shard_map/relay/pallas_call | solution.py:174
  134.4 4.8 %all-to-all-start.2 = ((bf16[4,8,176,128]{3,2,1,0:T(8,128)(2,1)}), bf16[4,8,176,128]{3,2,1,0:T(8,128)(2,1)}, u32[]{:S(2)}, u32[]{:S(2)}) async-start(bf16[4,8,176,128]{3,2,1,0:T(8,128)(2,1)} %get-tuple-element.24), calls=%async_computation.2 | async-start | bytes 2883584 | tf_op jit(solution)/shard_map/all_to_all | solution.py:463
  139.8 3.0 fusion.3.table_ref
  142.8 14.2 %all-to-all-done.2.across_ref = bf16[4,8,176,128]{3,2,1,0:T(8,128)(2,1)} async-done(((bf16[4,8,176,128]{3,2,1,0:T(8,128)(2,1)}), bf16[4,8,176,128]{3,2,1,0:T(8,128)(2,1)}, u32[]{:S(2)}, u32[]{:S(2)}) %all-to-all-start.2) | async-done | bytes 1441824 | tf_op jit(solution)/shard_map/all_to_all | solution.py:463
  157.0 4.2 %all-to-all-start.3 = ((bf16[8,288,128]{2,1,0:T(8,128)(2,1)}), bf16[8,288,128]{2,1,0:T(8,128)(2,1)}, u32[]{:S(2)}, u32[]{:S(2)}) async-start(bf16[8,288,128]{2,1,0:T(8,128)(2,1)} %get-tuple-element.26), calls=%async_computation.3 | async-start | bytes 1179648 | tf_op jit(solution)/shard_map/all_to_all | solution.py:466
  161.3 0.2 all-gather.7.cloned.1.call-start
  161.5 0.0 copy-start.4
  161.5 1.0 copy-done.4
  162.5 12.2 %attention.1 = bf16[8,192,128]{2,1,0:T(8,128)(2,1)} custom-call(s32[1]{0:T(128)S(6)} %copy.47.length_ref, bf16[1024,1536]{1,0:T(8,128)(2,1)S(1)} %fusion.2.normalized_ref, bf16[4,8,176,128]{3,2,1,0:T(8,128)(2,1)} %all-to-all-done.2.across_ref, f32[1024,128]{1,0:T(8,128)S(1)} %copy-done.4), custom_call_target="tpu_custom_call" | custom-call | flops 12000000000 | bytes 8388608 | tf_op jit(solution)/shard_map/attention/pallas_call | solution.py:132
  174.7 0.0 all-to-all-done.3
  174.7 0.0 all-gather.7.cloned.1.call-update
  174.7 6.3 %all-to-all-start.4 = ((bf16[8,192,128]{2,1,0:T(8,128)(2,1)}), bf16[8,192,128]{2,1,0:T(8,128)(2,1)S(1)}, u32[]{:S(2)}, u32[]{:S(2)}) async-start(bf16[8,192,128]{2,1,0:T(8,128)(2,1)} %attention.1), calls=%async_computation.4 | async-start | bytes 786432 | tf_op jit(solution)/shard_map/all_to_all | solution.py:469
  181.1 0.0 copy-done.9
  181.2 1.0 constant_dynamic-slice_fusion.rows_ref
  182.2 6.7 %all-to-all-done.4.parts_ref = bf16[8,192,128]{2,1,0:T(8,128)(2,1)S(1)} async-done(((bf16[8,192,128]{2,1,0:T(8,128)(2,1)}), bf16[8,192,128]{2,1,0:T(8,128)(2,1)S(1)}, u32[]{:S(2)}, u32[]{:S(2)}) %all-to-all-start.4) | async-done | bytes 393248 | tf_op jit(solution)/shard_map/all_to_all | solution.py:469
  188.9 6.9 %project_and_dispatch.1 = (f32[128,1536]{1,0:T(8,128)}, bf16[1536,1536]{1,0:T(8,128)(2,1)}, f32[64,128]{1,0:T(8,128)}) custom-call(bf16[8,192,128]{2,1,0:T(8,128)(2,1)S(1)} %all-to-all-done.4.parts_ref, bf16[8,2,96,1536]{3,2,1,0:T(8,128)(2,1)} %bitcast.64, bf16[128,1536]{1,0:T(8,128)(2,1)S(1)} %constant_dynamic-slice_fusion.rows_ref, ...), custom_call_target="tpu_custom_call" | custom-call | flops 1207959552 | bytes 9437184 | tf_op jit(solution)/shard_map/project_and_dispatch/pallas_call | solution.py:267
  195.8 7.6 %all-to-all-start.5 = ((bf16[32,48,1536]{2,1,0:T(8,128)(2,1)}), bf16[32,48,1536]{2,1,0:T(8,128)(2,1)}, u32[]{:S(2)}, u32[]{:S(2)}) async-start(bf16[32,48,1536]{2,1,0:T(8,128)(2,1)} %bitcast.65), calls=%async_computation.5 | async-start | bytes 9437184 | tf_op jit(solution)/shard_map/all_to_all | solution.py:431
  203.4 27.7 %all-gather.7.cloned.1.call-done = bf16[64,288,128]{2,1,0:T(8,128)(2,1)} async-done(((bf16[8,288,128]{2,1,0:T(8,128)(2,1)}), bf16[64,288,128]{2,1,0:T(8,128)(2,1)}) %all-gather.7.cloned.1.call-update) | async-done | bytes 4718608 | tf_op jit(solution)/shard_map/all_gather | solution.py:470
  231.1 2.1 slice.10
  233.2 0.9 copy.41
  234.1 0.8 copy.46
  235.0 1.5 slice_bitcast_fusion
  236.5 1.3 copy.42
  237.8 27.6 %all-to-all-done.5 = bf16[32,48,1536]{2,1,0:T(8,128)(2,1)} async-done(((bf16[32,48,1536]{2,1,0:T(8,128)(2,1)}), bf16[32,48,1536]{2,1,0:T(8,128)(2,1)}, u32[]{:S(2)}, u32[]{:S(2)}) %all-to-all-start.5) | async-done | bytes 4718624 | tf_op jit(solution)/shard_map/all_to_all | solution.py:431
  265.4 1.4 copy-done.2
  266.8 10.5 %experts.1 = bf16[1536,1536]{1,0:T(8,128)(2,1)} custom-call(bf16[1536,1536]{1,0:T(8,128)(2,1)} %bitcast.21.rows_ref, bf16[1536,1024]{1,0:T(8,128)(2,1)S(1)} %bitcast.56, bf16[512,1536]{1,0:T(8,128)(2,1)S(1)} %bitcast.57), custom_call_target="tpu_custom_call" | custom-call | flops 7247757312 | bytes 14155776 | tf_op jit(solution)/shard_map/experts/pallas_call | solution.py:345
  277.3 5.3 %all-to-all-start.6 = ((bf16[32,48,1536]{2,1,0:T(8,128)(2,1)}), bf16[32,48,1536]{2,1,0:T(8,128)(2,1)}, u32[]{:S(2)}, u32[]{:S(2)}) async-start(bf16[32,48,1536]{2,1,0:T(8,128)(2,1)} %bitcast.66), calls=%async_computation.6 | async-start | bytes 9437184 | tf_op jit(solution)/shard_map/all_to_all | solution.py:431
  282.6 1.9 weighing.1.both_ref
  284.6 60.0 %all-to-all-done.6 = bf16[32,48,1536]{2,1,0:T(8,128)(2,1)} async-done(((bf16[32,48,1536]{2,1,0:T(8,128)(2,1)}), bf16[32,48,1536]{2,1,0:T(8,128)(2,1)}, u32[]{:S(2)}, u32[]{:S(2)}) %all-to-all-start.6) | async-done | bytes 4718624 | tf_op jit(solution)/shard_map/all_to_all | solution.py:431
  344.6 1.1 copy-done.1
  345.8 4.1 %combine.1 = bf16[128,1536]{1,0:T(8,128)(2,1)} custom-call(s32[1]{0:T(128)S(6)} %sub.7.live_ref, bf16[256,1536]{1,0:T(8,128)(2,1)S(1)} %copy-done.1, bf16[1536,1536]{1,0:T(8,128)(2,1)} %bitcast.29.returned_ref, f32[128,1536]{1,0:T(8,128)S(1)} %copy-done.3), custom_call_target="tpu_custom_call" | custom-call | flops 1207959552 | bytes 5898240 | tf_op jit(solution)/shard_map/combine/pallas_call | solution.py:387
  (32 shorter events, 0.3 us)
Async XLA Ops:
  6.5 14.4 %copy-start = (bf16[8,16,128]{2,1,0:T(8,128)(2,1)S(1)}, bf16[8,16,128]{2,1,0:T(8,128)(2,1)}, u32[]{:S(2)}) copy-start(bf16[8,16,128]{2,1,0:T(8,128)(2,1)} %param.21) | copy-start | bytes 98308
  6.5 13.8 %copy-start.11 = (f32[48,64]{1,0:T(8,128)S(1)}, f32[48,64]{1,0:T(8,128)}, u32[]{:S(2)}) copy-start(f32[48,64]{1,0:T(8,128)} %param.18) | copy-start | bytes 36868
  6.5 13.9 %copy-start.12 = (f32[48,64]{1,0:T(8,128)S(1)}, f32[48,64]{1,0:T(8,128)}, u32[]{:S(2)}) copy-start(f32[48,64]{1,0:T(8,128)} %param.19) | copy-start | bytes 36868
  6.5 14.1 %copy-start.10 = (f32[48,192]{1,0:T(8,128)S(1)}, f32[48,192]{1,0:T(8,128)}, u32[]{:S(2)}) copy-start(f32[48,192]{1,0:T(8,128)} %param.17) | copy-start | bytes 110596
  6.5 14.3 %copy-start.8 = (f32[1,64,1536]{2,1,0:T(8,128)S(1)}, f32[1,64,1536]{2,1,0:T(8,128)}, u32[]{:S(2)}) copy-start(f32[1,64,1536]{2,1,0:T(8,128)} %param.27) | copy-start | bytes 1179652
  8.3 13.3 %copy-start.7 = (f32[1,192,1024]{2,1,0:T(8,128)S(1)}, f32[1,192,1024]{2,1,0:T(8,128)}, u32[]{:S(2)}) copy-start(f32[1,192,1024]{2,1,0:T(8,128)} %param.26) | copy-start | bytes 2359300
  8.3 23.6 %all-to-all-start = ((bf16[32,48,192]{2,1,0:T(8,128)(2,1)}), bf16[32,48,192]{2,1,0:T(8,128)(2,1)}, u32[]{:S(2)}, u32[]{:S(2)}) async-start(bf16[32,48,192]{2,1,0:T(8,128)(2,1)} %broadcast_in_dim.37), calls=%async_computation | async-start | bytes 1572864 | tf_op jit(solution)/shard_map/all_to_all | solution.py:431
  20.9 2.0 copy-start.13
  21.6 2.3 copy-start.6
  31.9 39.7 %all-to-all-start.1 = ((bf16[8,560,128]{2,1,0:T(8,128)(2,1)}), bf16[8,560,128]{2,1,0:T(8,128)(2,1)}, u32[]{:S(2)}, u32[]{:S(2)}) async-start(bf16[8,560,128]{2,1,0:T(8,128)(2,1)} %pad_maximum_fusion), calls=%async_computation.1 | async-start | bytes 2293760 | tf_op jit(solution)/shard_map/all_to_all | solution.py:456
  40.1 148.8 %all-gather.5.cloned.1.call-start = ((), (), s32[]{:S(2)}) async-start(), calls=%async_computation.7 | async-start | bytes 5308416 | tf_op jit(solution)/shard_map/all_gather | solution.py:461
  134.4 22.7 %all-to-all-start.2 = ((bf16[4,8,176,128]{3,2,1,0:T(8,128)(2,1)}), bf16[4,8,176,128]{3,2,1,0:T(8,128)(2,1)}, u32[]{:S(2)}, u32[]{:S(2)}) async-start(bf16[4,8,176,128]{3,2,1,0:T(8,128)(2,1)} %get-tuple-element.24), calls=%async_computation.2 | async-start | bytes 2883584 | tf_op jit(solution)/shard_map/all_to_all | solution.py:463
  157.0 17.7 %all-to-all-start.3 = ((bf16[8,288,128]{2,1,0:T(8,128)(2,1)}), bf16[8,288,128]{2,1,0:T(8,128)(2,1)}, u32[]{:S(2)}, u32[]{:S(2)}) async-start(bf16[8,288,128]{2,1,0:T(8,128)(2,1)} %get-tuple-element.26), calls=%async_computation.3 | async-start | bytes 1179648 | tf_op jit(solution)/shard_map/all_to_all | solution.py:466
  161.3 69.9 %all-gather.7.cloned.1.call-start = ((), (), s32[]{:S(2)}) async-start(), calls=%async_computation.8 | async-start | bytes 5308416 | tf_op jit(solution)/shard_map/all_gather | solution.py:470
  161.5 1.0 copy-start.4
  162.5 18.6 %copy-start.14 = (f32[1536]{0:T(1024)S(1)}, f32[1536]{0:T(1024)}, u32[]{:S(2)}) copy-start(f32[1536]{0:T(1024)} %param.23) | copy-start | bytes 18436
  162.5 18.6 %copy-start.9 = (bf16[1536,32]{0,1:T(8,128)(2,1)S(1)}, bf16[1536,32]{0,1:T(8,128)(2,1)}, u32[]{:S(2)}) copy-start(bf16[1536,32]{0,1:T(8,128)(2,1)} %param.24) | copy-start | bytes 294916
  162.5 26.4 %copy-start.5 = (s32[128,8]{0,1:T(8,128)S(1)}, s32[128,8]{0,1:T(8,128)}, u32[]{:S(2)}) copy-start(s32[128,8]{0,1:T(8,128)} %param.25) | copy-start | bytes 12292
  174.7 14.1 %all-to-all-start.4 = ((bf16[8,192,128]{2,1,0:T(8,128)(2,1)}), bf16[8,192,128]{2,1,0:T(8,128)(2,1)S(1)}, u32[]{:S(2)}, u32[]{:S(2)}) async-start(bf16[8,192,128]{2,1,0:T(8,128)(2,1)} %attention.1), calls=%async_computation.4 | async-start | bytes 786432 | tf_op jit(solution)/shard_map/all_to_all | solution.py:469
  195.8 69.6 %all-to-all-start.5 = ((bf16[32,48,1536]{2,1,0:T(8,128)(2,1)}), bf16[32,48,1536]{2,1,0:T(8,128)(2,1)}, u32[]{:S(2)}, u32[]{:S(2)}) async-start(bf16[32,48,1536]{2,1,0:T(8,128)(2,1)} %bitcast.65), calls=%async_computation.5 | async-start | bytes 9437184 | tf_op jit(solution)/shard_map/all_to_all | solution.py:431
  265.4 1.4 copy-start.2
  277.3 67.3 %copy-start.3 = (f32[128,1536]{1,0:T(8,128)S(1)}, f32[128,1536]{1,0:T(8,128)}, u32[]{:S(2)}) copy-start(f32[128,1536]{1,0:T(8,128)} %get-tuple-element.32.hidden_ref) | copy-start | bytes 2359300
  277.3 67.3 %all-to-all-start.6 = ((bf16[32,48,1536]{2,1,0:T(8,128)(2,1)}), bf16[32,48,1536]{2,1,0:T(8,128)(2,1)}, u32[]{:S(2)}, u32[]{:S(2)}) async-start(bf16[32,48,1536]{2,1,0:T(8,128)(2,1)} %bitcast.66), calls=%async_computation.6 | async-start | bytes 9437184 | tf_op jit(solution)/shard_map/all_to_all | solution.py:431
  344.6 1.1 copy-start.1
Sparse Core Ops, SparseCore 0:
  71.7 80.6 all-gather.4
  174.9 56.2 all-gather.6

commit v7 on v6

--- a/solution.py
+++ b/solution.py
@@ -148,21 +148,27 @@
     )(lengths, normalized, across, table)
 
 
-def relay_body(along_ref, payload_ref, expert_ref, sem):
-    copies = [pltpu.make_async_copy(along_ref.at[:, 272:], expert_ref, sem.at[8])]
+def relay_body(along_ref, payload_ref, expert_ref, held, sem):
+    loads = [pltpu.make_async_copy(along_ref.at[z], held.at[z], sem.at[z]) for z in range(8)]
+    for load in loads:
+        load.start()
+    for load in loads:
+        load.wait()
+    copies = []
     for d in range(4):
         copies.append(
             pltpu.make_async_copy(
-                along_ref.at[:, :144], payload_ref.at[d, :, pl.ds(0, 144)], sem.at[2 * d]
+                held.at[:, pl.ds(0, 144)], payload_ref.at[d, :, pl.ds(0, 144)], sem.at[2 * d]
             )
         )
         copies.append(
             pltpu.make_async_copy(
-                along_ref.at[:, pl.ds(144 + 32 * d, 32)],
+                held.at[:, pl.ds(144 + 32 * d, 32)],
                 payload_ref.at[d, :, pl.ds(144, 32)],
                 sem.at[2 * d + 1],
             )
         )
+    copies.append(pltpu.make_async_copy(held.at[:, pl.ds(272, 288)], expert_ref, sem.at[8]))
     for copy in copies:
         copy.start()
     for copy in copies:
@@ -179,7 +185,7 @@
         ),
         in_specs=[hbm],
         out_specs=(hbm, hbm),
-        scratch_shapes=[pltpu.SemaphoreType.DMA((9,))],
+        scratch_shapes=[pltpu.VMEM(along_z.shape, jnp.bfloat16), pltpu.SemaphoreType.DMA((9,))],
         cost_estimate=pl.CostEstimate(flops=0, bytes_accessed=4 << 20, transcendentals=0),
         name="relay",
     )(pltpu.with_memory_space_constraint(along_z, pltpu.HBM))
@@ -191,10 +197,10 @@
     weight, attended, place, staged, hidden_ref, rank_gates, sem, out_sem,
 ):
     copies = []
-    for z in range(8):
-        for y in range(2):
+    for y in range(2):
+        for z in range(8):
             copy = pltpu.make_async_copy(
-                weight_hbm.at[z, y], weight.at[pl.ds((y * 8 + z) * 96, 96)], sem.at[z * 2 + y]
+                weight_hbm.at[z, y], weight.at[pl.ds((y * 8 + z) * 96, 96)], sem.at[y * 8 + z]
             )
             copy.start()
             copies.append(copy)
@@ -224,9 +230,9 @@
         place[g * CAPACITY : (g + 1) * CAPACITY, :] = jnp.where(
             rank[g : g + 1, :] == slot, 1.0, 0.0
         ).astype(jnp.bfloat16)
-    for copy in copies:
-        copy.wait()
     for c in range(0, 1536, 256):
+        while copies and len(copies) > 16 - (c + 256 + 95) // 96:
+            copies.pop(0).wait()
         hidden_ref[:, c : c + 256] = rows_ref[:, c : c + 256].astype(jnp.float32) + lax.dot_general(
             attended[...],
             weight[c : c + 256, :],
@@ -362,40 +368,30 @@
     )(rows, gate_up, down)
 
 
-def combine_body(live_ref, both_ref, returned_ref, hidden_ref, out_ref, total):
-    step = pl.program_id(0)
+def combine_body(live_ref, both_ref, returned_ref, hidden_ref, out_ref):
     tokens = hidden_ref.shape[0]
-
-    @pl.when(step == 0)
-    def _():
-        total[...] = hidden_ref[...]
-
     mixed = jnp.dot(both_ref[...], returned_ref[...], preferred_element_type=jnp.float32)
-    total[...] += mixed[:tokens] + mixed[tokens:]
-
-    @pl.when(step == pl.num_programs(0) - 1)
-    def _():
-        row = lax.broadcasted_iota(jnp.int32, total.shape, 0)
-        out_ref[...] = jnp.where(row < live_ref[0], total[...], 0.0).astype(jnp.bfloat16)
+    total = hidden_ref[...] + (mixed[:tokens] + mixed[tokens:])
+    row = lax.broadcasted_iota(jnp.int32, total.shape, 0)
+    out_ref[...] = jnp.where(row < live_ref[0], total, 0.0).astype(jnp.bfloat16)
 
 
 def combine(live, both, returned, hidden):
     row_count, model_width = hidden.shape
     slots = returned.shape[0]
-    tile = slots // 2
-    whole = pl.BlockSpec((row_count, model_width), lambda i: (0, 0))
+    tile = model_width // 2
+    column = pl.BlockSpec((row_count, tile), lambda i: (0, i))
     return pl.pallas_call(
         combine_body,
         out_shape=jax.ShapeDtypeStruct((row_count, model_width), jnp.bfloat16),
-        grid=(slots // tile,),
+        grid=(model_width // tile,),
         in_specs=[
             pl.BlockSpec(memory_space=pltpu.SMEM),
-            pl.BlockSpec((2 * row_count, tile), lambda i: (0, i)),
-            pl.BlockSpec((tile, model_width), lambda i: (i, 0)),
-            whole,
+            pl.BlockSpec(memory_space=pltpu.VMEM),
+            pl.BlockSpec((slots, tile), lambda i: (0, i)),
+            column,
         ],
-        out_specs=whole,
-        scratch_shapes=[pltpu.VMEM((row_count, model_width), jnp.float32)],
+        out_specs=column,
         compiler_params=pltpu.CompilerParams(vmem_limit_bytes=24 << 20),
         cost_estimate=pl.CostEstimate(
             flops=4 * row_count * slots * model_width,
@@ -432,8 +428,13 @@
             rows, ("ep", "tp"), 0, 0, axis_index_groups=PLANE_GROUPS, tiled=True
         )
 
-    output_shard = o_proj.T.astype(jnp.bfloat16)
-    output_plane = in_plane(jnp.broadcast_to(output_shard[None], (EXPERTS, *output_shard.shape)))
+    def doubled(block, axis, bit):
+        size = lax.axis_size(axis)
+        other = lax.ppermute(block, axis, [(i, i ^ bit) for i in range(size)])
+        first = (lax.axis_index(axis) & bit) == 0
+        return jnp.concatenate(
+            [jnp.where(first, block, other), jnp.where(first, other, block)], axis=0
+        )
 
     weight_shard = jnp.concatenate(
         [q_proj, k_proj, value_projection, jnp.zeros_like(k_proj)], axis=1
@@ -452,11 +453,13 @@
         axis=1,
     )
     normalized = rms_scale(tokens_in.astype(jnp.float32), attn_gain).astype(jnp.bfloat16)
-    payload, output_plane, normalized = barrier((payload, output_plane, normalized))
+    output_plane = doubled(o_proj.T.astype(jnp.bfloat16)[None], "tp", 1)
+    output_plane, unused = barrier((output_plane, payload))
+    output_plane = doubled(doubled(output_plane, "tp", 2), "tp", 4)
+    output_plane = output_plane.transpose(1, 0, 2).reshape(48, model_width)
+    output_plane, normalized = barrier((output_plane, normalized))
+    output_plane = doubled(doubled(output_plane, "ep", 1), "ep", 16)
     along_z = lax.all_to_all(payload, "ep", 0, 0, axis_index_groups=Z_GROUPS, tiled=True)
-    output_plane = (
-        output_plane.reshape(4, 8, 48, 192).transpose(0, 2, 1, 3).reshape(192, model_width)
-    )
     output_plane, along_z = barrier((output_plane, along_z))
     output_weight = lax.all_gather(output_plane, "ep", axis_index_groups=Z_GROUPS)
     payload, by_expert = relay(along_z)

time: 358 us -> 285 us (0.80)
  Pallas kernels: 98.4 us -> 38.7 us
  waiting for transfers between devices: 170 us -> 152 us
  other arithmetic: 9.2 us -> 17.4 us
  local copies, waits for them, and re-layouts: 19.1 us -> 12.7 us
    pallas_call x1, Pallas kernels: 62.7 us -> 2.78 us  [relay(): pl.pallas_call(relay_body, out_shape=(pltpu.HBM((4, 8, 176, 128), jnp.bfl...]
    all_to_all x3 -> x2, waiting for transfers between devices: 94.9 us -> 72.7 us  [in_plane(): lax.all_to_all(rows, ('ep', 'tp'), 0, 0, axis_index_groups=PLANE_GROUPS,...]
    all_to_all x1, waiting for transfers between devices: 26.7 us -> 5.16 us  [on_device(): lax.all_to_all(payload, 'ep', 0, 0, axis_index_groups=Z_GROUPS, tiled=True)]
    all_gather x1, waiting for transfers between devices: 27.7 us -> 42.6 us  [on_device(): planes = lax.all_gather(hosted, 'ep', axis_index_groups=Z_GROUPS)]
    ppermute x0 -> x5, starting transfers between devices: none -> 11.4 us  [doubled(): other = lax.ppermute(block, axis, [(i, i ^ bit) for i in range(size)])]
    ppermute x0 -> x5, waiting for transfers between devices: none -> 11 us  [doubled(): other = lax.ppermute(block, axis, [(i, i ^ bit) for i in range(size)])]
    all_to_all x3 -> x2, starting transfers between devices: 21.7 us -> 12.9 us  [in_plane(): lax.all_to_all(rows, ('ep', 'tp'), 0, 0, axis_index_groups=PLANE_GROUPS,...]
  transfers between devices with their start and end apart: 9 -> 13, of which waited for: 7 -> 9; matrix products, arithmetic and copies ran while one was open for 6% -> 9% of each run, Pallas kernels for 23% -> 9%
where the time goes in v7:
time: 285 us; the launch traced here: 284 us
  waiting for transfers between devices  152 us (53%)
  starting transfers between devices  48.2 us (17%)
  Pallas kernels  38.7 us (14%)
  other arithmetic  17.4 us (6%)
  between operations  14.4 us (5%)
  local copies, waits for them, and re-layouts  12.7 us (4%)
    all_to_all x2, waiting for transfers between devices, in_plane(): lax.all_to_all(rows, ('ep', 'tp'), 0, 0, axis_index_groups=PLANE_GROUPS,...  72.7 us
    all_gather x1, waiting for transfers between devices, on_device(): planes = lax.all_gather(hosted, 'ep', axis_index_groups=Z_GROUPS)  42.6 us
    all_to_all x1, waiting for transfers between devices, on_device(): lax.all_to_all(payload, 'ep', 0, 0, axis_index_groups=CHIP_PAIR_GROUPS, t...  14.2 us
    all_to_all x2, starting transfers between devices, in_plane(): lax.all_to_all(rows, ('ep', 'tp'), 0, 0, axis_index_groups=PLANE_GROUPS,...  12.9 us
    pallas_call x1, Pallas kernels, attention(): pl.pallas_call(attention_body, out_shape=pltpu.HBM((seq_len // 128, 192,...  12.2 us
    ppermute x5, starting transfers between devices, doubled(): other = lax.ppermute(block, axis, [(i, i ^ bit) for i in range(size)])  11.4 us
    ppermute x5, waiting for transfers between devices, doubled(): other = lax.ppermute(block, axis, [(i, i ^ bit) for i in range(size)])  11 us
    pallas_call x1, Pallas kernels, experts(): pl.pallas_call(expert_body, out_shape=pltpu.HBM((count, model_width), jnp...  10.5 us
  transfers between devices with their start and end apart: 13, of which 9 were waited for; matrix products, arithmetic and copies ran while one was open for 9% of the time, Pallas kernels for 9%

profile of v7, /device:TPU:1, one launch (start us, length us, event | category | flops | bytes accessed | tf_op | source)
XLA Modules:
  0.0 283.9 jit_solution(13746321066058479270)
XLA Ops:
  6.5 0.8 convert_bitcast_fusion.2
  7.3 3.7 %collective-permute-start = (bf16[1,48,192]{2,1,0:T(8,128)(2,1)S(1)}, bf16[1,48,192]{2,1,0:T(8,128)(2,1)S(1)}, u32[]{:S(2)}, u32[]{:S(2)}) collective-permute-start(bf16[1,48,192]{2,1,0:T(8,128)(2,1)S(1)} %convert_bitcast_fusion.2), channel_id=1, source_target_pairs={{0,1},{1,0},{2,3},{3,2},{4,5},{5,4},{6,7},{7,6},{8,9},{9,8},{10,11... | collective-permute-start | bytes 55304 | tf_op jit(solution)/shard_map/ppermute | solution.py:433
  11.1 0.7 compare_select_fusion
  11.8 0.7 convert.12
  12.5 0.7 convert.13
  13.3 0.1 copy.37
  13.3 0.1 reshape.147
  13.5 0.8 convert.11
  14.3 0.1 pad.15.clone
  14.3 0.1 maximum_maximum_fusion
  14.5 1.0 convert_bitcast_fusion.1
  15.5 0.6 gather_fusion
  16.2 1.2 convert_bitcast_fusion
  17.4 0.0 copy-start.6
  17.4 0.1 copy.44
  17.5 0.1 copy.39
  17.6 1.1 pad_maximum_fusion
  18.7 8.3 %all-to-all-start = ((bf16[8,560,128]{2,1,0:T(8,128)(2,1)}), bf16[8,560,128]{2,1,0:T(8,128)(2,1)}, u32[]{:S(2)}, u32[]{:S(2)}) async-start(bf16[8,560,128]{2,1,0:T(8,128)(2,1)} %pad_maximum_fusion), calls=%async_computation | async-start | bytes 2293760 | tf_op jit(solution)/shard_map/all_to_all | solution.py:462
  27.0 0.0 all-gather.5.cloned.1.call-start
  27.1 0.7 fusion
  27.8 1.3 collective-permute-start.1
  29.1 1.7 collective-permute-done.1
  30.9 2.8 collective-permute-start.2
  33.7 2.7 fusion.2.normalized_ref
  36.5 0.1 copy.40
  36.6 0.2 reshape.132
  36.8 3.1 %collective-permute-start.3 = (bf16[48,1536]{1,0:T(8,128)(2,1)S(1)}, bf16[48,1536]{1,0:T(8,128)(2,1)}, u32[]{:S(2)}, u32[]{:S(2)}) collective-permute-start(bf16[48,1536]{1,0:T(8,128)(2,1)S(1)} %reshape.132), channel_id=1, source_target_pairs={{0,8},{8,0},{16,24},{24,16},{32,40},{40,32},{48,56},{56,48},{64,72... | collective-permute-start | bytes 442376 | tf_op jit(solution)/shard_map/ppermute | solution.py:433
  39.9 1.1 collective-permute-done.3
  41.0 1.0 broadcast_select_fusion.3
  42.1 0.7 pad_maximum_fusion.2
  42.8 0.4 collective-permute-start.4
  43.2 8.1 %collective-permute-done.4 = bf16[96,1536]{1,0:T(8,128)(2,1)} collective-permute-done((bf16[96,1536]{1,0:T(8,128)(2,1)}, bf16[96,1536]{1,0:T(8,128)(2,1)}, u32[]{:S(2)}, u32[]{:S(2)}) %collective-permute-start.4) | collective-permute-done | bytes 294944 | tf_op jit(solution)/shard_map/ppermute | solution.py:433
  51.3 1.1 broadcast_select_fusion.1
  52.4 0.9 pad_maximum_fusion.1
  53.3 5.2 %all-to-all-done.along_ref = bf16[8,560,128]{2,1,0:T(8,128)(2,1)} async-done(((bf16[8,560,128]{2,1,0:T(8,128)(2,1)}), bf16[8,560,128]{2,1,0:T(8,128)(2,1)}, u32[]{:S(2)}, u32[]{:S(2)}) %all-to-all-start) | async-done | bytes 1146912 | tf_op jit(solution)/shard_map/all_to_all | solution.py:462
  58.4 0.0 all-gather.5.cloned.1.call-update
  58.4 2.8 relay.1
  61.2 4.8 %all-to-all-start.1 = ((bf16[4,8,176,128]{3,2,1,0:T(8,128)(2,1)}), bf16[4,8,176,128]{3,2,1,0:T(8,128)(2,1)}, u32[]{:S(2)}, u32[]{:S(2)}) async-start(bf16[4,8,176,128]{3,2,1,0:T(8,128)(2,1)} %get-tuple-element.24), calls=%async_computation.1 | async-start | bytes 2883584 | tf_op jit(solution)/shard_map/all_to_all | solution.py:466
  66.7 3.0 %fusion.3.table_ref = f32[1024,128]{1,0:T(8,128)} fusion(f32[128]{0:T(128)S(1)} %get-tuple-element.43, f32[128]{0:T(128)S(1)} %get-tuple-element.44, f32[1024]{0:T(1024)S(1)} %add_convert_fusion, pred[128]{0:T(512)(128)(4,1)S(1)} %iota_compare_fusion), kind=kLoop, calls=%fused_computation.12 | loop fusion | flops 393216 | bytes 529536 | tf_op jit(solution)/shard_map/jit(_where)/select_n | solution.py:38
  69.7 14.2 %all-to-all-done.1.across_ref = bf16[4,8,176,128]{3,2,1,0:T(8,128)(2,1)} async-done(((bf16[4,8,176,128]{3,2,1,0:T(8,128)(2,1)}), bf16[4,8,176,128]{3,2,1,0:T(8,128)(2,1)}, u32[]{:S(2)}, u32[]{:S(2)}) %all-to-all-start.1) | async-done | bytes 1441824 | tf_op jit(solution)/shard_map/all_to_all | solution.py:466
  84.0 4.2 %all-to-all-start.2 = ((bf16[8,288,128]{2,1,0:T(8,128)(2,1)}), bf16[8,288,128]{2,1,0:T(8,128)(2,1)}, u32[]{:S(2)}, u32[]{:S(2)}) async-start(bf16[8,288,128]{2,1,0:T(8,128)(2,1)} %get-tuple-element.26), calls=%async_computation.2 | async-start | bytes 1179648 | tf_op jit(solution)/shard_map/all_to_all | solution.py:469
  88.2 0.2 all-gather.7.cloned.1.call-start
  88.4 1.0 copy-done.4
  89.5 12.2 %attention.1 = bf16[8,192,128]{2,1,0:T(8,128)(2,1)} custom-call(s32[1]{0:T(128)S(6)} %copy.48.length_ref, bf16[1024,1536]{1,0:T(8,128)(2,1)S(1)} %fusion.2.normalized_ref, bf16[4,8,176,128]{3,2,1,0:T(8,128)(2,1)} %all-to-all-done.1.across_ref, f32[1024,128]{1,0:T(8,128)S(1)} %copy-done.4), custom_call_target="tpu_custom_call" | custom-call | flops 12000000000 | bytes 8388608 | tf_op jit(solution)/shard_map/attention/pallas_call | solution.py:132
  101.7 0.0 all-gather.7.cloned.1.call-update
  101.7 6.3 %all-to-all-start.3 = ((bf16[8,192,128]{2,1,0:T(8,128)(2,1)}), bf16[8,192,128]{2,1,0:T(8,128)(2,1)S(1)}, u32[]{:S(2)}, u32[]{:S(2)}) async-start(bf16[8,192,128]{2,1,0:T(8,128)(2,1)} %attention.1), calls=%async_computation.3 | async-start | bytes 786432 | tf_op jit(solution)/shard_map/all_to_all | solution.py:472
  108.1 1.0 constant_dynamic-slice_fusion.rows_ref
  109.2 6.7 %all-to-all-done.3.parts_ref = bf16[8,192,128]{2,1,0:T(8,128)(2,1)S(1)} async-done(((bf16[8,192,128]{2,1,0:T(8,128)(2,1)}), bf16[8,192,128]{2,1,0:T(8,128)(2,1)S(1)}, u32[]{:S(2)}, u32[]{:S(2)}) %all-to-all-start.3) | async-done | bytes 393248 | tf_op jit(solution)/shard_map/all_to_all | solution.py:472
  115.9 7.4 %project_and_dispatch.1 = (f32[128,1536]{1,0:T(8,128)}, bf16[1536,1536]{1,0:T(8,128)(2,1)}, f32[64,128]{1,0:T(8,128)}) custom-call(bf16[8,192,128]{2,1,0:T(8,128)(2,1)S(1)} %all-to-all-done.3.parts_ref, bf16[8,2,96,1536]{3,2,1,0:T(8,128)(2,1)} %bitcast.65, bf16[128,1536]{1,0:T(8,128)(2,1)S(1)} %constant_dynamic-slice_fusion.rows_ref, ...), custom_call_target="tpu_custom_call" | custom-call | flops 1207959552 | bytes 9437184 | tf_op jit(solution)/shard_map/project_and_dispatch/pallas_call | solution.py:273
  123.2 7.6 %all-to-all-start.4 = ((bf16[32,48,1536]{2,1,0:T(8,128)(2,1)}), bf16[32,48,1536]{2,1,0:T(8,128)(2,1)}, u32[]{:S(2)}, u32[]{:S(2)}) async-start(bf16[32,48,1536]{2,1,0:T(8,128)(2,1)} %bitcast.66), calls=%async_computation.4 | async-start | bytes 9437184 | tf_op jit(solution)/shard_map/all_to_all | solution.py:427
  130.8 42.6 %all-gather.7.cloned.1.call-done = bf16[64,288,128]{2,1,0:T(8,128)(2,1)} async-done(((bf16[8,288,128]{2,1,0:T(8,128)(2,1)}), bf16[64,288,128]{2,1,0:T(8,128)(2,1)}) %all-gather.7.cloned.1.call-update) | async-done | bytes 4718608 | tf_op jit(solution)/shard_map/all_gather | solution.py:473
  173.4 2.1 slice.10
  175.5 0.9 copy.42
  176.4 0.8 copy.47
  177.2 1.5 slice_bitcast_fusion
  178.8 1.3 copy.43
  180.1 12.7 %all-to-all-done.4 = bf16[32,48,1536]{2,1,0:T(8,128)(2,1)} async-done(((bf16[32,48,1536]{2,1,0:T(8,128)(2,1)}), bf16[32,48,1536]{2,1,0:T(8,128)(2,1)}, u32[]{:S(2)}, u32[]{:S(2)}) %all-to-all-start.4) | async-done | bytes 4718624 | tf_op jit(solution)/shard_map/all_to_all | solution.py:427
  192.8 1.4 copy-done.2
  194.2 10.5 %experts.1 = bf16[1536,1536]{1,0:T(8,128)(2,1)} custom-call(bf16[1536,1536]{1,0:T(8,128)(2,1)} %bitcast.22.rows_ref, bf16[1536,1024]{1,0:T(8,128)(2,1)S(1)} %bitcast.57, bf16[512,1536]{1,0:T(8,128)(2,1)S(1)} %bitcast.58), custom_call_target="tpu_custom_call" | custom-call | flops 7247757312 | bytes 14155776 | tf_op jit(solution)/shard_map/experts/pallas_call | solution.py:351
  204.7 5.3 %all-to-all-start.5 = ((bf16[32,48,1536]{2,1,0:T(8,128)(2,1)}), bf16[32,48,1536]{2,1,0:T(8,128)(2,1)}, u32[]{:S(2)}, u32[]{:S(2)}) async-start(bf16[32,48,1536]{2,1,0:T(8,128)(2,1)} %bitcast.67), calls=%async_computation.5 | async-start | bytes 9437184 | tf_op jit(solution)/shard_map/all_to_all | solution.py:427
  210.0 1.9 weighing.1.both_ref
  211.9 60.0 %all-to-all-done.5 = bf16[32,48,1536]{2,1,0:T(8,128)(2,1)} async-done(((bf16[32,48,1536]{2,1,0:T(8,128)(2,1)}), bf16[32,48,1536]{2,1,0:T(8,128)(2,1)}, u32[]{:S(2)}, u32[]{:S(2)}) %all-to-all-start.5) | async-done | bytes 4718624 | tf_op jit(solution)/shard_map/all_to_all | solution.py:427
  272.0 1.1 copy-done.1
  273.1 3.9 %combine.1 = bf16[128,1536]{1,0:T(8,128)(2,1)} custom-call(s32[1]{0:T(128)S(6)} %sub.7.live_ref, bf16[256,1536]{1,0:T(8,128)(2,1)S(1)} %copy-done.1, bf16[1536,1536]{1,0:T(8,128)(2,1)} %bitcast.30.returned_ref, f32[128,1536]{1,0:T(8,128)S(1)} %copy-done.3), custom_call_target="tpu_custom_call" | custom-call | flops 1207959552 | bytes 5898240 | tf_op jit(solution)/shard_map/combine/pallas_call | solution.py:384
  (43 shorter events, 0.4 us)
Async XLA Ops:
  6.5 9.0 %copy-start = (bf16[8,16,128]{2,1,0:T(8,128)(2,1)S(1)}, bf16[8,16,128]{2,1,0:T(8,128)(2,1)}, u32[]{:S(2)}) copy-start(bf16[8,16,128]{2,1,0:T(8,128)(2,1)} %param.21) | copy-start | bytes 98308
  7.3 20.4 %collective-permute-start = (bf16[1,48,192]{2,1,0:T(8,128)(2,1)S(1)}, bf16[1,48,192]{2,1,0:T(8,128)(2,1)S(1)}, u32[]{:S(2)}, u32[]{:S(2)}) collective-permute-start(bf16[1,48,192]{2,1,0:T(8,128)(2,1)S(1)} %convert_bitcast_fusion.2), channel_id=1, source_target_pairs={{0,1},{1,0},{2,3},{3,2},{4,5},{5,4},{6,7},{7,6},{8,9},{9,8},{10,11... | collective-permute-start | bytes 55304 | tf_op jit(solution)/shard_map/ppermute | solution.py:433
  17.4 9.7 %copy-start.6 = (bf16[1024,1536]{1,0:T(8,128)(2,1)S(1)}, bf16[1024,1536]{1,0:T(8,128)(2,1)}, u32[]{:S(2)}) copy-start(bf16[1024,1536]{1,0:T(8,128)(2,1)} %param.14) | copy-start | bytes 9437188
  18.7 9.1 %copy-start.8 = (f32[192,48]{0,1:T(8,128)S(1)}, f32[192,48]{0,1:T(8,128)}, u32[]{:S(2)}) copy-start(f32[192,48]{0,1:T(8,128)} %param.20) | copy-start | bytes 110596
  18.7 15.0 %copy-start.10 = (f32[1536]{0:T(1024)S(1)}, f32[1536]{0:T(1024)}, u32[]{:S(2)}) copy-start(f32[1536]{0:T(1024)} %param.16) | copy-start | bytes 18436
  18.7 39.7 %all-to-all-start = ((bf16[8,560,128]{2,1,0:T(8,128)(2,1)}), bf16[8,560,128]{2,1,0:T(8,128)(2,1)}, u32[]{:S(2)}, u32[]{:S(2)}) async-start(bf16[8,560,128]{2,1,0:T(8,128)(2,1)} %pad_maximum_fusion), calls=%async_computation | async-start | bytes 2293760 | tf_op jit(solution)/shard_map/all_to_all | solution.py:462
  27.0 88.8 %all-gather.5.cloned.1.call-start = ((), (), s32[]{:S(2)}) async-start(), calls=%async_computation.6 | async-start | bytes 5308416 | tf_op jit(solution)/shard_map/all_gather | solution.py:464
  27.8 3.0 %collective-permute-start.1 = (bf16[2,48,192]{2,1,0:T(8,128)(2,1)S(1)}, bf16[2,48,192]{2,1,0:T(8,128)(2,1)S(1)}, u32[]{:S(2)}, u32[]{:S(2)}) collective-permute-start(bf16[2,48,192]{2,1,0:T(8,128)(2,1)S(1)} %pad_maximum_fusion.4), channel_id=1, source_target_pairs={{0,2},{1,3},{2,0},{3,1},{4,6},{5,7},{6,4},{7,5},{8,10},{9,11},{10,... | collective-permute-start | bytes 110600 | tf_op jit(solution)/shard_map/ppermute | solution.py:433
  30.9 5.5 %collective-permute-start.2 = (bf16[4,48,192]{2,1,0:T(8,128)(2,1)S(1)}, bf16[4,48,192]{2,1,0:T(8,128)(2,1)S(1)}, u32[]{:S(2)}, u32[]{:S(2)}) collective-permute-start(bf16[4,48,192]{2,1,0:T(8,128)(2,1)S(1)} %pad_maximum_fusion.3), channel_id=1, source_target_pairs={{0,4},{1,5},{2,6},{3,7},{4,0},{5,1},{6,2},{7,3},{8,12},{9,13},{10,... | collective-permute-start | bytes 221192 | tf_op jit(solution)/shard_map/ppermute | solution.py:433
  36.7 3.2 %copy-start.7 = (bf16[48,1536]{1,0:T(8,128)(2,1)}, bf16[48,1536]{1,0:T(8,128)(2,1)S(1)}, u32[]{:S(2)}) copy-start(bf16[48,1536]{1,0:T(8,128)(2,1)S(1)} %reshape.132) | copy-start | bytes 442372
  36.8 4.3 %collective-permute-start.3 = (bf16[48,1536]{1,0:T(8,128)(2,1)S(1)}, bf16[48,1536]{1,0:T(8,128)(2,1)}, u32[]{:S(2)}, u32[]{:S(2)}) collective-permute-start(bf16[48,1536]{1,0:T(8,128)(2,1)S(1)} %reshape.132), channel_id=1, source_target_pairs={{0,8},{8,0},{16,24},{24,16},{32,40},{40,32},{48,56},{56,48},{64,72... | collective-permute-start | bytes 442376 | tf_op jit(solution)/shard_map/ppermute | solution.py:433
  42.8 8.5 %collective-permute-start.4 = (bf16[96,1536]{1,0:T(8,128)(2,1)}, bf16[96,1536]{1,0:T(8,128)(2,1)}, u32[]{:S(2)}, u32[]{:S(2)}) collective-permute-start(bf16[96,1536]{1,0:T(8,128)(2,1)} %pad_maximum_fusion.2), channel_id=1, source_target_pairs={{0,128},{8,136},{16,144},{24,152},{32,160},{40,168},{48,176},{56,1... | collective-permute-start | bytes 884744 | tf_op jit(solution)/shard_map/ppermute | solution.py:433
  61.2 22.7 %all-to-all-start.1 = ((bf16[4,8,176,128]{3,2,1,0:T(8,128)(2,1)}), bf16[4,8,176,128]{3,2,1,0:T(8,128)(2,1)}, u32[]{:S(2)}, u32[]{:S(2)}) async-start(bf16[4,8,176,128]{3,2,1,0:T(8,128)(2,1)} %get-tuple-element.24), calls=%async_computation.1 | async-start | bytes 2883584 | tf_op jit(solution)/shard_map/all_to_all | solution.py:466
  84.0 17.7 %all-to-all-start.2 = ((bf16[8,288,128]{2,1,0:T(8,128)(2,1)}), bf16[8,288,128]{2,1,0:T(8,128)(2,1)}, u32[]{:S(2)}, u32[]{:S(2)}) async-start(bf16[8,288,128]{2,1,0:T(8,128)(2,1)} %get-tuple-element.26), calls=%async_computation.2 | async-start | bytes 1179648 | tf_op jit(solution)/shard_map/all_to_all | solution.py:469
  88.2 85.2 %all-gather.7.cloned.1.call-start = ((), (), s32[]{:S(2)}) async-start(), calls=%async_computation.7 | async-start | bytes 5308416 | tf_op jit(solution)/shard_map/all_gather | solution.py:473
  88.4 1.1 copy-start.4
  89.4 18.6 %copy-start.11 = (f32[1536]{0:T(1024)S(1)}, f32[1536]{0:T(1024)}, u32[]{:S(2)}) copy-start(f32[1536]{0:T(1024)} %param.23) | copy-start | bytes 18436
  89.4 18.6 %copy-start.9 = (bf16[1536,32]{0,1:T(8,128)(2,1)S(1)}, bf16[1536,32]{0,1:T(8,128)(2,1)}, u32[]{:S(2)}) copy-start(bf16[1536,32]{0,1:T(8,128)(2,1)} %param.24) | copy-start | bytes 294916
  89.5 26.4 %copy-start.5 = (s32[128,8]{0,1:T(8,128)S(1)}, s32[128,8]{0,1:T(8,128)}, u32[]{:S(2)}) copy-start(s32[128,8]{0,1:T(8,128)} %param.25) | copy-start | bytes 12292
  101.7 14.2 %all-to-all-start.3 = ((bf16[8,192,128]{2,1,0:T(8,128)(2,1)}), bf16[8,192,128]{2,1,0:T(8,128)(2,1)S(1)}, u32[]{:S(2)}, u32[]{:S(2)}) async-start(bf16[8,192,128]{2,1,0:T(8,128)(2,1)} %attention.1), calls=%async_computation.3 | async-start | bytes 786432 | tf_op jit(solution)/shard_map/all_to_all | solution.py:472
  123.2 69.6 %all-to-all-start.4 = ((bf16[32,48,1536]{2,1,0:T(8,128)(2,1)}), bf16[32,48,1536]{2,1,0:T(8,128)(2,1)}, u32[]{:S(2)}, u32[]{:S(2)}) async-start(bf16[32,48,1536]{2,1,0:T(8,128)(2,1)} %bitcast.66), calls=%async_computation.4 | async-start | bytes 9437184 | tf_op jit(solution)/shard_map/all_to_all | solution.py:427
  192.8 1.4 copy-start.2
  204.7 67.3 %copy-start.3 = (f32[128,1536]{1,0:T(8,128)S(1)}, f32[128,1536]{1,0:T(8,128)}, u32[]{:S(2)}) copy-start(f32[128,1536]{1,0:T(8,128)} %get-tuple-element.32.hidden_ref) | copy-start | bytes 2359300
  204.7 67.3 %all-to-all-start.5 = ((bf16[32,48,1536]{2,1,0:T(8,128)(2,1)}), bf16[32,48,1536]{2,1,0:T(8,128)(2,1)}, u32[]{:S(2)}, u32[]{:S(2)}) async-start(bf16[32,48,1536]{2,1,0:T(8,128)(2,1)} %bitcast.67), calls=%async_computation.5 | async-start | bytes 9437184 | tf_op jit(solution)/shard_map/all_to_all | solution.py:427
  272.0 1.1 copy-start.1
Sparse Core Ops, SparseCore 0:
  58.6 54.6 all-gather.4
  115.0 58.2 all-gather.6

commit v8 on v7

--- a/solution.py
+++ b/solution.py
@@ -39,8 +39,8 @@
 
 
 def attention_body(
-    length_ref, normalized_ref, across_ref, table_ref,
-    out_ref, queries, keys, values, weight,
+    length_ref, source_ref, normalized_ref, first_ref, mine_ref, core_ref, far_ref, both_ref, table_ref,
+    out_ref, queries, keys, values, weight, cached_rows,
 ):
     seq_len = normalized_ref.shape[0]
     heads = queries.shape[0]
@@ -48,20 +48,24 @@
     chunk = 256
     lane = lax.broadcasted_iota(jnp.int32, (chunk, 256), 1)
     ones = jnp.ones((chunk, HEAD_WIDTH), jnp.bfloat16)
-    for e in range(32):
-        pair, z = (e // 16) * 2 + e % 2, (e // 2) % 8
-        for j in range(3):
-            weight[e * 48 : (e + 1) * 48, j * 128 : (j + 1) * 128] = across_ref[
-                pair, z, j * 48 : (j + 1) * 48, :
+    arrived = (
+        (first_ref, 32, mine_ref, 0),
+        (core_ref, 32, core_ref, 0),
+        (far_ref, 0, far_ref, 176),
+        (both_ref, 0, both_ref, 144),
+    )
+    for r, (weights_ref, weights_at, pages_ref, pages_at) in enumerate(arrived):
+        for z in range(8):
+            e = source_ref[r] + 2 * z
+            for j in range(3):
+                weight[pl.ds(pl.multiple_of(e * 48, 16), 48), j * 128 : (j + 1) * 128] = weights_ref[
+                    z, weights_at + j * 48 : weights_at + (j + 1) * 48, :
+                ]
+            cached_rows[pl.ds(pl.multiple_of(e * 32, 32), 32), :] = pages_ref[
+                z, pages_at : pages_at + 32, :
             ]
     for c in range(0, prefix, chunk):
-        rows = jnp.concatenate(
-            [
-                across_ref[(e // 16) * 2 + e % 2, (e // 2) % 8, 144:176, :]
-                for e in range(c // 32, (c + chunk) // 32)
-            ],
-            axis=0,
-        )
+        rows = cached_rows[c : c + chunk, :]
         keys[:, c : c + chunk] = rows.astype(jnp.float32).T[:HEAD_WIDTH].astype(jnp.bfloat16)
         values[c : c + chunk, :] = jnp.concatenate([rows[:, HEAD_WIDTH:], ones], axis=1)
     for c in range(0, seq_len, chunk):
@@ -124,7 +128,7 @@
             out_ref[block, 128:, :] = jnp.concatenate([low, high], axis=1).astype(jnp.bfloat16)
 
 
-def attention(lengths, normalized, across, table):
+def attention(lengths, sources, normalized, first, mine, core, far, both, table):
     seq_len, model_width = normalized.shape
     heads = 3
     total = 2 * seq_len
@@ -132,43 +136,35 @@
     return pl.pallas_call(
         attention_body,
         out_shape=pltpu.HBM((seq_len // 128, 192, 128), jnp.bfloat16),
-        in_specs=[pl.BlockSpec(memory_space=pltpu.SMEM)] + [vmem] * 3,
+        in_specs=[pl.BlockSpec(memory_space=pltpu.SMEM)] * 2 + [vmem] * 7,
         out_specs=vmem,
         scratch_shapes=[
             pltpu.VMEM((heads, seq_len, HEAD_WIDTH), jnp.bfloat16),
             pltpu.VMEM((HEAD_WIDTH, total), jnp.bfloat16),
             pltpu.VMEM((total, 2 * HEAD_WIDTH), jnp.bfloat16),
             pltpu.VMEM((model_width, 384), jnp.bfloat16),
+            pltpu.VMEM((seq_len, 2 * HEAD_WIDTH), jnp.bfloat16),
         ],
         compiler_params=pltpu.CompilerParams(vmem_limit_bytes=48 << 20),
         cost_estimate=pl.CostEstimate(
             flops=12_000_000_000, bytes_accessed=8 << 20, transcendentals=heads * seq_len * total
         ),
         name="attention",
-    )(lengths, normalized, across, table)
-
-
-def relay_body(along_ref, payload_ref, expert_ref, held, sem):
+    )(lengths, sources, normalized, first, mine, core, far, both, table)
+
+
+def relay_body(along_ref, far_ref, first_ref, expert_ref, mine_ref, held, sem):
     loads = [pltpu.make_async_copy(along_ref.at[z], held.at[z], sem.at[z]) for z in range(8)]
     for load in loads:
         load.start()
     for load in loads:
         load.wait()
-    copies = []
-    for d in range(4):
-        copies.append(
-            pltpu.make_async_copy(
-                held.at[:, pl.ds(0, 144)], payload_ref.at[d, :, pl.ds(0, 144)], sem.at[2 * d]
-            )
-        )
-        copies.append(
-            pltpu.make_async_copy(
-                held.at[:, pl.ds(144 + 32 * d, 32)],
-                payload_ref.at[d, :, pl.ds(144, 32)],
-                sem.at[2 * d + 1],
-            )
-        )
-    copies.append(pltpu.make_async_copy(held.at[:, pl.ds(272, 288)], expert_ref, sem.at[8]))
+    copies = [
+        pltpu.make_async_copy(held.at[:, pl.ds(32, 208)], far_ref, sem.at[0]),
+        pltpu.make_async_copy(held.at[:, pl.ds(0, 176)], first_ref, sem.at[1]),
+        pltpu.make_async_copy(held.at[:, pl.ds(240, 32)], mine_ref, sem.at[2]),
+        pltpu.make_async_copy(held.at[:, pl.ds(272, 288)], expert_ref, sem.at[3]),
+    ]
     for copy in copies:
         copy.start()
     for copy in copies:
@@ -179,13 +175,10 @@
     hbm = pl.BlockSpec(memory_space=pltpu.HBM)
     return pl.pallas_call(
         relay_body,
-        out_shape=(
-            pltpu.HBM((4, 8, 176, 128), jnp.bfloat16),
-            pltpu.HBM((8, 288, 128), jnp.bfloat16),
-        ),
+        out_shape=tuple(pltpu.HBM((8, rows, 128), jnp.bfloat16) for rows in (208, 176, 288, 32)),
         in_specs=[hbm],
-        out_specs=(hbm, hbm),
-        scratch_shapes=[pltpu.VMEM(along_z.shape, jnp.bfloat16), pltpu.SemaphoreType.DMA((9,))],
+        out_specs=(hbm,) * 4,
+        scratch_shapes=[pltpu.VMEM(along_z.shape, jnp.bfloat16), pltpu.SemaphoreType.DMA((8,))],
         cost_estimate=pl.CostEstimate(flops=0, bytes_accessed=4 << 20, transcendentals=0),
         name="relay",
     )(pltpu.with_memory_space_constraint(along_z, pltpu.HBM))
@@ -440,13 +433,20 @@
         [q_proj, k_proj, value_projection, jnp.zeros_like(k_proj)], axis=1
     ).astype(jnp.bfloat16)
     slabs = weight_shard.reshape(48, 3, 128).transpose(1, 0, 2).reshape(144, 128)
-    pages = key_value_pages[page_table[:, 0, :]].reshape(2, 8, 2, 32, 128)
+    ep_index = lax.axis_index("ep")
+    pair = (ep_index // 16) * 2 + ep_index % 2
+    step_to = jnp.array([1, 3, 2, 0], jnp.int32) ^ pair
+    prompts = (step_to // 2 * 16 + step_to % 2)[None, :] + 2 * jnp.arange(8, dtype=jnp.int32)[:, None]
+    pages = key_value_pages[page_table[:, 0, :][prompts]].reshape(8, 4, 32, 128)
     gate_up_slabs = gate_up_proj.astype(jnp.bfloat16).reshape(8, 24, 8, 128).transpose(0, 2, 1, 3)
     down_slabs = down_proj.astype(jnp.bfloat16).reshape(8, 8, 12, 128).transpose(0, 2, 1, 3)
     payload = jnp.concatenate(
         [
+            pages[:, 0],
             jnp.broadcast_to(slabs[None], (8, 144, 128)),
-            pages.transpose(1, 0, 2, 3, 4).reshape(8, 128, 128),
+            pages[:, 1],
+            pages[:, 2],
+            pages[:, 3],
             gate_up_slabs.reshape(8, 192, 128),
             down_slabs.reshape(8, 96, 128),
         ],
@@ -462,12 +462,15 @@
     along_z = lax.all_to_all(payload, "ep", 0, 0, axis_index_groups=Z_GROUPS, tiled=True)
     output_plane, along_z = barrier((output_plane, along_z))
     output_weight = lax.all_gather(output_plane, "ep", axis_index_groups=Z_GROUPS)
-    payload, by_expert = relay(along_z)
-    across = lax.all_to_all(payload, "ep", 0, 0, axis_index_groups=CHIP_PAIR_GROUPS, tiled=True)
+    far_out, first, by_expert, mine = relay(along_z)
+    far = lax.ppermute(far_out, "ep", [(i, i ^ 16) for i in range(32)])
+    core = lax.ppermute(first, "ep", [(i, i ^ 1) for i in range(32)])
+    both = lax.ppermute(far, "ep", [(i, i ^ 1) for i in range(32)])
     table = rotary_table(seq_len, 32 * 32)
-    by_expert, across = barrier((by_expert, across))
     hosted = lax.all_to_all(by_expert, "tp", 0, 0, tiled=True)
-    attended = attention(lengths, normalized, across, table)
+    source = jnp.array([0, 1, 2, 3], jnp.int32) ^ pair
+    sources = source // 2 * 16 + source % 2
+    attended = attention(lengths, sources, normalized, first, mine, core, far, both, table)
     attended, hosted = barrier((attended, hosted))
     attn_parts = lax.all_to_all(attended, "tp", 0, 0, tiled=True)
     planes = lax.all_gather(hosted, "ep", axis_index_groups=Z_GROUPS)
@@ -488,11 +491,11 @@
         planes[:, :, 192:].reshape(8, 8, 12, 8, 128).transpose(1, 0, 3, 2, 4).reshape(FF, model_width)
     )
     received = in_plane(send_rows.reshape(EXPERTS, CAPACITY, model_width))
-    both = weighing(rank_gates)
+    weighed = weighing(rank_gates)
     expert_out = experts(received.reshape(-1, model_width), gate_up_full, down_full)
     returned = in_plane(expert_out.reshape(EXPERTS, CAPACITY, model_width))
     live = lengths - tp_index * row_count
-    return combine(live, both, returned.reshape(-1, model_width), hidden)
+    return combine(live, weighed, returned.reshape(-1, model_width), hidden)
 
 
 def solution(mesh):

time: 285 us -> 290 us (1.018)
  local copies, waits for them, and re-layouts: 12.7 us -> 22.2 us
    all_to_all x1 -> x0, waiting for transfers between devices: 14.2 us -> none  [on_device(): lax.all_to_all(payload, 'ep', 0, 0, axis_index_groups=CHIP_PAIR_GROUPS, t...]
    ppermute x0 -> x3, waiting for transfers between devices: none -> 9.93 us  [the longest x1 9.92 us: on_device(): far = lax.ppermute(far_out, 'ep', [(i, i ^ 16) for i in range(32)])]
    unnamed x26 -> x34, local copies, waits for them, and re-layouts: 4.51 us -> 10.8 us
    all_to_all x1 -> x0, starting transfers between devices: 4.81 us -> none  [on_device(): lax.all_to_all(payload, 'ep', 0, 0, axis_index_groups=CHIP_PAIR_GROUPS, t...]
  transfers between devices with their start and end apart: 13 -> 15, of which waited for: 9 -> 10; matrix products, arithmetic and copies ran while one was open for 9% -> 12% of each run, Pallas kernels for 9% -> 8%
where the time goes in v8:
time: 290 us; the launch traced here: 288 us
  waiting for transfers between devices  150 us (52%)
  starting transfers between devices  45.9 us (16%)
  Pallas kernels  38.4 us (13%)
  local copies, waits for them, and re-layouts  22.2 us (8%)
  other arithmetic  17 us (6%)
  between operations  14.4 us (5%)
    all_to_all x2, waiting for transfers between devices, in_plane(): lax.all_to_all(rows, ('ep', 'tp'), 0, 0, axis_index_groups=PLANE_GROUPS,...  70.1 us
    all_gather x1, waiting for transfers between devices, on_device(): planes = lax.all_gather(hosted, 'ep', axis_index_groups=Z_GROUPS)  45.2 us
    all_to_all x2, starting transfers between devices, in_plane(): lax.all_to_all(rows, ('ep', 'tp'), 0, 0, axis_index_groups=PLANE_GROUPS,...  12.7 us
    pallas_call x1, Pallas kernels, attention(): pl.pallas_call(attention_body, out_shape=pltpu.HBM((seq_len // 128, 192,...  12.2 us
    ppermute x5, starting transfers between devices, doubled(): other = lax.ppermute(block, axis, [(i, i ^ bit) for i in range(size)])  11.4 us
    ppermute x5, waiting for transfers between devices, doubled(): other = lax.ppermute(block, axis, [(i, i ^ bit) for i in range(size)])  11 us
    unnamed x34, local copies, waits for them, and re-layouts  10.8 us
    pallas_call x1, Pallas kernels, experts(): pl.pallas_call(expert_body, out_shape=pltpu.HBM((count, model_width), jnp...  10.5 us
  transfers between devices with their start and end apart: 15, of which 10 were waited for; matrix products, arithmetic and copies ran while one was open for 12% of the time, Pallas kernels for 8%

profile of v8, /device:TPU:1, one launch (start us, length us, event | category | flops | bytes accessed | tf_op | source)
XLA Modules:
  0.0 288.2 jit_solution(16102127452623818006)
XLA Ops:
  6.5 0.8 convert_bitcast_fusion.1
  7.3 3.7 %collective-permute-start = (bf16[1,48,192]{2,1,0:T(8,128)(2,1)S(1)}, bf16[1,48,192]{2,1,0:T(8,128)(2,1)S(1)}, u32[]{:S(2)}, u32[]{:S(2)}) collective-permute-start(bf16[1,48,192]{2,1,0:T(8,128)(2,1)S(1)} %convert_bitcast_fusion.1), channel_id=1, source_target_pairs={{0,1},{1,0},{2,3},{3,2},{4,5},{5,4},{6,7},{7,6},{8,9},{9,8},{10,11... | collective-permute-start | bytes 55304 | tf_op jit(solution)/shard_map/ppermute | solution.py:426
  11.1 0.7 fusion.10
  11.9 0.7 convert.12
  12.7 0.7 convert.13
  13.4 0.8 copy.49
  14.2 0.6 gather_fusion
  15.2 0.8 convert.11
  16.2 1.2 convert_bitcast_fusion
  17.4 0.8 copy.57
  18.3 0.6 gather_fusion.1
  18.9 0.6 fusion.8
  19.5 0.8 broadcast_dynamic-update-slice_fusion
  20.3 0.6 fusion.7
  21.0 0.7 fusion.6
  21.7 0.6 fusion.5
  22.3 2.0 constant_dynamic-update-slice_fusion
  24.3 1.7 bitcast_dynamic-update-slice_fusion
  26.0 8.2 %all-to-all-start = ((bf16[8,560,128]{2,1,0:T(8,128)(2,1)}), bf16[8,560,128]{2,1,0:T(8,128)(2,1)}, u32[]{:S(2)}, u32[]{:S(2)}) async-start(bf16[8,560,128]{2,1,0:T(8,128)(2,1)} %bitcast_dynamic-update-slice_fusion), calls=%async_computation | async-start | bytes 2293760 | tf_op jit(solution)/shard_map/all_to_all | solution.py:462
  34.3 0.7 fusion
  35.0 1.3 collective-permute-start.1
  36.3 1.7 collective-permute-done.1
  38.1 2.8 collective-permute-start.2
  40.9 2.7 fusion.2.normalized_ref
  44.0 3.1 %collective-permute-start.3 = (bf16[48,1536]{1,0:T(8,128)(2,1)S(1)}, bf16[48,1536]{1,0:T(8,128)(2,1)}, u32[]{:S(2)}, u32[]{:S(2)}) collective-permute-start(bf16[48,1536]{1,0:T(8,128)(2,1)S(1)} %reshape.169), channel_id=1, source_target_pairs={{0,8},{8,0},{16,24},{24,16},{32,40},{40,32},{48,56},{56,48},{64,72... | collective-permute-start | bytes 442376 | tf_op jit(solution)/shard_map/ppermute | solution.py:426
  47.1 1.1 collective-permute-done.3
  48.2 1.0 broadcast_select_fusion.3
  49.3 0.7 pad_maximum_fusion.1
  50.0 0.4 collective-permute-start.4
  50.4 8.1 %collective-permute-done.4 = bf16[96,1536]{1,0:T(8,128)(2,1)} collective-permute-done((bf16[96,1536]{1,0:T(8,128)(2,1)}, bf16[96,1536]{1,0:T(8,128)(2,1)}, u32[]{:S(2)}, u32[]{:S(2)}) %collective-permute-start.4) | collective-permute-done | bytes 294944 | tf_op jit(solution)/shard_map/ppermute | solution.py:426
  58.5 1.1 broadcast_select_fusion.1
  59.6 0.9 pad_maximum_fusion
  60.5 5.1 %all-to-all-done.along_ref = bf16[8,560,128]{2,1,0:T(8,128)(2,1)} async-done(((bf16[8,560,128]{2,1,0:T(8,128)(2,1)}), bf16[8,560,128]{2,1,0:T(8,128)(2,1)}, u32[]{:S(2)}, u32[]{:S(2)}) %all-to-all-start) | async-done | bytes 1146912 | tf_op jit(solution)/shard_map/all_to_all | solution.py:462
  65.6 2.5 relay.1
  68.1 0.5 collective-permute-start.6
  68.6 0.9 collective-permute-start.5
  69.5 9.9 %collective-permute-done.6.far_ref = bf16[8,208,128]{2,1,0:T(8,128)(2,1)} collective-permute-done((bf16[8,208,128]{2,1,0:T(8,128)(2,1)}, bf16[8,208,128]{2,1,0:T(8,128)(2,1)}, u32[]{:S(2)}, u32[]{:S(2)}) %collective-permute-start.6) | collective-permute-done | bytes 426016 | tf_op jit(solution)/shard_map/ppermute | solution.py:466
  79.4 1.3 collective-permute-start.7
  81.4 3.0 %fusion.3.table_ref = f32[1024,128]{1,0:T(8,128)} fusion(f32[128]{0:T(128)S(1)} %get-tuple-element.43, f32[128]{0:T(128)S(1)} %get-tuple-element.44, f32[1024]{0:T(1024)S(1)} %add_convert_fusion, pred[128]{0:T(512)(128)(4,1)S(1)} %iota_compare_fusion), kind=kLoop, calls=%fused_computation.12 | loop fusion | flops 393216 | bytes 529536 | tf_op jit(solution)/shard_map/jit(_where)/select_n | solution.py:38
  84.4 4.2 %all-to-all-start.1 = ((bf16[8,288,128]{2,1,0:T(8,128)(2,1)}), bf16[8,288,128]{2,1,0:T(8,128)(2,1)}, u32[]{:S(2)}, u32[]{:S(2)}) async-start(bf16[8,288,128]{2,1,0:T(8,128)(2,1)} %get-tuple-element.26), calls=%async_computation.1 | async-start | bytes 1179648 | tf_op jit(solution)/shard_map/all_to_all | solution.py:470
  88.9 1.0 copy-done.4
  90.0 0.8 copy-done.7
  90.8 12.2 %attention.1 = bf16[8,192,128]{2,1,0:T(8,128)(2,1)} custom-call(s32[1]{0:T(128)S(6)} %copy.77.length_ref, s32[4]{0:T(128)S(1)} %fusion.9.source_ref, bf16[1024,1536]{1,0:T(8,128)(2,1)S(1)} %fusion.2.normalized_ref, bf16[8,176,128]{2,1,0:T(8,128)(2,1)S(1)} %copy-done.6, bf16[8,32,128]{2,1,0:T(8,128)(2,1)S(1)} %copy-done.7, ...), custom_call_target="tpu_custom_call" | custom-call | flops 12000000000 | bytes 8388608 | tf_op jit(solution)/shard_map/attention/pallas_call | solution.py:136
  103.1 6.4 %all-to-all-start.2 = ((bf16[8,192,128]{2,1,0:T(8,128)(2,1)}), bf16[8,192,128]{2,1,0:T(8,128)(2,1)S(1)}, u32[]{:S(2)}, u32[]{:S(2)}) async-start(bf16[8,192,128]{2,1,0:T(8,128)(2,1)} %attention.1), calls=%async_computation.2 | async-start | bytes 786432 | tf_op jit(solution)/shard_map/all_to_all | solution.py:475
  109.5 0.9 reshape.172
  110.5 1.0 constant_dynamic-slice_fusion.rows_ref
  111.5 6.5 %all-to-all-done.2.parts_ref = bf16[8,192,128]{2,1,0:T(8,128)(2,1)S(1)} async-done(((bf16[8,192,128]{2,1,0:T(8,128)(2,1)}), bf16[8,192,128]{2,1,0:T(8,128)(2,1)S(1)}, u32[]{:S(2)}, u32[]{:S(2)}) %all-to-all-start.2) | async-done | bytes 393248 | tf_op jit(solution)/shard_map/all_to_all | solution.py:475
  118.0 2.5 all-gather.5.cloned.1.call-done
  120.5 7.4 %project_and_dispatch.1 = (f32[128,1536]{1,0:T(8,128)}, bf16[1536,1536]{1,0:T(8,128)(2,1)}, f32[64,128]{1,0:T(8,128)}) custom-call(bf16[8,192,128]{2,1,0:T(8,128)(2,1)S(1)} %all-to-all-done.2.parts_ref, bf16[8,2,96,1536]{3,2,1,0:T(8,128)(2,1)} %bitcast.88, bf16[128,1536]{1,0:T(8,128)(2,1)S(1)} %constant_dynamic-slice_fusion.rows_ref, ...), custom_call_target="tpu_custom_call" | custom-call | flops 1207959552 | bytes 9437184 | tf_op jit(solution)/shard_map/project_and_dispatch/pallas_call | solution.py:266
  127.9 7.6 %all-to-all-start.3 = ((bf16[32,48,1536]{2,1,0:T(8,128)(2,1)}), bf16[32,48,1536]{2,1,0:T(8,128)(2,1)}, u32[]{:S(2)}, u32[]{:S(2)}) async-start(bf16[32,48,1536]{2,1,0:T(8,128)(2,1)} %bitcast.89), calls=%async_computation.3 | async-start | bytes 9437184 | tf_op jit(solution)/shard_map/all_to_all | solution.py:420
  135.5 45.2 %all-gather.7.cloned.1.call-done = bf16[64,288,128]{2,1,0:T(8,128)(2,1)} async-done(((bf16[8,288,128]{2,1,0:T(8,128)(2,1)}), bf16[64,288,128]{2,1,0:T(8,128)(2,1)}) %all-gather.7.cloned.1.call-update) | async-done | bytes 4718608 | tf_op jit(solution)/shard_map/all_gather | solution.py:476
  180.6 2.1 slice.32
  182.7 0.9 copy.60
  183.6 0.8 copy.70
  184.5 1.5 slice_bitcast_fusion
  186.0 1.3 copy.61
  187.3 10.1 %all-to-all-done.3 = bf16[32,48,1536]{2,1,0:T(8,128)(2,1)} async-done(((bf16[32,48,1536]{2,1,0:T(8,128)(2,1)}), bf16[32,48,1536]{2,1,0:T(8,128)(2,1)}, u32[]{:S(2)}, u32[]{:S(2)}) %all-to-all-start.3) | async-done | bytes 4718624 | tf_op jit(solution)/shard_map/all_to_all | solution.py:420
  197.4 1.4 copy-done.2
  198.8 10.5 %experts.1 = bf16[1536,1536]{1,0:T(8,128)(2,1)} custom-call(bf16[1536,1536]{1,0:T(8,128)(2,1)} %bitcast.25.rows_ref, bf16[1536,1024]{1,0:T(8,128)(2,1)S(1)} %bitcast.80, bf16[512,1536]{1,0:T(8,128)(2,1)S(1)} %bitcast.81), custom_call_target="tpu_custom_call" | custom-call | flops 7247757312 | bytes 14155776 | tf_op jit(solution)/shard_map/experts/pallas_call | solution.py:344
  209.3 5.1 %all-to-all-start.4 = ((bf16[32,48,1536]{2,1,0:T(8,128)(2,1)}), bf16[32,48,1536]{2,1,0:T(8,128)(2,1)}, u32[]{:S(2)}, u32[]{:S(2)}) async-start(bf16[32,48,1536]{2,1,0:T(8,128)(2,1)} %bitcast.90), calls=%async_computation.4 | async-start | bytes 9437184 | tf_op jit(solution)/shard_map/all_to_all | solution.py:420
  214.4 1.9 weighing.1.both_ref
  216.3 60.0 %all-to-all-done.4 = bf16[32,48,1536]{2,1,0:T(8,128)(2,1)} async-done(((bf16[32,48,1536]{2,1,0:T(8,128)(2,1)}), bf16[32,48,1536]{2,1,0:T(8,128)(2,1)}, u32[]{:S(2)}, u32[]{:S(2)}) %all-to-all-start.4) | async-done | bytes 4718624 | tf_op jit(solution)/shard_map/all_to_all | solution.py:420
  276.3 1.1 copy-done.1
  277.5 3.9 %combine.1 = bf16[128,1536]{1,0:T(8,128)(2,1)} custom-call(s32[1]{0:T(128)S(6)} %sub.18.live_ref, bf16[256,1536]{1,0:T(8,128)(2,1)S(1)} %copy-done.1, bf16[1536,1536]{1,0:T(8,128)(2,1)} %bitcast.33.returned_ref, f32[128,1536]{1,0:T(8,128)S(1)} %copy-done.3), custom_call_target="tpu_custom_call" | custom-call | flops 1207959552 | bytes 5898240 | tf_op jit(solution)/shard_map/combine/pallas_call | solution.py:377
  (61 shorter events, 1.6 us)
Async XLA Ops:
  6.5 11.7 %copy-start = (bf16[8,16,128]{2,1,0:T(8,128)(2,1)S(1)}, bf16[8,16,128]{2,1,0:T(8,128)(2,1)}, u32[]{:S(2)}) copy-start(bf16[8,16,128]{2,1,0:T(8,128)(2,1)} %param.23) | copy-start | bytes 98308
  7.3 27.6 %collective-permute-start = (bf16[1,48,192]{2,1,0:T(8,128)(2,1)S(1)}, bf16[1,48,192]{2,1,0:T(8,128)(2,1)S(1)}, u32[]{:S(2)}, u32[]{:S(2)}) collective-permute-start(bf16[1,48,192]{2,1,0:T(8,128)(2,1)S(1)} %convert_bitcast_fusion.1), channel_id=1, source_target_pairs={{0,1},{1,0},{2,3},{3,2},{4,5},{5,4},{6,7},{7,6},{8,9},{9,8},{10,11... | collective-permute-start | bytes 55304 | tf_op jit(solution)/shard_map/ppermute | solution.py:426
  22.3 12.0 %copy-start.8 = (bf16[1024,1536]{1,0:T(8,128)(2,1)S(1)}, bf16[1024,1536]{1,0:T(8,128)(2,1)}, u32[]{:S(2)}) copy-start(bf16[1024,1536]{1,0:T(8,128)(2,1)} %param.16) | copy-start | bytes 9437188
  26.0 39.6 %all-to-all-start = ((bf16[8,560,128]{2,1,0:T(8,128)(2,1)}), bf16[8,560,128]{2,1,0:T(8,128)(2,1)}, u32[]{:S(2)}, u32[]{:S(2)}) async-start(bf16[8,560,128]{2,1,0:T(8,128)(2,1)} %bitcast_dynamic-update-slice_fusion), calls=%async_computation | async-start | bytes 2293760 | tf_op jit(solution)/shard_map/all_to_all | solution.py:462
  34.2 0.8 copy-start.10
  34.2 6.7 %copy-start.11 = (f32[1536]{0:T(1024)S(1)}, f32[1536]{0:T(1024)}, u32[]{:S(2)}) copy-start(f32[1536]{0:T(1024)} %param.18) | copy-start | bytes 18436
  34.2 86.3 %all-gather.5.cloned.1.call-start = ((), (), s32[]{:S(2)}) async-start(), calls=%async_computation.5 | async-start | bytes 5308416 | tf_op jit(solution)/shard_map/all_gather | solution.py:464
  35.0 3.0 %collective-permute-start.1 = (bf16[2,48,192]{2,1,0:T(8,128)(2,1)S(1)}, bf16[2,48,192]{2,1,0:T(8,128)(2,1)S(1)}, u32[]{:S(2)}, u32[]{:S(2)}) collective-permute-start(bf16[2,48,192]{2,1,0:T(8,128)(2,1)S(1)} %pad_maximum_fusion.3), channel_id=1, source_target_pairs={{0,2},{1,3},{2,0},{3,1},{4,6},{5,7},{6,4},{7,5},{8,10},{9,11},{10,... | collective-permute-start | bytes 110600 | tf_op jit(solution)/shard_map/ppermute | solution.py:426
  38.1 5.5 %collective-permute-start.2 = (bf16[4,48,192]{2,1,0:T(8,128)(2,1)S(1)}, bf16[4,48,192]{2,1,0:T(8,128)(2,1)S(1)}, u32[]{:S(2)}, u32[]{:S(2)}) collective-permute-start(bf16[4,48,192]{2,1,0:T(8,128)(2,1)S(1)} %pad_maximum_fusion.2), channel_id=1, source_target_pairs={{0,4},{1,5},{2,6},{3,7},{4,0},{5,1},{6,2},{7,3},{8,12},{9,13},{10,... | collective-permute-start | bytes 221192 | tf_op jit(solution)/shard_map/ppermute | solution.py:426
  43.9 3.2 %copy-start.9 = (bf16[48,1536]{1,0:T(8,128)(2,1)}, bf16[48,1536]{1,0:T(8,128)(2,1)S(1)}, u32[]{:S(2)}) copy-start(bf16[48,1536]{1,0:T(8,128)(2,1)S(1)} %reshape.169) | copy-start | bytes 442372
  44.0 4.3 %collective-permute-start.3 = (bf16[48,1536]{1,0:T(8,128)(2,1)S(1)}, bf16[48,1536]{1,0:T(8,128)(2,1)}, u32[]{:S(2)}, u32[]{:S(2)}) collective-permute-start(bf16[48,1536]{1,0:T(8,128)(2,1)S(1)} %reshape.169), channel_id=1, source_target_pairs={{0,8},{8,0},{16,24},{24,16},{32,40},{40,32},{48,56},{56,48},{64,72... | collective-permute-start | bytes 442376 | tf_op jit(solution)/shard_map/ppermute | solution.py:426
  50.0 8.5 %collective-permute-start.4 = (bf16[96,1536]{1,0:T(8,128)(2,1)}, bf16[96,1536]{1,0:T(8,128)(2,1)}, u32[]{:S(2)}, u32[]{:S(2)}) collective-permute-start(bf16[96,1536]{1,0:T(8,128)(2,1)} %pad_maximum_fusion.1), channel_id=1, source_target_pairs={{0,128},{8,136},{16,144},{24,152},{32,160},{40,168},{48,176},{56,1... | collective-permute-start | bytes 884744 | tf_op jit(solution)/shard_map/ppermute | solution.py:426
  68.1 20.8 %copy-start.6 = (bf16[8,176,128]{2,1,0:T(8,128)(2,1)S(1)}, bf16[8,176,128]{2,1,0:T(8,128)(2,1)}, u32[]{:S(2)}) copy-start(bf16[8,176,128]{2,1,0:T(8,128)(2,1)} %get-tuple-element.23.first_ref) | copy-start | bytes 1081348
  68.1 11.3 %collective-permute-start.6 = (bf16[8,208,128]{2,1,0:T(8,128)(2,1)}, bf16[8,208,128]{2,1,0:T(8,128)(2,1)}, u32[]{:S(2)}, u32[]{:S(2)}) collective-permute-start(bf16[8,208,128]{2,1,0:T(8,128)(2,1)} %get-tuple-element.25), channel_id=1, source_target_pairs={{0,128},{8,136},{16,144},{24,152},{32,160},{40,168},{48,176},{56,1... | collective-permute-start | bytes 1277960 | tf_op jit(solution)/shard_map/ppermute | solution.py:466
  68.6 20.3 %collective-permute-start.5 = (bf16[8,176,128]{2,1,0:T(8,128)(2,1)}, bf16[8,176,128]{2,1,0:T(8,128)(2,1)}, u32[]{:S(2)}, u32[]{:S(2)}) collective-permute-start(bf16[8,176,128]{2,1,0:T(8,128)(2,1)} %get-tuple-element.23.first_ref), channel_id=1, source_target_pairs={{0,8},{8,0},{16,24},{24,16},{32,40},{40,32},{48,56},{56,48},{64,72... | collective-permute-start | bytes 1081352 | tf_op jit(solution)/shard_map/ppermute | solution.py:467
  79.4 9.5 %collective-permute-start.7 = (bf16[8,208,128]{2,1,0:T(8,128)(2,1)}, bf16[8,208,128]{2,1,0:T(8,128)(2,1)}, u32[]{:S(2)}, u32[]{:S(2)}) collective-permute-start(bf16[8,208,128]{2,1,0:T(8,128)(2,1)} %collective-permute-done.6.far_ref), channel_id=1, source_target_pairs={{0,8},{8,0},{16,24},{24,16},{32,40},{40,32},{48,56},{56,48},{64,72... | collective-permute-start | bytes 1277960 | tf_op jit(solution)/shard_map/ppermute | solution.py:468
  84.4 18.6 %all-to-all-start.1 = ((bf16[8,288,128]{2,1,0:T(8,128)(2,1)}), bf16[8,288,128]{2,1,0:T(8,128)(2,1)}, u32[]{:S(2)}, u32[]{:S(2)}) async-start(bf16[8,288,128]{2,1,0:T(8,128)(2,1)} %get-tuple-element.26), calls=%async_computation.1 | async-start | bytes 1179648 | tf_op jit(solution)/shard_map/all_to_all | solution.py:470
  88.7 91.9 %all-gather.7.cloned.1.call-start = ((), (), s32[]{:S(2)}) async-start(), calls=%async_computation.6 | async-start | bytes 5308416 | tf_op jit(solution)/shard_map/all_gather | solution.py:476
  88.9 1.1 copy-start.4
  90.0 0.8 copy-start.7
  90.8 18.7 %copy-start.12 = (f32[1536]{0:T(1024)S(1)}, f32[1536]{0:T(1024)}, u32[]{:S(2)}) copy-start(f32[1536]{0:T(1024)} %param.25) | copy-start | bytes 18436
  103.0 17.4 %copy-start.5 = (s32[128,8]{0,1:T(8,128)S(1)}, s32[128,8]{0,1:T(8,128)}, u32[]{:S(2)}) copy-start(s32[128,8]{0,1:T(8,128)} %param.27) | copy-start | bytes 12292
  103.1 14.9 %all-to-all-start.2 = ((bf16[8,192,128]{2,1,0:T(8,128)(2,1)}), bf16[8,192,128]{2,1,0:T(8,128)(2,1)S(1)}, u32[]{:S(2)}, u32[]{:S(2)}) async-start(bf16[8,192,128]{2,1,0:T(8,128)(2,1)} %attention.1), calls=%async_computation.2 | async-start | bytes 786432 | tf_op jit(solution)/shard_map/all_to_all | solution.py:475
  127.9 69.5 %all-to-all-start.3 = ((bf16[32,48,1536]{2,1,0:T(8,128)(2,1)}), bf16[32,48,1536]{2,1,0:T(8,128)(2,1)}, u32[]{:S(2)}, u32[]{:S(2)}) async-start(bf16[32,48,1536]{2,1,0:T(8,128)(2,1)} %bitcast.89), calls=%async_computation.3 | async-start | bytes 9437184 | tf_op jit(solution)/shard_map/all_to_all | solution.py:420
  197.4 1.4 copy-start.2
  209.3 67.1 %copy-start.3 = (f32[128,1536]{1,0:T(8,128)S(1)}, f32[128,1536]{1,0:T(8,128)}, u32[]{:S(2)}) copy-start(f32[128,1536]{1,0:T(8,128)} %get-tuple-element.32.hidden_ref) | copy-start | bytes 2359300
  209.3 67.1 %all-to-all-start.4 = ((bf16[32,48,1536]{2,1,0:T(8,128)(2,1)}), bf16[32,48,1536]{2,1,0:T(8,128)(2,1)}, u32[]{:S(2)}, u32[]{:S(2)}) async-start(bf16[32,48,1536]{2,1,0:T(8,128)(2,1)} %bitcast.90), calls=%async_computation.4 | async-start | bytes 9437184 | tf_op jit(solution)/shard_map/all_to_all | solution.py:420
  276.3 1.1 copy-start.1
Sparse Core Ops, SparseCore 0:
  65.7 54.6 all-gather.4
  122.3 58.3 all-gather.6

commit v9 on v7

--- a/solution.py
+++ b/solution.py
@@ -148,6 +148,50 @@
     )(lengths, normalized, across, table)
 
 
+def prepare_body(
+    table_ref, query_ref, key_ref, value_ref, gate_up_ref, down_ref, pages_ref, payload_ref, held, sem
+):
+    weight = jnp.concatenate(
+        [query_ref[...], key_ref[...], value_ref[...], jnp.zeros(key_ref.shape, jnp.float32)], axis=1
+    ).astype(jnp.bfloat16)
+    copies = []
+    for z in range(8):
+        for j in range(3):
+            held[z, j * 48 : (j + 1) * 48, :] = weight[:, j * 128 : (j + 1) * 128]
+        for d in range(4):
+            prompt = (d // 2) * 16 + z * 2 + d % 2
+            for s in range(2):
+                at = 144 + 32 * d + 16 * s
+                held[z, at : at + 16, :] = pages_ref[table_ref[prompt * 2 + s]]
+        for b in range(8):
+            held[z, 272 + 24 * b : 296 + 24 * b, :] = gate_up_ref[
+                z * 24 : (z + 1) * 24, b * 128 : (b + 1) * 128
+            ].astype(jnp.bfloat16)
+        for b in range(12):
+            held[z, 464 + 8 * b : 472 + 8 * b, :] = down_ref[
+                z * 8 : (z + 1) * 8, b * 128 : (b + 1) * 128
+            ].astype(jnp.bfloat16)
+        copy = pltpu.make_async_copy(held.at[z], payload_ref.at[z], sem.at[z])
+        copy.start()
+        copies.append(copy)
+    for copy in copies:
+        copy.wait()
+
+
+def prepare(page_table, q_proj, k_proj, value_projection, gate_up, down, pages):
+    vmem = pl.BlockSpec(memory_space=pltpu.VMEM)
+    shape = (8, 560, 128)
+    return pl.pallas_call(
+        prepare_body,
+        out_shape=pltpu.HBM(shape, jnp.bfloat16),
+        in_specs=[pl.BlockSpec(memory_space=pltpu.SMEM)] + [vmem] * 6,
+        out_specs=pl.BlockSpec(memory_space=pltpu.HBM),
+        scratch_shapes=[pltpu.VMEM(shape, jnp.bfloat16), pltpu.SemaphoreType.DMA((8,))],
+        cost_estimate=pl.CostEstimate(flops=0, bytes_accessed=3 << 20, transcendentals=0),
+        name="prepare",
+    )(page_table, q_proj, k_proj, value_projection, gate_up, down, pages)
+
+
 def relay_body(along_ref, payload_ref, expert_ref, held, sem):
     loads = [pltpu.make_async_copy(along_ref.at[z], held.at[z], sem.at[z]) for z in range(8)]
     for load in loads:
@@ -436,21 +480,8 @@
             [jnp.where(first, block, other), jnp.where(first, other, block)], axis=0
         )
 
-    weight_shard = jnp.concatenate(
-        [q_proj, k_proj, value_projection, jnp.zeros_like(k_proj)], axis=1
-    ).astype(jnp.bfloat16)
-    slabs = weight_shard.reshape(48, 3, 128).transpose(1, 0, 2).reshape(144, 128)
-    pages = key_value_pages[page_table[:, 0, :]].reshape(2, 8, 2, 32, 128)
-    gate_up_slabs = gate_up_proj.astype(jnp.bfloat16).reshape(8, 24, 8, 128).transpose(0, 2, 1, 3)
-    down_slabs = down_proj.astype(jnp.bfloat16).reshape(8, 8, 12, 128).transpose(0, 2, 1, 3)
-    payload = jnp.concatenate(
-        [
-            jnp.broadcast_to(slabs[None], (8, 144, 128)),
-            pages.transpose(1, 0, 2, 3, 4).reshape(8, 128, 128),
-            gate_up_slabs.reshape(8, 192, 128),
-            down_slabs.reshape(8, 96, 128),
-        ],
-        axis=1,
+    payload = prepare(
+        page_table.reshape(-1), q_proj, k_proj, value_projection, gate_up_proj[0], down_proj[0], key_value_pages
     )
     normalized = rms_scale(tokens_in.astype(jnp.float32), attn_gain).astype(jnp.bfloat16)
     output_plane = doubled(o_proj.T.astype(jnp.bfloat16)[None], "tp", 1)

time: 285 us -> 281 us (0.986)
  other arithmetic: 17.4 us -> 11.1 us
  transfers between devices with their start and end apart: 13 -> 13, of which waited for: 9 -> 9; matrix products, arithmetic and copies ran while one was open for 9% -> 7% of each run, Pallas kernels for 9% -> 10%
where the time goes in v9:
time: 281 us; the launch traced here: 280 us
  waiting for transfers between devices  152 us (54%)
  starting transfers between devices  48.2 us (17%)
  Pallas kernels  41.2 us (15%)
  between operations  14.4 us (5%)
  local copies, waits for them, and re-layouts  13 us (5%)
  other arithmetic  11.1 us (4%)
    all_to_all x2, waiting for transfers between devices, in_plane(): lax.all_to_all(rows, ('ep', 'tp'), 0, 0, axis_index_groups=PLANE_GROUPS,...  72.7 us
    all_gather x1, waiting for transfers between devices, on_device(): planes = lax.all_gather(hosted, 'ep', axis_index_groups=Z_GROUPS)  42.6 us
    all_to_all x1, waiting for transfers between devices, on_device(): lax.all_to_all(payload, 'ep', 0, 0, axis_index_groups=CHIP_PAIR_GROUPS, t...  14.2 us
    all_to_all x2, starting transfers between devices, in_plane(): lax.all_to_all(rows, ('ep', 'tp'), 0, 0, axis_index_groups=PLANE_GROUPS,...  12.9 us
    pallas_call x1, Pallas kernels, attention(): pl.pallas_call(attention_body, out_shape=pltpu.HBM((seq_len // 128, 192,...  12.2 us
    ppermute x5, starting transfers between devices, doubled(): other = lax.ppermute(block, axis, [(i, i ^ bit) for i in range(size)])  11.4 us
    ppermute x5, waiting for transfers between devices, doubled(): other = lax.ppermute(block, axis, [(i, i ^ bit) for i in range(size)])  11 us
    pallas_call x1, Pallas kernels, experts(): pl.pallas_call(expert_body, out_shape=pltpu.HBM((count, model_width), jnp...  10.5 us
  transfers between devices with their start and end apart: 13, of which 9 were waited for; matrix products, arithmetic and copies ran while one was open for 7% of the time, Pallas kernels for 10%

profile of v9, /device:TPU:1, one launch (start us, length us, event | category | flops | bytes accessed | tf_op | source)
XLA Modules:
  0.0 280.3 jit_solution(9915201553154772904)
XLA Ops:
  6.5 1.0 convert_bitcast_fusion
  7.5 3.7 %collective-permute-start = (bf16[1,48,192]{2,1,0:T(8,128)(2,1)S(1)}, bf16[1,48,192]{2,1,0:T(8,128)(2,1)S(1)}, u32[]{:S(2)}, u32[]{:S(2)}) collective-permute-start(bf16[1,48,192]{2,1,0:T(8,128)(2,1)S(1)} %convert_bitcast_fusion), channel_id=1, source_target_pairs={{0,1},{1,0},{2,3},{3,2},{4,5},{5,4},{6,7},{7,6},{8,9},{9,8},{10,11... | collective-permute-start | bytes 55304 | tf_op jit(solution)/shard_map/ppermute | solution.py:477
  11.2 0.8 copy.23
  12.0 0.6 reshape.79.table_ref
  12.6 2.5 prepare.1
  15.1 0.0 copy-start.7
  15.1 0.0 copy-start.9
  15.1 8.3 %all-to-all-start = ((bf16[8,560,128]{2,1,0:T(8,128)(2,1)}), bf16[8,560,128]{2,1,0:T(8,128)(2,1)}, u32[]{:S(2)}, u32[]{:S(2)}) async-start(bf16[8,560,128]{2,1,0:T(8,128)(2,1)} %prepare.1), calls=%async_computation | async-start | bytes 2293760 | tf_op jit(solution)/shard_map/all_to_all | solution.py:493
  23.4 0.0 all-gather.5.cloned.1.call-start
  23.5 0.0 copy-done.5
  23.5 0.7 fusion
  24.2 0.0 collective-permute-done
  24.2 0.0 copy-done.7
  24.3 1.3 collective-permute-start.1
  25.6 1.7 collective-permute-done.1
  27.3 2.8 %collective-permute-start.2 = (bf16[4,48,192]{2,1,0:T(8,128)(2,1)S(1)}, bf16[4,48,192]{2,1,0:T(8,128)(2,1)S(1)}, u32[]{:S(2)}, u32[]{:S(2)}) collective-permute-start(bf16[4,48,192]{2,1,0:T(8,128)(2,1)S(1)} %pad_maximum_fusion.2), channel_id=1, source_target_pairs={{0,4},{1,5},{2,6},{3,7},{4,0},{5,1},{6,2},{7,3},{8,12},{9,13},{10,... | collective-permute-start | bytes 221192 | tf_op jit(solution)/shard_map/ppermute | solution.py:477
  30.2 0.0 copy-done.9
  30.2 2.7 fusion.2.normalized_ref
  32.8 0.0 collective-permute-done.2
  32.9 0.1 copy.24
  33.0 0.2 reshape.80
  33.2 0.0 copy-start.6
  33.2 3.1 %collective-permute-start.3 = (bf16[48,1536]{1,0:T(8,128)(2,1)S(1)}, bf16[48,1536]{1,0:T(8,128)(2,1)}, u32[]{:S(2)}, u32[]{:S(2)}) collective-permute-start(bf16[48,1536]{1,0:T(8,128)(2,1)S(1)} %reshape.80), channel_id=1, source_target_pairs={{0,8},{8,0},{16,24},{24,16},{32,40},{40,32},{48,56},{56,48},{64,72... | collective-permute-start | bytes 442376 | tf_op jit(solution)/shard_map/ppermute | solution.py:477
  36.3 0.0 copy-done.6
  36.3 1.1 collective-permute-done.3
  37.5 1.0 broadcast_select_fusion.3
  38.5 0.7 pad_maximum_fusion.1
  39.2 0.4 collective-permute-start.4
  39.6 8.1 %collective-permute-done.4 = bf16[96,1536]{1,0:T(8,128)(2,1)} collective-permute-done((bf16[96,1536]{1,0:T(8,128)(2,1)}, bf16[96,1536]{1,0:T(8,128)(2,1)}, u32[]{:S(2)}, u32[]{:S(2)}) %collective-permute-start.4) | collective-permute-done | bytes 294944 | tf_op jit(solution)/shard_map/ppermute | solution.py:477
  47.8 1.1 broadcast_select_fusion.1
  48.8 0.9 pad_maximum_fusion
  49.7 5.2 %all-to-all-done.along_ref = bf16[8,560,128]{2,1,0:T(8,128)(2,1)} async-done(((bf16[8,560,128]{2,1,0:T(8,128)(2,1)}), bf16[8,560,128]{2,1,0:T(8,128)(2,1)}, u32[]{:S(2)}, u32[]{:S(2)}) %all-to-all-start) | async-done | bytes 1146912 | tf_op jit(solution)/shard_map/all_to_all | solution.py:493
  54.9 0.0 all-gather.5.cloned.1.call-update
  54.9 2.8 relay.1
  57.7 4.8 %all-to-all-start.1 = ((bf16[4,8,176,128]{3,2,1,0:T(8,128)(2,1)}), bf16[4,8,176,128]{3,2,1,0:T(8,128)(2,1)}, u32[]{:S(2)}, u32[]{:S(2)}) async-start(bf16[4,8,176,128]{3,2,1,0:T(8,128)(2,1)} %get-tuple-element.24), calls=%async_computation.1 | async-start | bytes 2883584 | tf_op jit(solution)/shard_map/all_to_all | solution.py:497
  63.1 3.0 %fusion.3.table_ref = f32[1024,128]{1,0:T(8,128)} fusion(f32[128]{0:T(128)S(1)} %get-tuple-element.43, f32[128]{0:T(128)S(1)} %get-tuple-element.44, f32[1024]{0:T(1024)S(1)} %add_convert_fusion, pred[128]{0:T(512)(128)(4,1)S(1)} %iota_compare_fusion), kind=kLoop, calls=%fused_computation.10 | loop fusion | flops 393216 | bytes 529536 | tf_op jit(solution)/shard_map/jit(_where)/select_n | solution.py:38
  66.1 14.2 %all-to-all-done.1.across_ref = bf16[4,8,176,128]{3,2,1,0:T(8,128)(2,1)} async-done(((bf16[4,8,176,128]{3,2,1,0:T(8,128)(2,1)}), bf16[4,8,176,128]{3,2,1,0:T(8,128)(2,1)}, u32[]{:S(2)}, u32[]{:S(2)}) %all-to-all-start.1) | async-done | bytes 1441824 | tf_op jit(solution)/shard_map/all_to_all | solution.py:497
  80.4 4.2 %all-to-all-start.2 = ((bf16[8,288,128]{2,1,0:T(8,128)(2,1)}), bf16[8,288,128]{2,1,0:T(8,128)(2,1)}, u32[]{:S(2)}, u32[]{:S(2)}) async-start(bf16[8,288,128]{2,1,0:T(8,128)(2,1)} %get-tuple-element.26), calls=%async_computation.2 | async-start | bytes 1179648 | tf_op jit(solution)/shard_map/all_to_all | solution.py:500
  84.6 0.2 all-gather.7.cloned.1.call-start
  84.8 0.0 copy-start.3
  84.8 1.0 copy-done.3
  85.9 12.2 %attention.1 = bf16[8,192,128]{2,1,0:T(8,128)(2,1)} custom-call(s32[1]{0:T(128)S(6)} %copy.31.length_ref, bf16[1024,1536]{1,0:T(8,128)(2,1)S(1)} %fusion.2.normalized_ref, bf16[4,8,176,128]{3,2,1,0:T(8,128)(2,1)} %all-to-all-done.1.across_ref, f32[1024,128]{1,0:T(8,128)S(1)} %copy-done.3), custom_call_target="tpu_custom_call" | custom-call | flops 12000000000 | bytes 8388608 | tf_op jit(solution)/shard_map/attention/pallas_call | solution.py:132
  98.1 0.0 all-to-all-done.2
  98.1 0.0 all-gather.7.cloned.1.call-update
  98.1 6.3 %all-to-all-start.3 = ((bf16[8,192,128]{2,1,0:T(8,128)(2,1)}), bf16[8,192,128]{2,1,0:T(8,128)(2,1)S(1)}, u32[]{:S(2)}, u32[]{:S(2)}) async-start(bf16[8,192,128]{2,1,0:T(8,128)(2,1)} %attention.1), calls=%async_computation.3 | async-start | bytes 786432 | tf_op jit(solution)/shard_map/all_to_all | solution.py:503
  104.4 0.0 copy-done.10
  104.5 1.0 constant_dynamic-slice_fusion.rows_ref
  105.6 6.7 %all-to-all-done.3.parts_ref = bf16[8,192,128]{2,1,0:T(8,128)(2,1)S(1)} async-done(((bf16[8,192,128]{2,1,0:T(8,128)(2,1)}), bf16[8,192,128]{2,1,0:T(8,128)(2,1)S(1)}, u32[]{:S(2)}, u32[]{:S(2)}) %all-to-all-start.3) | async-done | bytes 393248 | tf_op jit(solution)/shard_map/all_to_all | solution.py:503
  112.3 7.4 %project_and_dispatch.1 = (f32[128,1536]{1,0:T(8,128)}, bf16[1536,1536]{1,0:T(8,128)(2,1)}, f32[64,128]{1,0:T(8,128)}) custom-call(bf16[8,192,128]{2,1,0:T(8,128)(2,1)S(1)} %all-to-all-done.3.parts_ref, bf16[8,2,96,1536]{3,2,1,0:T(8,128)(2,1)} %bitcast.45, bf16[128,1536]{1,0:T(8,128)(2,1)S(1)} %constant_dynamic-slice_fusion.rows_ref, ...), custom_call_target="tpu_custom_call" | custom-call | flops 1207959552 | bytes 9437184 | tf_op jit(solution)/shard_map/project_and_dispatch/pallas_call | solution.py:317
  119.6 7.6 %all-to-all-start.4 = ((bf16[32,48,1536]{2,1,0:T(8,128)(2,1)}), bf16[32,48,1536]{2,1,0:T(8,128)(2,1)}, u32[]{:S(2)}, u32[]{:S(2)}) async-start(bf16[32,48,1536]{2,1,0:T(8,128)(2,1)} %bitcast.46), calls=%async_computation.4 | async-start | bytes 9437184 | tf_op jit(solution)/shard_map/all_to_all | solution.py:471
  127.2 42.6 %all-gather.7.cloned.1.call-done = bf16[64,288,128]{2,1,0:T(8,128)(2,1)} async-done(((bf16[8,288,128]{2,1,0:T(8,128)(2,1)}), bf16[64,288,128]{2,1,0:T(8,128)(2,1)}) %all-gather.7.cloned.1.call-update) | async-done | bytes 4718608 | tf_op jit(solution)/shard_map/all_gather | solution.py:504
  169.8 2.1 slice.8
  171.9 0.9 copy.26
  172.8 0.8 copy.30
  173.6 1.5 slice_bitcast_fusion
  175.2 1.3 copy.27
  176.5 12.7 %all-to-all-done.4 = bf16[32,48,1536]{2,1,0:T(8,128)(2,1)} async-done(((bf16[32,48,1536]{2,1,0:T(8,128)(2,1)}), bf16[32,48,1536]{2,1,0:T(8,128)(2,1)}, u32[]{:S(2)}, u32[]{:S(2)}) %all-to-all-start.4) | async-done | bytes 4718624 | tf_op jit(solution)/shard_map/all_to_all | solution.py:471
  189.2 1.4 copy-done.1
  190.6 10.5 %experts.1 = bf16[1536,1536]{1,0:T(8,128)(2,1)} custom-call(bf16[1536,1536]{1,0:T(8,128)(2,1)} %bitcast.13.rows_ref, bf16[1536,1024]{1,0:T(8,128)(2,1)S(1)} %bitcast.37, bf16[512,1536]{1,0:T(8,128)(2,1)S(1)} %bitcast.38), custom_call_target="tpu_custom_call" | custom-call | flops 7247757312 | bytes 14155776 | tf_op jit(solution)/shard_map/experts/pallas_call | solution.py:395
  201.1 5.3 %all-to-all-start.5 = ((bf16[32,48,1536]{2,1,0:T(8,128)(2,1)}), bf16[32,48,1536]{2,1,0:T(8,128)(2,1)}, u32[]{:S(2)}, u32[]{:S(2)}) async-start(bf16[32,48,1536]{2,1,0:T(8,128)(2,1)} %bitcast.47), calls=%async_computation.5 | async-start | bytes 9437184 | tf_op jit(solution)/shard_map/all_to_all | solution.py:471
  206.4 1.9 weighing.1.both_ref
  208.4 60.0 %all-to-all-done.5 = bf16[32,48,1536]{2,1,0:T(8,128)(2,1)} async-done(((bf16[32,48,1536]{2,1,0:T(8,128)(2,1)}), bf16[32,48,1536]{2,1,0:T(8,128)(2,1)}, u32[]{:S(2)}, u32[]{:S(2)}) %all-to-all-start.5) | async-done | bytes 4718624 | tf_op jit(solution)/shard_map/all_to_all | solution.py:471
  268.4 1.1 copy-done
  269.5 3.9 %combine.1 = bf16[128,1536]{1,0:T(8,128)(2,1)} custom-call(s32[1]{0:T(128)S(6)} %sub.7.live_ref, bf16[256,1536]{1,0:T(8,128)(2,1)S(1)} %copy-done, bf16[1536,1536]{1,0:T(8,128)(2,1)} %bitcast.21.returned_ref, f32[128,1536]{1,0:T(8,128)S(1)} %copy-done.2), custom_call_target="tpu_custom_call" | custom-call | flops 1207959552 | bytes 5898240 | tf_op jit(solution)/shard_map/combine/pallas_call | solution.py:428
  (24 shorter events, 0.2 us)
Async XLA Ops:
  6.5 17.0 %copy-start.5 = (bf16[1024,1536]{1,0:T(8,128)(2,1)S(1)}, bf16[1024,1536]{1,0:T(8,128)(2,1)}, u32[]{:S(2)}) copy-start(bf16[1024,1536]{1,0:T(8,128)(2,1)} %param.14) | copy-start | bytes 9437188
  7.5 16.7 %collective-permute-start = (bf16[1,48,192]{2,1,0:T(8,128)(2,1)S(1)}, bf16[1,48,192]{2,1,0:T(8,128)(2,1)S(1)}, u32[]{:S(2)}, u32[]{:S(2)}) collective-permute-start(bf16[1,48,192]{2,1,0:T(8,128)(2,1)S(1)} %convert_bitcast_fusion), channel_id=1, source_target_pairs={{0,1},{1,0},{2,3},{3,2},{4,5},{5,4},{6,7},{7,6},{8,9},{9,8},{10,11... | collective-permute-start | bytes 55304 | tf_op jit(solution)/shard_map/ppermute | solution.py:477
  15.1 9.1 %copy-start.7 = (f32[192,48]{0,1:T(8,128)S(1)}, f32[192,48]{0,1:T(8,128)}, u32[]{:S(2)}) copy-start(f32[192,48]{0,1:T(8,128)} %param.20) | copy-start | bytes 110596
  15.1 15.1 %copy-start.9 = (f32[1536]{0:T(1024)S(1)}, f32[1536]{0:T(1024)}, u32[]{:S(2)}) copy-start(f32[1536]{0:T(1024)} %param.16) | copy-start | bytes 18436
  15.1 39.7 %all-to-all-start = ((bf16[8,560,128]{2,1,0:T(8,128)(2,1)}), bf16[8,560,128]{2,1,0:T(8,128)(2,1)}, u32[]{:S(2)}, u32[]{:S(2)}) async-start(bf16[8,560,128]{2,1,0:T(8,128)(2,1)} %prepare.1), calls=%async_computation | async-start | bytes 2293760 | tf_op jit(solution)/shard_map/all_to_all | solution.py:493
  23.4 88.8 %all-gather.5.cloned.1.call-start = ((), (), s32[]{:S(2)}) async-start(), calls=%async_computation.6 | async-start | bytes 5308416 | tf_op jit(solution)/shard_map/all_gather | solution.py:495
  24.3 3.0 %collective-permute-start.1 = (bf16[2,48,192]{2,1,0:T(8,128)(2,1)S(1)}, bf16[2,48,192]{2,1,0:T(8,128)(2,1)S(1)}, u32[]{:S(2)}, u32[]{:S(2)}) collective-permute-start(bf16[2,48,192]{2,1,0:T(8,128)(2,1)S(1)} %pad_maximum_fusion.3), channel_id=1, source_target_pairs={{0,2},{1,3},{2,0},{3,1},{4,6},{5,7},{6,4},{7,5},{8,10},{9,11},{10,... | collective-permute-start | bytes 110600 | tf_op jit(solution)/shard_map/ppermute | solution.py:477
  27.3 5.5 %collective-permute-start.2 = (bf16[4,48,192]{2,1,0:T(8,128)(2,1)S(1)}, bf16[4,48,192]{2,1,0:T(8,128)(2,1)S(1)}, u32[]{:S(2)}, u32[]{:S(2)}) collective-permute-start(bf16[4,48,192]{2,1,0:T(8,128)(2,1)S(1)} %pad_maximum_fusion.2), channel_id=1, source_target_pairs={{0,4},{1,5},{2,6},{3,7},{4,0},{5,1},{6,2},{7,3},{8,12},{9,13},{10,... | collective-permute-start | bytes 221192 | tf_op jit(solution)/shard_map/ppermute | solution.py:477
  33.2 3.2 %copy-start.6 = (bf16[48,1536]{1,0:T(8,128)(2,1)}, bf16[48,1536]{1,0:T(8,128)(2,1)S(1)}, u32[]{:S(2)}) copy-start(bf16[48,1536]{1,0:T(8,128)(2,1)S(1)} %reshape.80) | copy-start | bytes 442372
  33.2 4.3 %collective-permute-start.3 = (bf16[48,1536]{1,0:T(8,128)(2,1)S(1)}, bf16[48,1536]{1,0:T(8,128)(2,1)}, u32[]{:S(2)}, u32[]{:S(2)}) collective-permute-start(bf16[48,1536]{1,0:T(8,128)(2,1)S(1)} %reshape.80), channel_id=1, source_target_pairs={{0,8},{8,0},{16,24},{24,16},{32,40},{40,32},{48,56},{56,48},{64,72... | collective-permute-start | bytes 442376 | tf_op jit(solution)/shard_map/ppermute | solution.py:477
  39.2 8.5 %collective-permute-start.4 = (bf16[96,1536]{1,0:T(8,128)(2,1)}, bf16[96,1536]{1,0:T(8,128)(2,1)}, u32[]{:S(2)}, u32[]{:S(2)}) collective-permute-start(bf16[96,1536]{1,0:T(8,128)(2,1)} %pad_maximum_fusion.1), channel_id=1, source_target_pairs={{0,128},{8,136},{16,144},{24,152},{32,160},{40,168},{48,176},{56,1... | collective-permute-start | bytes 884744 | tf_op jit(solution)/shard_map/ppermute | solution.py:477
  57.7 22.7 %all-to-all-start.1 = ((bf16[4,8,176,128]{3,2,1,0:T(8,128)(2,1)}), bf16[4,8,176,128]{3,2,1,0:T(8,128)(2,1)}, u32[]{:S(2)}, u32[]{:S(2)}) async-start(bf16[4,8,176,128]{3,2,1,0:T(8,128)(2,1)} %get-tuple-element.24), calls=%async_computation.1 | async-start | bytes 2883584 | tf_op jit(solution)/shard_map/all_to_all | solution.py:497
  80.4 17.7 %all-to-all-start.2 = ((bf16[8,288,128]{2,1,0:T(8,128)(2,1)}), bf16[8,288,128]{2,1,0:T(8,128)(2,1)}, u32[]{:S(2)}, u32[]{:S(2)}) async-start(bf16[8,288,128]{2,1,0:T(8,128)(2,1)} %get-tuple-element.26), calls=%async_computation.2 | async-start | bytes 1179648 | tf_op jit(solution)/shard_map/all_to_all | solution.py:500
  84.6 85.2 %all-gather.7.cloned.1.call-start = ((), (), s32[]{:S(2)}) async-start(), calls=%async_computation.7 | async-start | bytes 5308416 | tf_op jit(solution)/shard_map/all_gather | solution.py:504
  84.8 1.1 copy-start.3
  85.9 18.6 %copy-start.10 = (f32[1536]{0:T(1024)S(1)}, f32[1536]{0:T(1024)}, u32[]{:S(2)}) copy-start(f32[1536]{0:T(1024)} %param.23) | copy-start | bytes 18436
  85.9 18.6 %copy-start.8 = (bf16[1536,32]{0,1:T(8,128)(2,1)S(1)}, bf16[1536,32]{0,1:T(8,128)(2,1)}, u32[]{:S(2)}) copy-start(bf16[1536,32]{0,1:T(8,128)(2,1)} %param.24) | copy-start | bytes 294916
  85.9 26.4 %copy-start.4 = (s32[128,8]{0,1:T(8,128)S(1)}, s32[128,8]{0,1:T(8,128)}, u32[]{:S(2)}) copy-start(s32[128,8]{0,1:T(8,128)} %param.25) | copy-start | bytes 12292
  98.1 14.1 %all-to-all-start.3 = ((bf16[8,192,128]{2,1,0:T(8,128)(2,1)}), bf16[8,192,128]{2,1,0:T(8,128)(2,1)S(1)}, u32[]{:S(2)}, u32[]{:S(2)}) async-start(bf16[8,192,128]{2,1,0:T(8,128)(2,1)} %attention.1), calls=%async_computation.3 | async-start | bytes 786432 | tf_op jit(solution)/shard_map/all_to_all | solution.py:503
  119.6 69.6 %all-to-all-start.4 = ((bf16[32,48,1536]{2,1,0:T(8,128)(2,1)}), bf16[32,48,1536]{2,1,0:T(8,128)(2,1)}, u32[]{:S(2)}, u32[]{:S(2)}) async-start(bf16[32,48,1536]{2,1,0:T(8,128)(2,1)} %bitcast.46), calls=%async_computation.4 | async-start | bytes 9437184 | tf_op jit(solution)/shard_map/all_to_all | solution.py:471
  189.2 1.4 copy-start.1
  201.1 67.3 %copy-start.2 = (f32[128,1536]{1,0:T(8,128)S(1)}, f32[128,1536]{1,0:T(8,128)}, u32[]{:S(2)}) copy-start(f32[128,1536]{1,0:T(8,128)} %get-tuple-element.32.hidden_ref) | copy-start | bytes 2359300
  201.1 67.3 %all-to-all-start.5 = ((bf16[32,48,1536]{2,1,0:T(8,128)(2,1)}), bf16[32,48,1536]{2,1,0:T(8,128)(2,1)}, u32[]{:S(2)}, u32[]{:S(2)}) async-start(bf16[32,48,1536]{2,1,0:T(8,128)(2,1)} %bitcast.47), calls=%async_computation.5 | async-start | bytes 9437184 | tf_op jit(solution)/shard_map/all_to_all | solution.py:471
  268.4 1.1 copy-start
Sparse Core Ops, SparseCore 0:
  55.0 54.6 all-gather.4
  111.4 58.3 all-gather.6

commit v10 on v9

--- a/solution.py
+++ b/solution.py
@@ -409,7 +409,7 @@
             transcendentals=count * FF,
         ),
         name="experts",
-    )(rows, gate_up, down)
+    )(rows, gate_up, pltpu.with_memory_space_constraint(down, pltpu.HBM))
 
 
 def combine_body(live_ref, both_ref, returned_ref, hidden_ref, out_ref):
@@ -431,7 +431,7 @@
         grid=(model_width // tile,),
         in_specs=[
             pl.BlockSpec(memory_space=pltpu.SMEM),
-            pl.BlockSpec(memory_space=pltpu.VMEM),
+            pl.BlockSpec(both.shape, lambda i: (0, 0)),
             pl.BlockSpec((slots, tile), lambda i: (0, i)),
             column,
         ],
@@ -443,7 +443,12 @@
             transcendentals=0,
         ),
         name="combine",
-    )(live, both, returned, hidden)
+    )(
+        live,
+        pltpu.with_memory_space_constraint(both, pltpu.HBM),
+        returned,
+        pltpu.with_memory_space_constraint(hidden, pltpu.HBM),
+    )
 
 
 def on_device(

time: 281 us -> 279 us (level)
  no operation moved by 1% of the time
where the time goes in v10:
time: 279 us; the launch traced here: 278 us
  waiting for transfers between devices  152 us (54%)
  starting transfers between devices  48.1 us (17%)
  Pallas kernels  42 us (15%)
  between operations  14.4 us (5%)
  other arithmetic  11.1 us (4%)
  local copies, waits for them, and re-layouts  10.4 us (4%)
    all_to_all x2, waiting for transfers between devices, in_plane(): lax.all_to_all(rows, ('ep', 'tp'), 0, 0, axis_index_groups=PLANE_GROUPS,...  72.8 us
    all_gather x1, waiting for transfers between devices, on_device(): planes = lax.all_gather(hosted, 'ep', axis_index_groups=Z_GROUPS)  42.6 us
    all_to_all x1, waiting for transfers between devices, on_device(): lax.all_to_all(payload, 'ep', 0, 0, axis_index_groups=CHIP_PAIR_GROUPS, t...  14.2 us
    all_to_all x2, starting transfers between devices, in_plane(): lax.all_to_all(rows, ('ep', 'tp'), 0, 0, axis_index_groups=PLANE_GROUPS,...  12.7 us
    pallas_call x1, Pallas kernels, attention(): pl.pallas_call(attention_body, out_shape=pltpu.HBM((seq_len // 128, 192,...  12.2 us
    ppermute x5, starting transfers between devices, doubled(): other = lax.ppermute(block, axis, [(i, i ^ bit) for i in range(size)])  11.4 us
    ppermute x5, waiting for transfers between devices, doubled(): other = lax.ppermute(block, axis, [(i, i ^ bit) for i in range(size)])  11 us
    pallas_call x1, Pallas kernels, experts(): pl.pallas_call(expert_body, out_shape=pltpu.HBM((count, model_width), jnp...  11 us
  transfers between devices with their start and end apart: 13, of which 9 were waited for; matrix products, arithmetic and copies ran while one was open for 7% of the time, Pallas kernels for 10%

profile of v10, /device:TPU:1, one launch (start us, length us, event | category | flops | bytes accessed | tf_op | source)
XLA Modules:
  0.0 278.4 jit_solution(2500882654182659699)
XLA Ops:
  6.5 1.0 convert_bitcast_fusion
  7.5 3.7 %collective-permute-start = (bf16[1,48,192]{2,1,0:T(8,128)(2,1)S(1)}, bf16[1,48,192]{2,1,0:T(8,128)(2,1)S(1)}, u32[]{:S(2)}, u32[]{:S(2)}) collective-permute-start(bf16[1,48,192]{2,1,0:T(8,128)(2,1)S(1)} %convert_bitcast_fusion), channel_id=1, source_target_pairs={{0,1},{1,0},{2,3},{3,2},{4,5},{5,4},{6,7},{7,6},{8,9},{9,8},{10,11... | collective-permute-start | bytes 55304 | tf_op jit(solution)/shard_map/ppermute | solution.py:482
  11.2 0.8 copy.23
  12.0 0.6 reshape.79.table_ref
  12.6 2.5 prepare.1
  15.1 0.0 copy-start.4
  15.1 0.0 copy-start.6
  15.1 8.3 %all-to-all-start = ((bf16[8,560,128]{2,1,0:T(8,128)(2,1)}), bf16[8,560,128]{2,1,0:T(8,128)(2,1)}, u32[]{:S(2)}, u32[]{:S(2)}) async-start(bf16[8,560,128]{2,1,0:T(8,128)(2,1)} %prepare.1), calls=%async_computation | async-start | bytes 2293760 | tf_op jit(solution)/shard_map/all_to_all | solution.py:498
  23.4 0.0 all-gather.5.cloned.1.call-start
  23.5 0.0 copy-done.2
  23.5 0.7 fusion
  24.2 0.0 collective-permute-done
  24.2 0.0 copy-done.4
  24.2 1.3 collective-permute-start.1
  25.6 1.7 collective-permute-done.1
  27.3 2.8 %collective-permute-start.2 = (bf16[4,48,192]{2,1,0:T(8,128)(2,1)S(1)}, bf16[4,48,192]{2,1,0:T(8,128)(2,1)S(1)}, u32[]{:S(2)}, u32[]{:S(2)}) collective-permute-start(bf16[4,48,192]{2,1,0:T(8,128)(2,1)S(1)} %pad_maximum_fusion.2), channel_id=1, source_target_pairs={{0,4},{1,5},{2,6},{3,7},{4,0},{5,1},{6,2},{7,3},{8,12},{9,13},{10,... | collective-permute-start | bytes 221192 | tf_op jit(solution)/shard_map/ppermute | solution.py:482
  30.2 0.0 copy-done.6
  30.2 2.7 fusion.2.normalized_ref
  32.8 0.0 collective-permute-done.2
  32.9 0.1 copy.24
  33.0 0.2 reshape.80
  33.2 0.0 copy-start.3
  33.2 3.1 %collective-permute-start.3 = (bf16[48,1536]{1,0:T(8,128)(2,1)S(1)}, bf16[48,1536]{1,0:T(8,128)(2,1)}, u32[]{:S(2)}, u32[]{:S(2)}) collective-permute-start(bf16[48,1536]{1,0:T(8,128)(2,1)S(1)} %reshape.80), channel_id=1, source_target_pairs={{0,8},{8,0},{16,24},{24,16},{32,40},{40,32},{48,56},{56,48},{64,72... | collective-permute-start | bytes 442376 | tf_op jit(solution)/shard_map/ppermute | solution.py:482
  36.3 0.0 copy-done.3
  36.3 1.1 collective-permute-done.3
  37.5 1.0 broadcast_select_fusion.3
  38.5 0.7 pad_maximum_fusion.1
  39.2 0.4 collective-permute-start.4
  39.6 8.1 %collective-permute-done.4 = bf16[96,1536]{1,0:T(8,128)(2,1)} collective-permute-done((bf16[96,1536]{1,0:T(8,128)(2,1)}, bf16[96,1536]{1,0:T(8,128)(2,1)}, u32[]{:S(2)}, u32[]{:S(2)}) %collective-permute-start.4) | collective-permute-done | bytes 294944 | tf_op jit(solution)/shard_map/ppermute | solution.py:482
  47.8 1.1 broadcast_select_fusion.1
  48.8 0.8 pad_maximum_fusion
  49.7 5.2 %all-to-all-done.along_ref = bf16[8,560,128]{2,1,0:T(8,128)(2,1)} async-done(((bf16[8,560,128]{2,1,0:T(8,128)(2,1)}), bf16[8,560,128]{2,1,0:T(8,128)(2,1)}, u32[]{:S(2)}, u32[]{:S(2)}) %all-to-all-start) | async-done | bytes 1146912 | tf_op jit(solution)/shard_map/all_to_all | solution.py:498
  54.8 0.0 all-gather.5.cloned.1.call-update
  54.9 2.8 relay.1
  57.6 4.8 %all-to-all-start.1 = ((bf16[4,8,176,128]{3,2,1,0:T(8,128)(2,1)}), bf16[4,8,176,128]{3,2,1,0:T(8,128)(2,1)}, u32[]{:S(2)}, u32[]{:S(2)}) async-start(bf16[4,8,176,128]{3,2,1,0:T(8,128)(2,1)} %get-tuple-element.24), calls=%async_computation.1 | async-start | bytes 2883584 | tf_op jit(solution)/shard_map/all_to_all | solution.py:502
  63.1 3.0 %fusion.3.table_ref = f32[1024,128]{1,0:T(8,128)} fusion(f32[128]{0:T(128)S(1)} %get-tuple-element.43, f32[128]{0:T(128)S(1)} %get-tuple-element.44, f32[1024]{0:T(1024)S(1)} %add_convert_fusion, pred[128]{0:T(512)(128)(4,1)S(1)} %iota_compare_fusion), kind=kLoop, calls=%fused_computation.10 | loop fusion | flops 393216 | bytes 529536 | tf_op jit(solution)/shard_map/jit(_where)/select_n | solution.py:38
  66.1 14.2 %all-to-all-done.1.across_ref = bf16[4,8,176,128]{3,2,1,0:T(8,128)(2,1)} async-done(((bf16[4,8,176,128]{3,2,1,0:T(8,128)(2,1)}), bf16[4,8,176,128]{3,2,1,0:T(8,128)(2,1)}, u32[]{:S(2)}, u32[]{:S(2)}) %all-to-all-start.1) | async-done | bytes 1441824 | tf_op jit(solution)/shard_map/all_to_all | solution.py:502
  80.3 4.2 %all-to-all-start.2 = ((bf16[8,288,128]{2,1,0:T(8,128)(2,1)}), bf16[8,288,128]{2,1,0:T(8,128)(2,1)}, u32[]{:S(2)}, u32[]{:S(2)}) async-start(bf16[8,288,128]{2,1,0:T(8,128)(2,1)} %get-tuple-element.26), calls=%async_computation.2 | async-start | bytes 1179648 | tf_op jit(solution)/shard_map/all_to_all | solution.py:505
  84.5 0.2 all-gather.7.cloned.1.call-start
  84.8 0.0 copy-start
  84.8 1.0 copy-done
  85.8 12.2 %attention.1 = bf16[8,192,128]{2,1,0:T(8,128)(2,1)} custom-call(s32[1]{0:T(128)S(6)} %copy.31.length_ref, bf16[1024,1536]{1,0:T(8,128)(2,1)S(1)} %fusion.2.normalized_ref, bf16[4,8,176,128]{3,2,1,0:T(8,128)(2,1)} %all-to-all-done.1.across_ref, f32[1024,128]{1,0:T(8,128)S(1)} %copy-done), custom_call_target="tpu_custom_call" | custom-call | flops 12000000000 | bytes 8388608 | tf_op jit(solution)/shard_map/attention/pallas_call | solution.py:132
  98.0 0.0 all-to-all-done.2
  98.1 0.0 all-gather.7.cloned.1.call-update
  98.1 6.3 %all-to-all-start.3 = ((bf16[8,192,128]{2,1,0:T(8,128)(2,1)}), bf16[8,192,128]{2,1,0:T(8,128)(2,1)S(1)}, u32[]{:S(2)}, u32[]{:S(2)}) async-start(bf16[8,192,128]{2,1,0:T(8,128)(2,1)} %attention.1), calls=%async_computation.3 | async-start | bytes 786432 | tf_op jit(solution)/shard_map/all_to_all | solution.py:508
  104.4 0.0 copy-done.7
  104.4 0.0 copy-done.5
  104.5 1.0 constant_dynamic-slice_fusion.rows_ref
  105.5 6.7 %all-to-all-done.3.parts_ref = bf16[8,192,128]{2,1,0:T(8,128)(2,1)S(1)} async-done(((bf16[8,192,128]{2,1,0:T(8,128)(2,1)}), bf16[8,192,128]{2,1,0:T(8,128)(2,1)S(1)}, u32[]{:S(2)}, u32[]{:S(2)}) %all-to-all-start.3) | async-done | bytes 393248 | tf_op jit(solution)/shard_map/all_to_all | solution.py:508
  112.2 0.0 copy-done.1
  112.2 7.4 %project_and_dispatch.1 = (f32[128,1536]{1,0:T(8,128)}, bf16[1536,1536]{1,0:T(8,128)(2,1)}, f32[64,128]{1,0:T(8,128)}) custom-call(bf16[8,192,128]{2,1,0:T(8,128)(2,1)S(1)} %all-to-all-done.3.parts_ref, bf16[8,2,96,1536]{3,2,1,0:T(8,128)(2,1)} %bitcast.44, bf16[128,1536]{1,0:T(8,128)(2,1)S(1)} %constant_dynamic-slice_fusion.rows_ref, ...), custom_call_target="tpu_custom_call" | custom-call | flops 1207959552 | bytes 9437184 | tf_op jit(solution)/shard_map/project_and_dispatch/pallas_call | solution.py:317
  119.6 7.6 %all-to-all-start.4 = ((bf16[32,48,1536]{2,1,0:T(8,128)(2,1)}), bf16[32,48,1536]{2,1,0:T(8,128)(2,1)}, u32[]{:S(2)}, u32[]{:S(2)}) async-start(bf16[32,48,1536]{2,1,0:T(8,128)(2,1)} %bitcast.45), calls=%async_computation.4 | async-start | bytes 9437184 | tf_op jit(solution)/shard_map/all_to_all | solution.py:476
  127.2 42.6 %all-gather.7.cloned.1.call-done = bf16[64,288,128]{2,1,0:T(8,128)(2,1)} async-done(((bf16[8,288,128]{2,1,0:T(8,128)(2,1)}), bf16[64,288,128]{2,1,0:T(8,128)(2,1)}) %all-gather.7.cloned.1.call-update) | async-done | bytes 4718608 | tf_op jit(solution)/shard_map/all_gather | solution.py:509
  169.8 2.1 slice.8
  171.9 0.9 copy.26
  172.8 0.8 copy.30
  173.6 1.5 slice_bitcast_fusion
  175.2 1.3 copy.27
  176.5 12.7 %all-to-all-done.4 = bf16[32,48,1536]{2,1,0:T(8,128)(2,1)} async-done(((bf16[32,48,1536]{2,1,0:T(8,128)(2,1)}), bf16[32,48,1536]{2,1,0:T(8,128)(2,1)}, u32[]{:S(2)}, u32[]{:S(2)}) %all-to-all-start.4) | async-done | bytes 4718624 | tf_op jit(solution)/shard_map/all_to_all | solution.py:476
  189.2 11.0 %experts.1 = bf16[1536,1536]{1,0:T(8,128)(2,1)} custom-call(bf16[1536,1536]{1,0:T(8,128)(2,1)} %bitcast.13.rows_ref, bf16[1536,1024]{1,0:T(8,128)(2,1)S(1)} %bitcast.37, bf16[512,1536]{1,0:T(8,128)(2,1)} %bitcast.47), custom_call_target="tpu_custom_call" | custom-call | flops 7247757312 | bytes 14155776 | tf_op jit(solution)/shard_map/experts/pallas_call | solution.py:395
  200.2 5.2 %all-to-all-start.5 = ((bf16[32,48,1536]{2,1,0:T(8,128)(2,1)}), bf16[32,48,1536]{2,1,0:T(8,128)(2,1)}, u32[]{:S(2)}, u32[]{:S(2)}) async-start(bf16[32,48,1536]{2,1,0:T(8,128)(2,1)} %bitcast.46), calls=%async_computation.5 | async-start | bytes 9437184 | tf_op jit(solution)/shard_map/all_to_all | solution.py:476
  205.4 1.9 weighing.1.both_ref
  207.3 60.0 %all-to-all-done.5 = bf16[32,48,1536]{2,1,0:T(8,128)(2,1)} async-done(((bf16[32,48,1536]{2,1,0:T(8,128)(2,1)}), bf16[32,48,1536]{2,1,0:T(8,128)(2,1)}, u32[]{:S(2)}, u32[]{:S(2)}) %all-to-all-start.5) | async-done | bytes 4718624 | tf_op jit(solution)/shard_map/all_to_all | solution.py:476
  267.3 4.2 %combine.1 = bf16[128,1536]{1,0:T(8,128)(2,1)} custom-call(s32[1]{0:T(128)S(6)} %sub.7.live_ref, bf16[256,1536]{1,0:T(8,128)(2,1)} %weighing.1.both_ref, bf16[1536,1536]{1,0:T(8,128)(2,1)} %bitcast.21.returned_ref, f32[128,1536]{1,0:T(8,128)} %get-tuple-element.32.hidden_ref), custom_call_target="tpu_custom_call" | custom-call | flops 1207959552 | bytes 5898240 | tf_op jit(solution)/shard_map/combine/pallas_call | solution.py:428
  (18 shorter events, 0.2 us)
Async XLA Ops:
  6.5 17.0 %copy-start.2 = (bf16[1024,1536]{1,0:T(8,128)(2,1)S(1)}, bf16[1024,1536]{1,0:T(8,128)(2,1)}, u32[]{:S(2)}) copy-start(bf16[1024,1536]{1,0:T(8,128)(2,1)} %param.14) | copy-start | bytes 9437188
  7.5 16.7 %collective-permute-start = (bf16[1,48,192]{2,1,0:T(8,128)(2,1)S(1)}, bf16[1,48,192]{2,1,0:T(8,128)(2,1)S(1)}, u32[]{:S(2)}, u32[]{:S(2)}) collective-permute-start(bf16[1,48,192]{2,1,0:T(8,128)(2,1)S(1)} %convert_bitcast_fusion), channel_id=1, source_target_pairs={{0,1},{1,0},{2,3},{3,2},{4,5},{5,4},{6,7},{7,6},{8,9},{9,8},{10,11... | collective-permute-start | bytes 55304 | tf_op jit(solution)/shard_map/ppermute | solution.py:482
  15.1 9.1 %copy-start.4 = (f32[192,48]{0,1:T(8,128)S(1)}, f32[192,48]{0,1:T(8,128)}, u32[]{:S(2)}) copy-start(f32[192,48]{0,1:T(8,128)} %param.20) | copy-start | bytes 110596
  15.1 15.0 %copy-start.6 = (f32[1536]{0:T(1024)S(1)}, f32[1536]{0:T(1024)}, u32[]{:S(2)}) copy-start(f32[1536]{0:T(1024)} %param.16) | copy-start | bytes 18436
  15.1 39.7 %all-to-all-start = ((bf16[8,560,128]{2,1,0:T(8,128)(2,1)}), bf16[8,560,128]{2,1,0:T(8,128)(2,1)}, u32[]{:S(2)}, u32[]{:S(2)}) async-start(bf16[8,560,128]{2,1,0:T(8,128)(2,1)} %prepare.1), calls=%async_computation | async-start | bytes 2293760 | tf_op jit(solution)/shard_map/all_to_all | solution.py:498
  23.4 88.8 %all-gather.5.cloned.1.call-start = ((), (), s32[]{:S(2)}) async-start(), calls=%async_computation.6 | async-start | bytes 5308416 | tf_op jit(solution)/shard_map/all_gather | solution.py:500
  24.2 3.0 %collective-permute-start.1 = (bf16[2,48,192]{2,1,0:T(8,128)(2,1)S(1)}, bf16[2,48,192]{2,1,0:T(8,128)(2,1)S(1)}, u32[]{:S(2)}, u32[]{:S(2)}) collective-permute-start(bf16[2,48,192]{2,1,0:T(8,128)(2,1)S(1)} %pad_maximum_fusion.3), channel_id=1, source_target_pairs={{0,2},{1,3},{2,0},{3,1},{4,6},{5,7},{6,4},{7,5},{8,10},{9,11},{10,... | collective-permute-start | bytes 110600 | tf_op jit(solution)/shard_map/ppermute | solution.py:482
  27.3 5.5 %collective-permute-start.2 = (bf16[4,48,192]{2,1,0:T(8,128)(2,1)S(1)}, bf16[4,48,192]{2,1,0:T(8,128)(2,1)S(1)}, u32[]{:S(2)}, u32[]{:S(2)}) collective-permute-start(bf16[4,48,192]{2,1,0:T(8,128)(2,1)S(1)} %pad_maximum_fusion.2), channel_id=1, source_target_pairs={{0,4},{1,5},{2,6},{3,7},{4,0},{5,1},{6,2},{7,3},{8,12},{9,13},{10,... | collective-permute-start | bytes 221192 | tf_op jit(solution)/shard_map/ppermute | solution.py:482
  33.2 3.2 %copy-start.3 = (bf16[48,1536]{1,0:T(8,128)(2,1)}, bf16[48,1536]{1,0:T(8,128)(2,1)S(1)}, u32[]{:S(2)}) copy-start(bf16[48,1536]{1,0:T(8,128)(2,1)S(1)} %reshape.80) | copy-start | bytes 442372
  33.2 4.3 %collective-permute-start.3 = (bf16[48,1536]{1,0:T(8,128)(2,1)S(1)}, bf16[48,1536]{1,0:T(8,128)(2,1)}, u32[]{:S(2)}, u32[]{:S(2)}) collective-permute-start(bf16[48,1536]{1,0:T(8,128)(2,1)S(1)} %reshape.80), channel_id=1, source_target_pairs={{0,8},{8,0},{16,24},{24,16},{32,40},{40,32},{48,56},{56,48},{64,72... | collective-permute-start | bytes 442376 | tf_op jit(solution)/shard_map/ppermute | solution.py:482
  39.2 8.5 %collective-permute-start.4 = (bf16[96,1536]{1,0:T(8,128)(2,1)}, bf16[96,1536]{1,0:T(8,128)(2,1)}, u32[]{:S(2)}, u32[]{:S(2)}) collective-permute-start(bf16[96,1536]{1,0:T(8,128)(2,1)} %pad_maximum_fusion.1), channel_id=1, source_target_pairs={{0,128},{8,136},{16,144},{24,152},{32,160},{40,168},{48,176},{56,1... | collective-permute-start | bytes 884744 | tf_op jit(solution)/shard_map/ppermute | solution.py:482
  57.6 22.7 %all-to-all-start.1 = ((bf16[4,8,176,128]{3,2,1,0:T(8,128)(2,1)}), bf16[4,8,176,128]{3,2,1,0:T(8,128)(2,1)}, u32[]{:S(2)}, u32[]{:S(2)}) async-start(bf16[4,8,176,128]{3,2,1,0:T(8,128)(2,1)} %get-tuple-element.24), calls=%async_computation.1 | async-start | bytes 2883584 | tf_op jit(solution)/shard_map/all_to_all | solution.py:502
  80.3 17.7 %all-to-all-start.2 = ((bf16[8,288,128]{2,1,0:T(8,128)(2,1)}), bf16[8,288,128]{2,1,0:T(8,128)(2,1)}, u32[]{:S(2)}, u32[]{:S(2)}) async-start(bf16[8,288,128]{2,1,0:T(8,128)(2,1)} %get-tuple-element.26), calls=%async_computation.2 | async-start | bytes 1179648 | tf_op jit(solution)/shard_map/all_to_all | solution.py:505
  84.5 85.3 %all-gather.7.cloned.1.call-start = ((), (), s32[]{:S(2)}) async-start(), calls=%async_computation.7 | async-start | bytes 5308416 | tf_op jit(solution)/shard_map/all_gather | solution.py:509
  84.8 1.1 copy-start
  85.8 18.6 %copy-start.7 = (f32[1536]{0:T(1024)S(1)}, f32[1536]{0:T(1024)}, u32[]{:S(2)}) copy-start(f32[1536]{0:T(1024)} %param.23) | copy-start | bytes 18436
  85.8 18.6 %copy-start.5 = (bf16[1536,32]{0,1:T(8,128)(2,1)S(1)}, bf16[1536,32]{0,1:T(8,128)(2,1)}, u32[]{:S(2)}) copy-start(bf16[1536,32]{0,1:T(8,128)(2,1)} %param.24) | copy-start | bytes 294916
  85.8 26.4 %copy-start.1 = (s32[128,8]{0,1:T(8,128)S(1)}, s32[128,8]{0,1:T(8,128)}, u32[]{:S(2)}) copy-start(s32[128,8]{0,1:T(8,128)} %param.25) | copy-start | bytes 12292
  98.1 14.1 %all-to-all-start.3 = ((bf16[8,192,128]{2,1,0:T(8,128)(2,1)}), bf16[8,192,128]{2,1,0:T(8,128)(2,1)S(1)}, u32[]{:S(2)}, u32[]{:S(2)}) async-start(bf16[8,192,128]{2,1,0:T(8,128)(2,1)} %attention.1), calls=%async_computation.3 | async-start | bytes 786432 | tf_op jit(solution)/shard_map/all_to_all | solution.py:508
  119.6 69.6 %all-to-all-start.4 = ((bf16[32,48,1536]{2,1,0:T(8,128)(2,1)}), bf16[32,48,1536]{2,1,0:T(8,128)(2,1)}, u32[]{:S(2)}, u32[]{:S(2)}) async-start(bf16[32,48,1536]{2,1,0:T(8,128)(2,1)} %bitcast.45), calls=%async_computation.4 | async-start | bytes 9437184 | tf_op jit(solution)/shard_map/all_to_all | solution.py:476
  200.2 67.1 %all-to-all-start.5 = ((bf16[32,48,1536]{2,1,0:T(8,128)(2,1)}), bf16[32,48,1536]{2,1,0:T(8,128)(2,1)}, u32[]{:S(2)}, u32[]{:S(2)}) async-start(bf16[32,48,1536]{2,1,0:T(8,128)(2,1)} %bitcast.46), calls=%async_computation.5 | async-start | bytes 9437184 | tf_op jit(solution)/shard_map/all_to_all | solution.py:476
Sparse Core Ops, SparseCore 0:
  55.0 54.6 all-gather.4
  111.4 58.3 all-gather.6
